TPU v7x, 128 devices: a whole 4x4x4 slice. The times are simulated.
128 devices in a mesh: gz: 8 (over z, core), yx: 16 (over y, x).
Axes of the slice: x: 4, y: 4, z: 4, core: 2. Of those that a mesh axis runs over, the one named last changes fastest.
Arguments:
- features: bfloat16 [12, 4, 256, 2048], P(None, None, 'yx', 'gz'), may hold values from -6 to 6
- conv_weight: bfloat16 [3, 12, 3, 3, 3], replicated, may hold values from -0.3125 to 0.3125
- conv_bias: float32 [3], replicated, may hold values from -3 to 3
- fragments: int32 [4, 256, 2048], P(None, 'yx', 'gz'), may hold values from 1 to 16000, as said below
- pair_slot: int32 [3, 4, 256, 2048], P(None, None, 'yx', 'gz'), may hold values from 0 to 4095
- slot_bucket: int32 [128, 4096], P(('gz', 'yx')), may hold values from 0 to 8191, as said below
- arrival_row: int32 [128, 128, 64], P(('gz', 'yx')), may hold values from 0 to 4095
Outputs:
- affinity: bfloat16 [3, 4, 256, 2048], P(None, None, 'yx', 'gz')
- edge_mean: float32 [524288], P(('gz', 'yx'))
Inputs may be any that keep to these rules, and one draw needn't show every extreme that they name: Ids of supervoxel fragments; neighbouring voxels within a slice mostly share an id. `slot_bucket`: each row holds distinct values; row s lists the slots of device s, value // 64 is the slot's owner (its index along gz+yx) and value % 64 its place in the bucket for that owner.
All inputs are finite; a program needn't handle non-finite values.
Results may differ from a plain program's by a relative error of at most 0.005.
Values may be sent and summed in bfloat16 or wider, within the bound.
No kernel may reach another device: no remote copies, remote signals or barrier semaphores. Data moves between devices by JAX's collectives and lax.ppermute only.
A program may use at most 64 MiB of HBM per device.

v0:
```python
import jax
import jax.numpy as jnp
from jax import lax
from jax.sharding import PartitionSpec as P

BUCKET = 64
E_OWN = 4096


def with_halo(cells, sides, width):
    for axis, dim in sides:
        count = lax.axis_size(axis)
        ends = count - 1
        head = lax.slice_in_dim(cells, 0, width, axis=dim)
        tail = lax.slice_in_dim(cells, cells.shape[dim] - width, cells.shape[dim], axis=dim)
        cells = jnp.concatenate(
            [
                lax.ppermute(tail, axis, [(i, (i + 1) % count) for i in range(ends)]),
                cells,
                lax.ppermute(head, axis, [((i + 1) % count, i) for i in range(ends)]),
            ],
            axis=dim,
        )
    return cells


def passed_along(block, axis, distance):
    devices = range(lax.axis_size(axis))
    route = [(i - distance, i) for i in devices if i - distance in devices]
    return lax.ppermute(block, axis, route)


def convolve(volume, kernel, padding):
    result = lax.conv_general_dilated(
        volume[None],
        kernel,
        (1, 1, 1),
        padding,
        dimension_numbers=("NCDHW", "OIDHW", "NCDHW"),
        preferred_element_type=jnp.float32,
    )
    return result[0]


def local(features, conv_weight, conv_bias, fragments, pair_slot, slot_bucket, arrival_row):
    widened = with_halo(features, (("gz", 3), ("yx", 2)), 1)
    logits = convolve(widened, conv_weight, ((1, 1), (0, 0), (0, 0)))
    logits = logits + conv_bias[:, None, None, None]
    affinity = jax.nn.sigmoid(logits).astype(jnp.bfloat16)
    from_before_rows = passed_along(fragments[:, -1:], "yx", 1)
    from_before_columns = passed_along(fragments[:, :, -1:], "gz", 1)
    under_z = jnp.concatenate([fragments[:1], fragments[:-1]], axis=0)
    under_y = jnp.concatenate([from_before_rows, fragments[:, :-1]], axis=1)
    under_x = jnp.concatenate([from_before_columns, fragments[:, :, :-1]], axis=2)
    depth_ids = lax.broadcasted_iota(jnp.int32, fragments.shape, 0)
    height_ids = (
        lax.broadcasted_iota(jnp.int32, fragments.shape, 1)
        + lax.axis_index("yx") * fragments.shape[1]
    )
    width_ids = (
        lax.broadcasted_iota(jnp.int32, fragments.shape, 2)
        + lax.axis_index("gz") * fragments.shape[2]
    )
    crossing = jnp.stack(
        [
            (fragments != under_z) & (depth_ids > 0),
            (fragments != under_y) & (height_ids > 0),
            (fragments != under_x) & (width_ids > 0),
        ]
    ).astype(jnp.int32)
    slot_total = slot_bucket.shape[1]
    slot_ids = jnp.where(crossing == 1, pair_slot, slot_total).ravel()
    values = jnp.where(crossing == 1, affinity.astype(jnp.float32), jnp.float32(0.0)).ravel()
    tallies = crossing.astype(jnp.float32).ravel()
    slot_sums = jax.ops.segment_sum(values, slot_ids, slot_total + 1)[:slot_total]
    slot_counts = jax.ops.segment_sum(tallies, slot_ids, slot_total + 1)[:slot_total]
    device_total = lax.axis_size("gz") * lax.axis_size("yx")
    outgoing = (
        jnp.zeros((2, device_total * BUCKET), jnp.float32)
        .at[:, slot_bucket[0]]
        .set(jnp.stack([slot_sums, slot_counts]))
    )
    outgoing = outgoing.reshape(2, device_total, BUCKET)
    arrived = lax.all_to_all(
        outgoing.astype(jnp.bfloat16), ("gz", "yx"), split_axis=1, concat_axis=1, tiled=True
    ).astype(outgoing.dtype)
    targets = arrival_row[0].ravel()
    edge_sums = jax.ops.segment_sum(arrived[0].ravel(), targets, E_OWN)
    edge_counts = jax.ops.segment_sum(arrived[1].ravel(), targets, E_OWN)
    return (affinity, edge_sums / jnp.maximum(edge_counts, 1.0))


def solution(mesh):
    return jax.shard_map(
        local,
        mesh=mesh,
        in_specs=(
            P(None, None, "yx", "gz"),
            P(),
            P(),
            P(None, "yx", "gz"),
            P(None, None, "yx", "gz"),
            P(("gz", "yx"), None),
            P(("gz", "yx"), None, None),
        ),
        out_specs=(P(None, None, "yx", "gz"), P(("gz", "yx"))),
        check_vma=False,
    )
```

profile of v0, /device:TPU:1, one launch (start us, length us, event | category | flops | bytes accessed | tf_op | source)
XLA Modules:
  0.0 990.3 jit_solution(14638027915106680523)
XLA Ops:
  0.7 1.2 fusion.36
  1.9 4.9 collective-permute-start
  6.8 1.9 collective-permute-start.1
  9.6 3.6 collective-permute-start.5
  14.0 3.1 collective-permute-start.4
  21.2 1.4 pad_maximum_fusion.2
  22.6 3.1 collective-permute-start.2
  25.7 1.3 collective-permute-start.3
  27.1 1.1 fusion.21
  29.4 267.0 %scatter_custom_fusion.1 = f32[4097]{0:T(1024)S(1)} fusion(s32[49152]{0:T(1024)S(1)} %bitcast.63, f32[49152]{0:T(1024)S(1)} %bitcast.65, f32[]{:T(128)} %constant.12.clone.1), kind=kCustom, calls=%fused_computation.49 | custom fusion | flops 49152 | bytes 16392 | tf_op jit(solution)/shard_map/scatter-add | solution.py:76
  296.5 1.0 maximum_bitcast_fusion
  297.6 1.6 reshape.101
  299.2 6.2 copy.44
  305.4 1.0 slice.58
  306.5 292.2 %broadcast_select_fusion = f32[4,16,8,33,3]{2,4,3,1,0:T(4,128)} fusion(pred[8,33]{0,1:T(8,128)(4,1)S(1)} %copy-done.4, bf16[12,4,18,1,7,2]{0,4,5,2,1,3:T(8,128)(2,1)S(1)} %slice.58, bf16[12,4,18,1,8,33]{0,4,5,2,1,3:T(8,128)(2,1)} %copy.44, bf16[3,12,3,3,3]{1,4,3,2,0:T(4,128)(2,1)S(1)} %copy-done), kind=kOutput, calls=%fused_computation.14 | convolution fusion | flops 28873728 | bytes 685344 | tf_op jit(solution)/shard_map/conv_general_dilated | solution.py:34
  598.8 3.7 copy.46
  603.0 267.0 %scatter_custom_fusion = f32[4097]{0:T(1024)S(1)} fusion(s32[49152]{0:T(1024)S(1)} %bitcast.64, f32[49152]{0:T(1024)S(1)} %convert_select_fusion, f32[]{:T(128)} %constant.12.clone.1), kind=kCustom, calls=%fused_computation.51 | custom fusion | flops 49152 | bytes 16392 | tf_op jit(solution)/shard_map/scatter-add | solution.py:75
  870.7 12.8 %scatter_custom_fusion.2 = f32[2,8192]{0,1:T(8,128)} fusion(s32[4096]{0:T(1024)S(1)} %bitcast.68, f32[4096,2]{1,0:T(8,128)S(1)} %copy.50, f32[]{:T(128)} %constant.12.clone.1), kind=kCustom, calls=%fused_computation.15 | custom fusion | bytes 65540 | tf_op jit(solution)/shard_map/scatter | solution.py:81
  883.5 2.4 convert_element_type.38
  885.9 1.7 copy.51
  887.5 5.0 all-to-all-start
  893.4 8.8 all-to-all-done
  902.7 43.2 %scatter_custom_fusion.4 = f32[4096]{0:T(1024)S(1)} fusion(s32[8192]{0:T(1024)S(1)} %reshape.83, f32[8192]{0:T(1024)S(1)} %reshape.93, f32[]{:T(128)} %constant.12.clone.1), kind=kCustom, calls=%fused_computation.53 | custom fusion | flops 8192 | bytes 16388 | tf_op jit(solution)/shard_map/scatter-add | solution.py:89
  946.0 43.2 %scatter_custom_fusion.3 = f32[4096]{0:T(1024)S(1)} fusion(s32[8192]{0:T(1024)S(1)} %reshape.83, f32[8192]{0:T(1024)S(1)} %reshape.85, f32[]{:T(128)} %constant.12.clone.1), kind=kCustom, calls=%fused_computation.55 | custom fusion | flops 8192 | bytes 16388 | tf_op jit(solution)/shard_map/scatter-add | solution.py:88
  (51 shorter events, 10.2 us)
Async XLA Ops:
  0.6 305.8 %copy-start = (bf16[3,12,3,3,3]{1,4,3,2,0:T(4,128)(2,1)S(1)}, bf16[3,12,3,3,3]{1,4,3,2,0:T(4,128)(2,1)}, u32[]{:S(2)}) copy-start(bf16[3,12,3,3,3]{1,4,3,2,0:T(4,128)(2,1)} %param.8) | copy-start | bytes 5836
  0.6 295.8 %copy-start.1 = (bf16[12,4,16,256]{3,2,1,0:T(8,128)(2,1)S(1)}, bf16[12,4,16,256]{3,2,1,0:T(8,128)(2,1)}, u32[]{:S(2)}) copy-start(bf16[12,4,16,256]{3,2,1,0:T(8,128)(2,1)} %param.7) | copy-start | bytes 1179652
  1.9 19.3 %collective-permute-start = (bf16[12,4,16,1]{3,2,1,0:T(8,128)(2,1)S(1)}, bf16[12,4,16,1]{3,2,1,0:T(8,128)(2,1)S(1)}, u32[]{:S(2)}, u32[]{:S(2)}) collective-permute-start(bf16[12,4,16,1]{3,2,1,0:T(8,128)(2,1)S(1)} %get-tuple-element.14), channel_id=1, source_target_pairs={{0,16},{16,32},{32,48},{48,64},{64,80},{80,96},{96,112},{1,17},{17... | collective-permute-start | bytes 4616 | tf_op jit(solution)/shard_map/ppermute | solution.py:18
  6.8 14.4 %collective-permute-start.1 = (bf16[12,4,16,1]{3,2,1,0:T(8,128)(2,1)S(1)}, bf16[12,4,16,1]{3,2,1,0:T(8,128)(2,1)S(1)}, u32[]{:S(2)}, u32[]{:S(2)}) collective-permute-start(bf16[12,4,16,1]{3,2,1,0:T(8,128)(2,1)S(1)} %get-tuple-element.15), channel_id=1, source_target_pairs={{16,0},{32,16},{48,32},{64,48},{80,64},{96,80},{112,96},{17,1},{33... | collective-permute-start | bytes 4616 | tf_op jit(solution)/shard_map/ppermute | solution.py:20
  9.6 17.5 %collective-permute-start.5 = (s32[4,16,1]{2,1,0:T(8,128)S(1)}, s32[4,16,1]{2,1,0:T(8,128)S(1)}, u32[]{:S(2)}, u32[]{:S(2)}) collective-permute-start(s32[4,16,1]{2,1,0:T(8,128)S(1)} %slice.50), channel_id=1, source_target_pairs={{0,16},{16,32},{32,48},{48,64},{64,80},{80,96},{96,112},{1,17},{17... | collective-permute-start | bytes 776 | tf_op jit(solution)/shard_map/ppermute | solution.py:30
  14.0 13.1 %collective-permute-start.4 = (s32[4,1,256]{2,1,0:T(1,128)S(1)}, s32[4,1,256]{2,1,0:T(1,128)S(1)}, u32[]{:S(2)}, u32[]{:S(2)}) collective-permute-start(s32[4,1,256]{2,1,0:T(1,128)S(1)} %slice.48), channel_id=1, source_target_pairs={{0,1},{1,2},{2,3},{3,4},{4,5},{5,6},{6,7},{7,8},{8,9},{9,10},{10,1... | collective-permute-start | bytes 12296 | tf_op jit(solution)/shard_map/ppermute | solution.py:30
  22.6 273.8 %collective-permute-start.2 = (bf16[12,4,1,258]{3,2,1,0:T(2,128)(2,1)S(1)}, bf16[12,4,1,258]{3,2,1,0:T(2,128)(2,1)S(1)}, u32[]{:S(2)}, u32[]{:S(2)}) collective-permute-start(bf16[12,4,1,258]{3,2,1,0:T(2,128)(2,1)S(1)} %get-tuple-element.12), channel_id=1, source_target_pairs={{0,1},{1,2},{2,3},{3,4},{4,5},{5,6},{6,7},{7,8},{8,9},{9,10},{10,1... | collective-permute-start | bytes 74312 | tf_op jit(solution)/shard_map/ppermute | solution.py:18
  25.7 270.7 %collective-permute-start.3 = (bf16[12,4,1,258]{3,2,1,0:T(2,128)(2,1)S(1)}, bf16[12,4,1,258]{3,2,1,0:T(2,128)(2,1)S(1)}, u32[]{:S(2)}, u32[]{:S(2)}) collective-permute-start(bf16[12,4,1,258]{3,2,1,0:T(2,128)(2,1)S(1)} %get-tuple-element.13), channel_id=1, source_target_pairs={{1,0},{2,1},{3,2},{4,3},{5,4},{6,5},{7,6},{8,7},{9,8},{10,9},{11,1... | collective-permute-start | bytes 74312 | tf_op jit(solution)/shard_map/ppermute | solution.py:20
  296.4 9.0 copy-start.2
  299.2 7.3 copy-start.4
  598.7 271.2 %slice-start = ((f32[4097]{0:T(1024)}), f32[4096]{0:T(1024)S(1)}, s32[]{:S(2)}) async-start(f32[4097]{0:T(1024)} %copy-done.2), calls=%async_computation.1 | async-start | bytes 32768 | tf_op jit(solution)/shard_map/slice | solution.py:76
  883.5 9.1 copy-start.3
  887.5 14.6 %all-to-all-start = ((bf16[2,128,64]{2,0,1:T(2,128)(2,1)}), bf16[2,128,64]{2,0,1:T(2,128)(2,1)S(1)}, u32[]{:S(2)}, u32[]{:S(2)}) async-start(bf16[2,128,64]{2,0,1:T(2,128)(2,1)} %copy.51), calls=%async_computation | async-start | bytes 131072 | tf_op jit(solution)/shard_map/all_to_all | solution.py:84
where the time goes:
time: 996 us; the launch traced here: 990 us
  other arithmetic  629 us (63%)
  matrix products  292 us (29%)
  local copies, waits for them, and re-layouts  35.7 us (4%)
  starting transfers between devices  23 us (2%)
    conv_general_dilated x1, matrix products, convolve(): lax.conv_general_dilated(volume[None], kernel, (1, 1, 1), padding, dimens...  292 us
    scatter-add x1, other arithmetic, local(): jax.ops.segment_sum(tallies, slot_ids, slot_total + 1)[:slot_total]  267 us
    scatter-add x1, other arithmetic, local(): jax.ops.segment_sum(values, slot_ids, slot_total + 1)[:slot_total]  267 us
    scatter-add x1, other arithmetic, local(): edge_sums = jax.ops.segment_sum(arrived[0].ravel(), targets, E_OWN)  43.2 us
    scatter-add x1, other arithmetic, local(): edge_counts = jax.ops.segment_sum(arrived[1].ravel(), targets, E_OWN)  43.2 us
  transfers between devices with their start and end apart: 7, of which 1 were waited for; matrix products, arithmetic and copies ran while one was open for 28% of the time, Pallas kernels for 0%

commit v1 on v0

v1 whole, which is shorter than its diff:
```python
import functools

import jax
import jax.numpy as jnp
from jax import lax
from jax.experimental import pallas as pl
from jax.experimental.pallas import tpu as pltpu
from jax.sharding import PartitionSpec as P

C_IN, C_OUT, Z, YD, XD = 12, 3, 4, 16, 256
BUCKET, E_OWN, P_LOC = 64, 4096, 4096
CZ = C_IN * Z
CELLS = CZ * YD
DEPTH = CELLS + 2 * CZ + 32
WIDE = DEPTH + 2 * Z * YD
ROWS = Z * YD
LANES = 128
HIGH = P_LOC // LANES

f32, bf16, i32 = jnp.float32, jnp.bfloat16, jnp.int32


def iota(shape, dim):
    return lax.broadcasted_iota(i32, shape, dim)


def along(a, b):
    return lax.dot_general(a, b, (((1,), (1,)), ((), ())), preferred_element_type=f32)


def whole(count):
    return [pl.BlockSpec(memory_space=pltpu.VMEM)] * count


def rows_kernel(cells, ids, up, down):
    row = iota((2 * CZ, CELLS), 0)
    wanted = jnp.where(row < CZ, row * YD, (row - CZ) * YD + YD - 1)
    pick = jnp.where(iota((2 * CZ, CELLS), 1) == wanted, 1.0, 0.0).astype(bf16)
    picked = jnp.dot(pick, cells[...], preferred_element_type=f32).astype(bf16)
    up[...] = picked[:CZ]
    down[:CZ] = picked[CZ:]
    last = jnp.concatenate([ids[(z + 1) * YD - 1 : (z + 1) * YD] for z in range(Z)], axis=0)
    pair = jnp.concatenate([last >> 7, last & 127], axis=0)
    down[CZ:] = pair.astype(f32).astype(bf16)


def fill(wide, cells, top, bottom):
    wide[:CELLS] = cells[...]
    wide[CELLS : CELLS + CZ] = top[:CZ]
    wide[CELLS + CZ : CELLS + 2 * CZ] = bottom[...]
    wide[CELLS + 2 * CZ : DEPTH] = jnp.zeros((DEPTH - CELLS - 2 * CZ, XD), bf16)


def columns_kernel(cells, top, bottom, ids, left, right, wide):
    fill(wide, cells, top, bottom)
    wide[DEPTH : DEPTH + ROWS] = (ids[...] >> 7).astype(f32).astype(bf16)
    wide[DEPTH + ROWS :] = (ids[...] & 127).astype(f32).astype(bf16)
    row, lane = iota((8, XD), 0), iota((8, XD), 1)
    pick = jnp.where(lane == jnp.where(row == 0, 0, XD - 1), 1.0, 0.0).astype(bf16)
    picked = along(pick, wide[...])
    left[...] = picked[0:1]
    right[...] = picked[1:2]


def build_taps(weights, taps):
    k = iota((LANES, DEPTH), 1)
    channel = jnp.where(k < CELLS, k // (Z * YD), ((k - CELLS) % CZ) // Z)
    channel = jnp.where(k < CELLS + 2 * CZ, channel, LANES)
    spread = jnp.where(iota((LANES, DEPTH), 0) == channel, 1.0, 0.0).astype(bf16)
    lines = jnp.dot(weights[...], spread, preferred_element_type=f32)
    m, k = iota((ROWS, DEPTH), 0), iota((ROWS, DEPTH), 1)
    inner = k < CELLS
    z_in = jnp.where(inner, (k // YD) % Z, (k - CELLS) % Z)
    y_in = jnp.where(inner, k % YD, jnp.where(k < CELLS + CZ, -1, YD))
    y_in = jnp.where(k < CELLS + 2 * CZ, y_in, 2 * YD)
    dz, dy = z_in - m // YD + 1, y_in - m % YD + 1
    code = jnp.where((dz >= 0) & (dz < 3) & (dy >= 0) & (dy < 3), dz * 3 + dy, -1)
    for block in range(9):
        tap = jnp.zeros((ROWS, DEPTH), f32)
        for ab in range(9):
            line = lines[block * 9 + ab : block * 9 + ab + 1]
            tap = jnp.where(code == ab, line, tap)
        taps[block * ROWS : (block + 1) * ROWS] = tap.astype(bf16)


def one_hot(line, count, value=None):
    hit = iota((count, line.shape[1]), 0) == line
    return jnp.where(hit, 1.0 if value is None else value, 0.0).astype(bf16)


def main_kernel(cells, top, bottom, left, right, ids, slots, bucket, weights, bias, affinity, outgoing, wide, taps, value, cross):
    fill(wide, cells, top, bottom)
    build_taps(weights, taps)
    product = jnp.dot(taps[...], wide[...], preferred_element_type=f32)
    edge_row = iota((8, WIDE), 0)
    edges = jnp.where(edge_row == 0, left[...], jnp.where(edge_row == 1, right[...], 0.0)).astype(bf16)
    outer = along(taps[...], edges[:, :DEPTH])
    part = C_OUT * ROWS
    lane = iota((part, XD), 1)
    logits = product[part : 2 * part]
    logits += jnp.where(lane == 0, outer[:part, 0:1], pltpu.roll(product[:part], 1, 1))
    logits += jnp.where(lane == XD - 1, outer[2 * part :, 1:2], pltpu.roll(product[2 * part :], XD - 1, 1))
    channel = iota((part, XD), 0) // ROWS
    logits += jnp.where(channel == 0, bias[0], jnp.where(channel == 1, bias[1], bias[2]))
    soft = (1.0 / (1.0 + jnp.exp(-logits))).astype(bf16)
    affinity[...] = soft
    soft = soft.astype(f32)

    here = ids[...]
    m, n = iota((ROWS, XD), 0), iota((ROWS, XD), 1)
    under_z = jnp.concatenate([here[:YD], here[:-YD]], axis=0)
    above = top[CZ:].astype(f32)
    above = (above[:Z] * 128.0 + above[Z:]).astype(i32)
    above = jnp.concatenate([jnp.broadcast_to(above[z : z + 1], (YD, XD)) for z in range(Z)], axis=0)
    under_y = jnp.where(m % YD == 0, above, pltpu.roll(here, 1, 0))
    k = iota((ROWS, 2 * ROWS), 1)
    r = iota((ROWS, 2 * ROWS), 0)
    join = jnp.where(k == r, 128.0, jnp.where(k == r + ROWS, 1.0, 0.0)).astype(bf16)
    beside = along(join, edges[:, DEPTH:])[:, 0:1].astype(i32)
    under_x = jnp.where(n == 0, beside, pltpu.roll(here, 1, 1))
    for d, under in enumerate((under_z, under_y, under_x)):
        differs = (here != under) & (under > 0)
        differs = jnp.where(differs, 1.0, 0.0)
        cross[d * ROWS : (d + 1) * ROWS] = differs
        value[d * ROWS : (d + 1) * ROWS] = differs * soft[d * ROWS : (d + 1) * ROWS]

    group = 8

    def step(i, total):
        a_parts, b_parts = [], []
        base = pl.multiple_of(i * group, group)
        slot8, value8, cross8 = slots[pl.ds(base, group)], value[pl.ds(base, group)], cross[pl.ds(base, group)]
        for j in range(group):
            slot = slot8[j : j + 1]
            high, low = slot >> 7, slot & 127
            a_parts.append(
                jnp.concatenate([one_hot(high, HIGH, value8[j : j + 1]), one_hot(high, HIGH, cross8[j : j + 1])], axis=0)
            )
            b_parts.append(one_hot(low, LANES))
        return total + along(jnp.concatenate(a_parts, axis=1), jnp.concatenate(b_parts, axis=1))

    total = lax.fori_loop(0, 3 * ROWS // group, step, jnp.zeros((2 * HIGH, LANES), f32))
    total = total.astype(bf16).astype(f32)

    sent = jnp.zeros((LANES, LANES), f32)
    for h0 in range(0, HIGH, 8):
        a_parts, b_parts = [], []
        for h in range(h0, h0 + 8):
            place = bucket[h : h + 1]
            owner, place = place >> 6, place & 63
            a_parts.append(one_hot(owner, LANES))
            b_parts.append(
                jnp.concatenate(
                    [one_hot(place, BUCKET, total[h : h + 1]), one_hot(place, BUCKET, total[HIGH + h : HIGH + h + 1])],
                    axis=0,
                )
            )
        sent += along(jnp.concatenate(a_parts, axis=1), jnp.concatenate(b_parts, axis=1))
    outgoing[...] = sent.astype(bf16)


def edges_kernel(arrived, rows, mean):
    got = arrived[...].astype(f32)
    half = got.shape[0] // 2
    lane = iota((half, LANES), 1)
    first, second = got[:half], got[half:]
    sums = jnp.where(lane < BUCKET, first, pltpu.roll(second, BUCKET, 1))
    counts = jnp.where(lane < BUCKET, pltpu.roll(first, BUCKET, 1), second)
    targets = jnp.concatenate([rows[:half], rows[half:]], axis=1)
    total = jnp.zeros((2 * HIGH, LANES), f32)
    for h0 in range(0, half, 16):
        a_parts, b_parts = [], []
        for h in range(h0, h0 + 16):
            target = targets[h : h + 1]
            high, low = target >> 7, target & 127
            a_parts.append(
                jnp.concatenate([one_hot(high, HIGH, sums[h : h + 1]), one_hot(high, HIGH, counts[h : h + 1])], axis=0)
            )
            b_parts.append(one_hot(low, LANES))
        total += along(jnp.concatenate(a_parts, axis=1), jnp.concatenate(b_parts, axis=1))
    mean[...] = total[:HIGH] / jnp.maximum(total[HIGH:], 1.0)


def passed(block, axis, distance):
    size = lax.axis_size(axis)
    return lax.ppermute(block, axis, [(i, i + distance) for i in range(size) if 0 <= i + distance < size])


def local(features, conv_weight, conv_bias, fragments, pair_slot, slot_bucket, arrival_row):
    devices = lax.axis_size("gz") * lax.axis_size("yx")
    cells = features.reshape(CELLS, XD)
    ids = fragments.reshape(ROWS, XD)
    slots = pair_slot.reshape(C_OUT * ROWS, XD)
    bucket = slot_bucket.reshape(HIGH, LANES)
    weights = conv_weight.transpose(4, 0, 2, 3, 1).reshape(81, C_IN)
    weights = jnp.pad(weights, ((0, 7), (0, LANES - C_IN)))

    shape = jax.ShapeDtypeStruct
    up, down = pl.pallas_call(
        rows_kernel,
        out_shape=(shape((CZ, XD), bf16), shape((CZ + 2 * Z, XD), bf16)),
        in_specs=whole(2),
        out_specs=tuple(whole(2)),
    )(cells, ids)
    top = passed(down, "yx", 1)
    bottom = passed(up, "yx", -1)
    to_left, to_right = pl.pallas_call(
        columns_kernel,
        out_shape=(shape((1, WIDE), f32), shape((1, WIDE), f32)),
        in_specs=whole(4),
        out_specs=tuple(whole(2)),
        scratch_shapes=[pltpu.VMEM((WIDE, XD), bf16)],
    )(cells, top, bottom, ids)
    left = passed(to_right, "gz", 1)
    right = passed(to_left, "gz", -1)
    affinity, outgoing = pl.pallas_call(
        main_kernel,
        out_shape=(shape((C_OUT * ROWS, XD), bf16), shape((devices, 2 * BUCKET), bf16)),
        in_specs=whole(9) + [pl.BlockSpec(memory_space=pltpu.SMEM)],
        out_specs=tuple(whole(2)),
        scratch_shapes=[
            pltpu.VMEM((DEPTH, XD), bf16),
            pltpu.VMEM((9 * ROWS, DEPTH), bf16),
            pltpu.VMEM((C_OUT * ROWS, XD), f32),
            pltpu.VMEM((C_OUT * ROWS, XD), f32),
        ],
    )(cells, top, bottom, left, right, ids, slots, bucket, weights, conv_bias)
    arrived = lax.all_to_all(outgoing, ("gz", "yx"), split_axis=0, concat_axis=0, tiled=True)
    mean = pl.pallas_call(
        edges_kernel,
        out_shape=shape((HIGH, LANES), f32),
        in_specs=whole(2),
        out_specs=whole(1)[0],
    )(arrived, arrival_row[0])
    return affinity.reshape(C_OUT, Z, YD, XD), mean.reshape(E_OWN)


def solution(mesh):
    return jax.shard_map(
        local,
        mesh=mesh,
        in_specs=(
            P(None, None, "yx", "gz"),
            P(),
            P(),
            P(None, "yx", "gz"),
            P(None, None, "yx", "gz"),
            P(("gz", "yx"), None),
            P(("gz", "yx"), None, None),
        ),
        out_specs=(P(None, None, "yx", "gz"), P(("gz", "yx"))),
        check_vma=False,
    )
```

time: 996 us -> 62.9 us (0.06)
  other arithmetic: 629 us -> 0 us
  matrix products: 292 us -> 0 us
  local copies, waits for them, and re-layouts: 35.7 us -> 5.25 us
  Pallas kernels: 0 us -> 17.7 us
    scatter-add x4 -> x0, other arithmetic: 620 us -> none  [the longest x1 267 us: local(): jax.ops.segment_sum(tallies, slot_ids, slot_total + 1)[:slot_total]]
    conv_general_dilated x1 -> x0, matrix products: 292 us -> none  [convolve(): lax.conv_general_dilated(volume[None], kernel, (1, 1, 1), padding, dimens...]
    pallas_call x0 -> x4, Pallas kernels: none -> 17.7 us  [the longest x1 11.6 us: local(): pl.pallas_call(main_kernel, out_shape=(shape((C_OUT * ROWS, XD), bf16), s...]
    conv_general_dilated x7 -> x0, local copies, waits for them, and re-layouts: 12.9 us -> none  [convolve(): lax.conv_general_dilated(volume[None], kernel, (1, 1, 1), padding, dimens...]
    scatter x1 -> x0, local copies, waits for them, and re-layouts: 12.8 us -> none  [local(): outgoing = jnp.zeros((2, device_total * BUCKET), jnp.float32).at[:, slot_...]
  transfers between devices with their start and end apart: 7 -> 5, of which waited for: 1 -> 3; matrix products, arithmetic and copies ran while one was open for 28% -> 2% of each run, Pallas kernels for 0% -> 0%
where the time goes in v1:
time: 62.9 us; the launch traced here: 62.4 us
  starting transfers between devices  23.9 us (38%)
  Pallas kernels  17.7 us (28%)
  waiting for transfers between devices  14.9 us (24%)
  local copies, waits for them, and re-layouts  5.25 us (8%)
  between operations  0.71 us (1%)
    ppermute x4, starting transfers between devices, passed(): lax.ppermute(block, axis, [(i, i + distance) for i in range(size) if 0 <=...  12.7 us
    pallas_call x1, Pallas kernels, local(): pl.pallas_call(main_kernel, out_shape=(shape((C_OUT * ROWS, XD), bf16), s...  11.6 us
    all_to_all x1, starting transfers between devices, local(): lax.all_to_all(outgoing, ('gz', 'yx'), split_axis=0, concat_axis=0, tiled...  11.2 us
    all_to_all x1, waiting for transfers between devices, local(): lax.all_to_all(outgoing, ('gz', 'yx'), split_axis=0, concat_axis=0, tiled...  8.87 us
    ppermute x4, waiting for transfers between devices, passed(): lax.ppermute(block, axis, [(i, i + distance) for i in range(size) if 0 <=...  6.01 us
    unnamed x14, local copies, waits for them, and re-layouts  3.17 us
    pallas_call x1, Pallas kernels, local(): pl.pallas_call(edges_kernel, out_shape=shape((HIGH, LANES), f32), in_spec...  2.39 us
    pallas_call x1, Pallas kernels, local(): pl.pallas_call(columns_kernel, out_shape=(shape((1, WIDE), f32), shape((1...  1.87 us
  transfers between devices with their start and end apart: 5, of which 3 were waited for; matrix products, arithmetic and copies ran while one was open for 2% of the time, Pallas kernels for 0%

profile of v1, /device:TPU:1, one launch (start us, length us, event | category | flops | bytes accessed | tf_op | source)
XLA Modules:
  0.0 62.4 jit_solution(18402501956126890301)
XLA Ops:
  0.6 1.8 %shard_map.86 = (bf16[48,256]{1,0:T(8,128)(2,1)}, bf16[56,256]{1,0:T(8,128)(2,1)}) custom-call(bf16[768,256]{1,0:T(8,128)(2,1)} %bitcast.12, s32[64,256]{1,0:T(8,128)} %bitcast.15), custom_call_target="tpu_custom_call" | custom-call | tf_op jit(solution)/shard_map/pallas_call | solution.py:199
  2.5 3.9 %collective-permute-start = (bf16[56,256]{1,0:T(8,128)(2,1)}, bf16[56,256]{1,0:T(8,128)(2,1)S(1)}, u32[]{:S(2)}, u32[]{:S(2)}) collective-permute-start(bf16[56,256]{1,0:T(8,128)(2,1)} %get-tuple-element.8), channel_id=1, source_target_pairs={{0,1},{1,2},{2,3},{3,4},{4,5},{5,6},{6,7},{7,8},{8,9},{9,10},{10,1... | collective-permute-start | bytes 86024 | tf_op jit(solution)/shard_map/ppermute | solution.py:186
  6.4 0.0 copy-start.3
  6.4 1.3 %collective-permute-start.1 = (bf16[48,256]{1,0:T(8,128)(2,1)}, bf16[48,256]{1,0:T(8,128)(2,1)S(1)}, u32[]{:S(2)}, u32[]{:S(2)}) collective-permute-start(bf16[48,256]{1,0:T(8,128)(2,1)} %get-tuple-element.9), channel_id=1, source_target_pairs={{1,0},{2,1},{3,2},{4,3},{5,4},{6,5},{7,6},{8,7},{9,8},{10,9},{11,1... | collective-permute-start | bytes 73736 | tf_op jit(solution)/shard_map/ppermute | solution.py:186
  7.7 3.5 %collective-permute-done.1.bottom = bf16[48,256]{1,0:T(8,128)(2,1)S(1)} collective-permute-done((bf16[48,256]{1,0:T(8,128)(2,1)}, bf16[48,256]{1,0:T(8,128)(2,1)S(1)}, u32[]{:S(2)}, u32[]{:S(2)}) %collective-permute-start.1) | collective-permute-done | bytes 24608 | tf_op jit(solution)/shard_map/ppermute | solution.py:186
  11.2 0.0 collective-permute-done.top
  11.2 0.6 copy-done.1
  11.8 0.6 copy-done
  12.4 1.9 %shard_map.87 = (f32[1,1024]{1,0:T(1,128)}, f32[1,1024]{1,0:T(1,128)}) custom-call(bf16[768,256]{1,0:T(8,128)(2,1)} %bitcast.13, bf16[56,256]{1,0:T(8,128)(2,1)} %copy-done, bf16[48,256]{1,0:T(8,128)(2,1)} %copy-done.1, s32[64,256]{1,0:T(8,128)} %bitcast.16), custom_call_target="tpu_custom_call" | custom-call | tf_op jit(solution)/shard_map/pallas_call | solution.py:207
  14.3 5.5 %collective-permute-start.2 = (f32[1,1024]{1,0:T(1,128)}, f32[1,1024]{1,0:T(1,128)S(1)}, u32[]{:S(2)}, u32[]{:S(2)}) collective-permute-start(f32[1,1024]{1,0:T(1,128)} %get-tuple-element.10), channel_id=1, source_target_pairs={{0,16},{16,32},{32,48},{48,64},{64,80},{80,96},{96,112},{1,17},{17... | collective-permute-start | bytes 12296 | tf_op jit(solution)/shard_map/ppermute | solution.py:186
  19.8 1.9 %collective-permute-start.3 = (f32[1,1024]{1,0:T(1,128)}, f32[1,1024]{1,0:T(1,128)S(1)}, u32[]{:S(2)}, u32[]{:S(2)}) collective-permute-start(f32[1,1024]{1,0:T(1,128)} %get-tuple-element.11), channel_id=1, source_target_pairs={{16,0},{32,16},{48,32},{64,48},{80,64},{96,80},{112,96},{17,1},{33... | collective-permute-start | bytes 12296 | tf_op jit(solution)/shard_map/ppermute | solution.py:186
  21.7 0.0 copy-done.3
  21.8 0.6 pad.4.weights
  22.4 0.0 collective-permute-done.2.left
  22.4 2.5 %collective-permute-done.3.right = f32[1,1024]{1,0:T(1,128)S(1)} collective-permute-done((f32[1,1024]{1,0:T(1,128)}, f32[1,1024]{1,0:T(1,128)S(1)}, u32[]{:S(2)}, u32[]{:S(2)}) %collective-permute-start.3) | collective-permute-done | bytes 4128 | tf_op jit(solution)/shard_map/ppermute | solution.py:186
  24.9 0.0 copy-done.4
  24.9 0.6 copy-done.5
  25.5 11.6 %shard_map.88 = (bf16[192,256]{1,0:T(8,128)(2,1)}, bf16[128,128]{1,0:T(8,128)(2,1)}) custom-call(bf16[768,256]{1,0:T(8,128)(2,1)} %bitcast.14, bf16[56,256]{1,0:T(8,128)(2,1)} %copy-done, bf16[48,256]{1,0:T(8,128)(2,1)} %copy-done.1, f32[1,1024]{1,0:T(1,128)} %copy-done.4, f32[1,1024]{1,0:T(1,128)} %copy-done.5, s32[64,256]{1,0:T(8,128)} %bitcast.17, ...), custom_call_target="tpu_custom_call" | custom-call | tf_op jit(solution)/shard_map/pallas_call | solution.py:216
  37.1 1.4 %copy.17 = bf16[128,1,128]{2,1,0:T(2,128)(2,1)} copy(bf16[128,1,128]{2,0,1:T(8,128)(2,1)} %bitcast.21) | data formatting | bytes 65536 | tf_op jit(solution)/shard_map/all_to_all | solution.py:228
  38.6 11.2 %all-to-all-start = ((bf16[128,1,128]{2,1,0:T(2,128)(2,1)}), bf16[128,1,128]{2,1,0:T(2,128)(2,1)S(1)}, u32[]{:S(2)}, u32[]{:S(2)}) async-start(bf16[128,1,128]{2,1,0:T(2,128)(2,1)} %copy.17), calls=%async_computation | async-start | bytes 131072 | tf_op jit(solution)/shard_map/all_to_all | solution.py:228
  49.8 0.7 %copy.18 = s32[1,128,64]{2,1,0:T(8,128)} copy(s32[1,128,64]{1,2,0:T(8,128)S(1)} %copy-done.2) | data formatting | bytes 65536 | tf_op args[6]
  50.5 8.9 %all-to-all-done = bf16[128,1,128]{2,1,0:T(2,128)(2,1)S(1)} async-done(((bf16[128,1,128]{2,1,0:T(2,128)(2,1)}), bf16[128,1,128]{2,1,0:T(2,128)(2,1)S(1)}, u32[]{:S(2)}, u32[]{:S(2)}) %all-to-all-start) | async-done | bytes 32800 | tf_op jit(solution)/shard_map/all_to_all | solution.py:228
  59.4 0.6 copy.21
  60.0 2.4 %shard_map.89 = f32[32,128]{1,0:T(8,128)} custom-call(bf16[128,128]{1,0:T(8,128)(2,1)} %bitcast.20, s32[128,64]{1,0:T(8,128)} %bitcast.18), custom_call_target="tpu_custom_call" | custom-call | tf_op jit(solution)/shard_map/pallas_call | solution.py:229
  (8 shorter events, 0.0 us)
Async XLA Ops:
  2.5 8.7 %collective-permute-start = (bf16[56,256]{1,0:T(8,128)(2,1)}, bf16[56,256]{1,0:T(8,128)(2,1)S(1)}, u32[]{:S(2)}, u32[]{:S(2)}) collective-permute-start(bf16[56,256]{1,0:T(8,128)(2,1)} %get-tuple-element.8), channel_id=1, source_target_pairs={{0,1},{1,2},{2,3},{3,4},{4,5},{5,6},{6,7},{7,8},{8,9},{9,10},{10,1... | collective-permute-start | bytes 86024 | tf_op jit(solution)/shard_map/ppermute | solution.py:186
  6.4 15.3 %copy-start.3 = (bf16[3,12,3,3,3]{1,4,3,2,0:T(4,128)(2,1)S(1)}, bf16[3,12,3,3,3]{1,4,3,2,0:T(4,128)(2,1)}, u32[]{:S(2)}) copy-start(bf16[3,12,3,3,3]{1,4,3,2,0:T(4,128)(2,1)} %param.8) | copy-start | bytes 5836
  6.4 4.8 %collective-permute-start.1 = (bf16[48,256]{1,0:T(8,128)(2,1)}, bf16[48,256]{1,0:T(8,128)(2,1)S(1)}, u32[]{:S(2)}, u32[]{:S(2)}) collective-permute-start(bf16[48,256]{1,0:T(8,128)(2,1)} %get-tuple-element.9), channel_id=1, source_target_pairs={{1,0},{2,1},{3,2},{4,3},{5,4},{6,5},{7,6},{8,7},{9,8},{10,9},{11,1... | collective-permute-start | bytes 73736 | tf_op jit(solution)/shard_map/ppermute | solution.py:186
  11.2 0.6 copy-start.1
  11.8 0.6 copy-start
  14.3 8.1 %collective-permute-start.2 = (f32[1,1024]{1,0:T(1,128)}, f32[1,1024]{1,0:T(1,128)S(1)}, u32[]{:S(2)}, u32[]{:S(2)}) collective-permute-start(f32[1,1024]{1,0:T(1,128)} %get-tuple-element.10), channel_id=1, source_target_pairs={{0,16},{16,32},{32,48},{48,64},{64,80},{80,96},{96,112},{1,17},{17... | collective-permute-start | bytes 12296 | tf_op jit(solution)/shard_map/ppermute | solution.py:186
  19.8 5.1 %collective-permute-start.3 = (f32[1,1024]{1,0:T(1,128)}, f32[1,1024]{1,0:T(1,128)S(1)}, u32[]{:S(2)}, u32[]{:S(2)}) collective-permute-start(f32[1,1024]{1,0:T(1,128)} %get-tuple-element.11), channel_id=1, source_target_pairs={{16,0},{32,16},{48,32},{64,48},{80,64},{96,80},{112,96},{17,1},{33... | collective-permute-start | bytes 12296 | tf_op jit(solution)/shard_map/ppermute | solution.py:186
  22.4 2.5 %copy-start.4 = (f32[1,1024]{1,0:T(1,128)}, f32[1,1024]{1,0:T(1,128)S(1)}, u32[]{:S(2)}) copy-start(f32[1,1024]{1,0:T(1,128)S(1)} %collective-permute-done.2.left) | copy-start | bytes 12292
  24.9 0.6 copy-start.5
  38.6 11.2 %copy-start.2 = (s32[1,128,64]{1,2,0:T(8,128)S(1)}, s32[1,128,64]{1,2,0:T(8,128)}, u32[]{:S(2)}) copy-start(s32[1,128,64]{1,2,0:T(8,128)} %param.13) | copy-start | bytes 98308
  38.6 20.8 %all-to-all-start = ((bf16[128,1,128]{2,1,0:T(2,128)(2,1)}), bf16[128,1,128]{2,1,0:T(2,128)(2,1)S(1)}, u32[]{:S(2)}, u32[]{:S(2)}) async-start(bf16[128,1,128]{2,1,0:T(2,128)(2,1)} %copy.17), calls=%async_computation | async-start | bytes 131072 | tf_op jit(solution)/shard_map/all_to_all | solution.py:228

commit v2 on v1

v2 whole, which is shorter than its diff:
```python
import functools

import jax
import jax.numpy as jnp
from jax import lax
from jax.experimental import pallas as pl
from jax.experimental.pallas import tpu as pltpu
from jax.sharding import PartitionSpec as P

C_IN, C_OUT, Z, YD, XD = 12, 3, 4, 16, 256
BUCKET, E_OWN, P_LOC = 64, 4096, 4096
CZ = C_IN * Z
CELLS = CZ * YD
DEPTH = CELLS + 2 * CZ + 32
WIDE = DEPTH + 2 * Z * YD
ROWS = Z * YD
LANES = 128
HIGH = P_LOC // LANES

TAP_ROWS = 9 * ROWS
PART = C_OUT * ROWS

f32, bf16, i32 = jnp.float32, jnp.bfloat16, jnp.int32


def iota(shape, dim):
    return lax.broadcasted_iota(i32, shape, dim)


def along(a, b):
    return lax.dot_general(a, b, (((1,), (1,)), ((), ())), preferred_element_type=f32)


def whole(count):
    return [pl.BlockSpec(memory_space=pltpu.VMEM)] * count


def near(shape, dtype):
    return pltpu.VMEM(shape, dtype)


def held(x):
    return pltpu.with_memory_space_constraint(x, pltpu.VMEM)


def rows_kernel(cells, ids, up, down):
    row = iota((2 * CZ, CELLS), 0)
    wanted = jnp.where(row < CZ, row * YD, (row - CZ) * YD + YD - 1)
    pick = jnp.where(iota((2 * CZ, CELLS), 1) == wanted, 1.0, 0.0).astype(bf16)
    picked = jnp.dot(pick, cells[...], preferred_element_type=f32).astype(bf16)
    up[...] = picked[:CZ]
    down[:CZ] = picked[CZ:]
    last = jnp.concatenate([ids[(z + 1) * YD - 1 : (z + 1) * YD] for z in range(Z)], axis=0)
    pair = jnp.concatenate([last >> 7, last & 127], axis=0)
    down[CZ:] = pair.astype(f32).astype(bf16)


def pick_ends():
    row, lane = iota((8, XD), 0), iota((8, XD), 1)
    return jnp.where((row < 2) & (lane == row * (XD - 1)), 1.0, 0.0).astype(bf16)


def columns_kernel(cells, top, bottom, ids, after, left, right, wide):
    wide[:CELLS] = cells[...]
    wide[CELLS : CELLS + CZ] = top[:CZ]
    wide[CELLS + CZ : CELLS + 2 * CZ] = bottom[...]
    wide[CELLS + 2 * CZ : DEPTH] = jnp.zeros((DEPTH - CELLS - 2 * CZ, XD), bf16)
    wide[DEPTH : DEPTH + ROWS] = (ids[...] >> 7).astype(f32).astype(bf16)
    wide[DEPTH + ROWS :] = (ids[...] & 127).astype(f32).astype(bf16)
    picked = along(pick_ends(), wide[...])
    left[...] = picked[0:1]
    right[...] = picked[1:2]


def taps_kernel(cells, weights, bias, taps, logits, flat):
    flat[...] = jnp.zeros(flat.shape, f32)
    for i in range(27):
        flat[8 * i : 8 * i + 3, :C_IN] = weights[i].astype(f32)
    k = iota((LANES, DEPTH), 1)
    channel = jnp.where(k < CELLS, k // (Z * YD), ((k - CELLS) % CZ) // Z)
    channel = jnp.where(k < CELLS + 2 * CZ, channel, LANES)
    spread = jnp.where(iota((LANES, DEPTH), 0) == channel, 1.0, 0.0).astype(bf16)
    lines = jnp.dot(flat[...].astype(bf16), spread, preferred_element_type=f32)
    for t in range(DEPTH // LANES):
        y, k = iota((YD, LANES), 0), iota((YD, LANES), 1) + t * LANES
        inner = k < CELLS
        z_in = jnp.where(inner, (k // YD) % Z, (k - CELLS) % Z)
        y_in = jnp.where(inner, k % YD, jnp.where(k < CELLS + CZ, -1, YD))
        y_in = jnp.where(k < CELLS + 2 * CZ, y_in, 3 * YD)
        dy = y_in - y + 1
        for e in range(3):
            for o in range(C_OUT):
                bands = []
                for a in range(3):
                    band = jnp.zeros((YD, LANES), f32)
                    for b in range(3):
                        r = (o * 9 + a * 3 + b) * 8 + e
                        band = jnp.where(dy == b, lines[r : r + 1, t * LANES : (t + 1) * LANES], band)
                    bands.append(band)
                for z in range(Z):
                    tap = jnp.zeros((YD, LANES), f32)
                    for a in range(3):
                        if 0 <= z + a - 1 < Z:
                            tap = jnp.where(z_in == z + a - 1, bands[a], tap)
                    row = ((e * C_OUT + o) * Z + z) * YD
                    taps[row : row + YD, t * LANES : (t + 1) * LANES] = tap.astype(bf16)
    product = jnp.dot(taps[:, :CELLS], cells[...], preferred_element_type=f32)
    channel = iota((PART, XD), 0) // ROWS
    bias = jnp.where(channel == 0, bias[0], jnp.where(channel == 1, bias[1], bias[2]))
    logits[...] = shifted(product) + bias


def shifted(product):
    lane = iota((PART, XD), 1)
    total = product[PART : 2 * PART]
    total += jnp.where(lane == 0, 0.0, pltpu.roll(product[:PART], 1, 1))
    return total + jnp.where(lane == XD - 1, 0.0, pltpu.roll(product[2 * PART :], XD - 1, 1))


def sigmoid(x):
    return (1.0 / (1.0 + jnp.exp(-x))).astype(bf16)


def one_hot(line, count, value=None):
    hit = iota((count, line.shape[1]), 0) == line
    return jnp.where(hit, 1.0 if value is None else value, 0.0).astype(bf16)


def pair_hot(line, count, first, second):
    return jnp.concatenate([one_hot(line, count, first), one_hot(line, count, second)], axis=0)


def inner_kernel(taps, logits, top, bottom, ids, slots, full, sums, ends, halo, value, cross):
    halo[:CZ] = top[:CZ]
    halo[CZ : 2 * CZ] = bottom[...]
    halo[2 * CZ :] = jnp.zeros((LANES - 2 * CZ, XD), bf16)
    total = logits[...] + shifted(jnp.dot(taps[:, CELLS:], halo[...], preferred_element_type=f32))
    full[...] = total
    soft = sigmoid(total).astype(f32)

    here = ids[...]
    m, n = iota((ROWS, XD), 0), iota((ROWS, XD), 1)
    under_z = jnp.concatenate([here[:YD], here[:-YD]], axis=0)
    above = top[CZ:].astype(f32)
    above = (above[:Z] * 128.0 + above[Z:]).astype(i32)
    above = jnp.concatenate([jnp.broadcast_to(above[z : z + 1], (YD, XD)) for z in range(Z)], axis=0)
    under_y = jnp.where(m % YD == 0, above, pltpu.roll(here, 1, 0))
    under_x = jnp.where(n == 0, here, pltpu.roll(here, 1, 1))
    inside = (n > 0) & (n < XD - 1)
    whole_cross = []
    for d, under in enumerate((under_z, under_y, under_x)):
        differs = jnp.where((here != under) & (under > 0), 1.0, 0.0)
        whole_cross.append(differs)
        differs = jnp.where(inside, differs, 0.0)
        cross[d * ROWS : (d + 1) * ROWS] = differs
        value[d * ROWS : (d + 1) * ROWS] = differs * soft[d * ROWS : (d + 1) * ROWS]
    pad = jnp.zeros((XD - PART, XD), f32)
    numbers = slots[...]
    kinds = jnp.concatenate(
        whole_cross + [pad, (numbers >> 7).astype(f32), pad, (numbers & 127).astype(f32), pad], axis=0
    )
    ends[...] = along(pick_ends(), kinds.astype(bf16))

    group = 16

    def step(i, total):
        a_parts, b_parts = [], []
        base = pl.multiple_of(i * group, group)
        slot_g, value_g, cross_g = slots[pl.ds(base, group)], value[pl.ds(base, group)], cross[pl.ds(base, group)]
        for j in range(group):
            slot = slot_g[j : j + 1]
            a_parts.append(pair_hot(slot >> 7, HIGH, value_g[j : j + 1], cross_g[j : j + 1]))
            b_parts.append(one_hot(slot & 127, LANES))
        return total + along(jnp.concatenate(a_parts, axis=1), jnp.concatenate(b_parts, axis=1))

    sums[...] = lax.fori_loop(0, PART // group, step, jnp.zeros((2 * HIGH, LANES), f32))


def send_kernel(taps, logits, left, right, ids_ends, ends, sums, bucket, affinity, outgoing):
    row = iota((8, DEPTH), 0)
    left_row = jnp.where(row == 0, left[:, :DEPTH], 0.0).astype(bf16)
    right_row = jnp.where(row == 0, right[:, :DEPTH], 0.0).astype(bf16)
    first = along(taps[:PART], left_row)[:, 0:1]
    last = along(taps[2 * PART :], right_row)[:, 0:1]
    lane = iota((PART, XD), 1)
    soft = sigmoid(logits[...] + jnp.where(lane == 0, first, jnp.where(lane == XD - 1, last, 0.0)))
    affinity[...] = soft
    soft = along(pick_ends(), soft)
    soft = jnp.concatenate([soft, jnp.zeros((8, XD - PART), f32)], axis=1)

    beside = left[:, DEPTH : DEPTH + ROWS] * 128.0 + left[:, DEPTH + ROWS :]
    here = ids_ends[:, DEPTH : DEPTH + ROWS] * 128.0 + ids_ends[:, DEPTH + ROWS :]
    differs = jnp.where((beside != here) & (beside > 0.0), 1.0, 0.0)
    differs = jnp.concatenate([jnp.zeros((1, 2 * ROWS), f32), differs, jnp.zeros((1, XD - PART), f32)], axis=1)
    total = sums[...]
    a_parts, b_parts = [], []
    for end in range(2):
        cross = ends[end : end + 1, :XD]
        if end == 0:
            cross = cross + differs
        high = ends[end : end + 1, XD : 2 * XD].astype(i32)
        low = ends[end : end + 1, 2 * XD :].astype(i32)
        a_parts.append(pair_hot(high, HIGH, soft[end : end + 1] * cross, cross))
        b_parts.append(one_hot(low, LANES))
    total += along(jnp.concatenate(a_parts, axis=1), jnp.concatenate(b_parts, axis=1))
    total = total.astype(bf16).astype(f32)

    sent = jnp.zeros((LANES, LANES), f32)
    for h0 in range(0, HIGH, 16):
        a_parts, b_parts = [], []
        for h in range(h0, h0 + 16):
            place = bucket[h : h + 1]
            a_parts.append(one_hot(place >> 6, LANES))
            b_parts.append(pair_hot(place & 63, BUCKET, total[h : h + 1], total[HIGH + h : HIGH + h + 1]))
        sent += along(jnp.concatenate(a_parts, axis=1), jnp.concatenate(b_parts, axis=1))
    outgoing[...] = sent


def edges_kernel(arrived, rows, mean):
    n = arrived.shape[0]
    same = jnp.where(iota((n, n), 0) == iota((n, n), 1), 1.0, 0.0).astype(bf16)
    got = lax.dot_general(arrived[...].astype(bf16), same, (((0,), (0,)), ((), ())), preferred_element_type=f32)
    total = jnp.zeros((2 * HIGH, LANES), f32)
    for q0 in range(0, BUCKET, 16):
        a_parts, b_parts = [], []
        for q in range(q0, q0 + 16):
            target = rows[q : q + 1]
            a_parts.append(pair_hot(target >> 7, HIGH, got[q : q + 1], got[BUCKET + q : BUCKET + q + 1]))
            b_parts.append(one_hot(target & 127, LANES))
        total += along(jnp.concatenate(a_parts, axis=1), jnp.concatenate(b_parts, axis=1))
    mean[...] = total[:HIGH] / jnp.maximum(total[HIGH:], 1.0)


def passed(block, axis, distance):
    size = lax.axis_size(axis)
    return lax.ppermute(block, axis, [(i, i + distance) for i in range(size) if 0 <= i + distance < size])


def local(features, conv_weight, conv_bias, fragments, pair_slot, slot_bucket, arrival_row):
    devices = lax.axis_size("gz") * lax.axis_size("yx")
    cells = features.reshape(CELLS, XD)
    ids = fragments.reshape(ROWS, XD)
    slots = pair_slot.reshape(PART, XD)
    bucket = slot_bucket.reshape(HIGH, LANES)
    weights = conv_weight.transpose(0, 2, 3, 4, 1).reshape(27, 3, C_IN)
    scalar = pl.BlockSpec(memory_space=pltpu.SMEM)
    up, down = pl.pallas_call(
        rows_kernel,
        out_shape=(near((CZ, XD), bf16), near((CZ + 2 * Z, XD), bf16)),
        in_specs=whole(2),
        out_specs=tuple(whole(2)),
    )(cells, ids)
    top = held(passed(down, "yx", 1))
    bottom = held(passed(up, "yx", -1))
    taps, logits = pl.pallas_call(
        taps_kernel,
        out_shape=(near((TAP_ROWS, DEPTH), bf16), near((PART, XD), f32)),
        in_specs=whole(2) + [scalar],
        out_specs=tuple(whole(2)),
        scratch_shapes=[pltpu.VMEM((27 * 8, LANES), f32)],
    )(cells, weights, conv_bias)
    to_left, to_right = pl.pallas_call(
        columns_kernel,
        out_shape=(near((1, WIDE), f32), near((1, WIDE), f32)),
        in_specs=whole(5),
        out_specs=tuple(whole(2)),
        scratch_shapes=[pltpu.VMEM((WIDE, XD), bf16)],
    )(cells, top, bottom, ids, held(logits))
    left = held(passed(to_right, "gz", 1))
    right = held(passed(to_left, "gz", -1))
    taps = held(taps)
    logits, sums, ends = pl.pallas_call(
        inner_kernel,
        out_shape=(near((PART, XD), f32), near((2 * HIGH, LANES), f32), near((8, 3 * XD), f32)),
        in_specs=whole(6),
        out_specs=tuple(whole(3)),
        scratch_shapes=[pltpu.VMEM((LANES, XD), bf16), pltpu.VMEM((PART, XD), f32), pltpu.VMEM((PART, XD), f32)],
    )(taps, held(logits), top, bottom, ids, slots)
    affinity, outgoing = pl.pallas_call(
        send_kernel,
        out_shape=(jax.ShapeDtypeStruct((PART, XD), bf16), near((devices, 2 * BUCKET), f32)),
        in_specs=whole(8),
        out_specs=tuple(whole(2)),
    )(taps, held(logits), left, right, held(to_left), held(ends), held(sums), bucket)
    arrived = lax.all_to_all(outgoing, ("gz", "yx"), split_axis=0, concat_axis=0, tiled=True)
    mean = pl.pallas_call(
        edges_kernel,
        out_shape=jax.ShapeDtypeStruct((HIGH, LANES), f32),
        in_specs=whole(2),
        out_specs=whole(1)[0],
    )(held(arrived), arrival_row[0].T)
    return affinity.reshape(C_OUT, Z, YD, XD), mean.reshape(E_OWN)


def solution(mesh):
    return jax.shard_map(
        local,
        mesh=mesh,
        in_specs=(
            P(None, None, "yx", "gz"),
            P(),
            P(),
            P(None, "yx", "gz"),
            P(None, None, "yx", "gz"),
            P(("gz", "yx"), None),
            P(("gz", "yx"), None, None),
        ),
        out_specs=(P(None, None, "yx", "gz"), P(("gz", "yx"))),
        check_vma=False,
    )
```

time: 62.9 us -> 52.5 us (0.83)
  blocking collectives: 0 us -> 21.2 us
  waiting for transfers between devices: 14.9 us -> 1.14 us
  starting transfers between devices: 23.9 us -> 12.7 us
  local copies, waits for them, and re-layouts: 5.25 us -> 0 us
  Pallas kernels: 17.7 us -> 16.4 us
    all_to_all x0 -> x1, blocking collectives: none -> 21.2 us  [local(): lax.all_to_all(outgoing, ('gz', 'yx'), split_axis=0, concat_axis=0, tiled...]
    all_to_all x1 -> x0, starting transfers between devices: 11.2 us -> none  [local(): lax.all_to_all(outgoing, ('gz', 'yx'), split_axis=0, concat_axis=0, tiled...]
    all_to_all x1 -> x0, waiting for transfers between devices: 8.87 us -> none  [local(): lax.all_to_all(outgoing, ('gz', 'yx'), split_axis=0, concat_axis=0, tiled...]
    ppermute x4, waiting for transfers between devices: 6.01 us -> 1.14 us  [passed(): lax.ppermute(block, axis, [(i, i + distance) for i in range(size) if 0 <=...]
    unnamed x14 -> x0, local copies, waits for them, and re-layouts: 3.17 us -> none
    all_to_all x1 -> x0, local copies, waits for them, and re-layouts: 1.43 us -> none  [local(): lax.all_to_all(outgoing, ('gz', 'yx'), split_axis=0, concat_axis=0, tiled...]
    pallas_call x4 -> x6, Pallas kernels: 17.7 us -> 16.4 us  [the longest x1 7.26 us: local(): pl.pallas_call(inner_kernel, out_shape=(near((PART, XD), f32), near((2 *...]
  transfers between devices with their start and end apart: 5 -> 4, of which waited for: 3 -> 1; matrix products, arithmetic and copies ran while one was open for 2% -> 0% of each run, Pallas kernels for 0% -> 18%
where the time goes in v2:
time: 52.5 us; the launch traced here: 52.1 us
  blocking collectives  21.2 us (40%)
  Pallas kernels  16.4 us (31%)
  starting transfers between devices  12.7 us (24%)
  waiting for transfers between devices  1.14 us (2%)
  between operations  0.7 us (1%)
    all_to_all x1, blocking collectives, local(): lax.all_to_all(outgoing, ('gz', 'yx'), split_axis=0, concat_axis=0, tiled...  21.2 us
    ppermute x4, starting transfers between devices, passed(): lax.ppermute(block, axis, [(i, i + distance) for i in range(size) if 0 <=...  12.7 us
    pallas_call x1, Pallas kernels, local(): pl.pallas_call(inner_kernel, out_shape=(near((PART, XD), f32), near((2 *...  7.26 us
    pallas_call x1, Pallas kernels, local(): pl.pallas_call(edges_kernel, out_shape=jax.ShapeDtypeStruct((HIGH, LANES)...  2.35 us
    pallas_call x1, Pallas kernels, local(): pl.pallas_call(send_kernel, out_shape=(jax.ShapeDtypeStruct((PART, XD), b...  2.19 us
    pallas_call x1, Pallas kernels, local(): pl.pallas_call(taps_kernel, out_shape=(near((TAP_ROWS, DEPTH), bf16), nea...  2.13 us
    pallas_call x1, Pallas kernels, local(): pl.pallas_call(columns_kernel, out_shape=(near((1, WIDE), f32), near((1,...  1.22 us
    pallas_call x1, Pallas kernels, local(): pl.pallas_call(rows_kernel, out_shape=(near((CZ, XD), bf16), near((CZ + 2...  1.21 us
  transfers between devices with their start and end apart: 4, of which 1 were waited for; matrix products, arithmetic and copies ran while one was open for 0% of the time, Pallas kernels for 18%

profile of v2, /device:TPU:1, one launch (start us, length us, event | category | flops | bytes accessed | tf_op | source)
XLA Modules:
  0.0 52.1 jit_solution(10587824903890453898)
XLA Ops:
  0.6 1.2 %shard_map.87 = (bf16[48,256]{1,0:T(8,128)(2,1)S(1)}, bf16[56,256]{1,0:T(8,128)(2,1)S(1)}) custom-call(bf16[768,256]{1,0:T(8,128)(2,1)} %bitcast.18, s32[64,256]{1,0:T(8,128)} %bitcast.21), custom_call_target="tpu_custom_call" | custom-call | tf_op jit(solution)/shard_map/pallas_call | solution.py:247
  1.8 3.9 %collective-permute-start = (bf16[56,256]{1,0:T(8,128)(2,1)S(1)}, bf16[56,256]{1,0:T(8,128)(2,1)S(1)}, u32[]{:S(2)}, u32[]{:S(2)}) collective-permute-start(bf16[56,256]{1,0:T(8,128)(2,1)S(1)} %get-tuple-element.15), channel_id=1, source_target_pairs={{0,1},{1,2},{2,3},{3,4},{4,5},{5,6},{6,7},{7,8},{8,9},{9,10},{10,1... | collective-permute-start | bytes 86024 | tf_op jit(solution)/shard_map/ppermute | solution.py:236
  5.8 1.3 %collective-permute-start.1 = (bf16[48,256]{1,0:T(8,128)(2,1)S(1)}, bf16[48,256]{1,0:T(8,128)(2,1)S(1)}, u32[]{:S(2)}, u32[]{:S(2)}) collective-permute-start(bf16[48,256]{1,0:T(8,128)(2,1)S(1)} %get-tuple-element.16), channel_id=1, source_target_pairs={{1,0},{2,1},{3,2},{4,3},{5,4},{6,5},{7,6},{8,7},{9,8},{10,9},{11,1... | collective-permute-start | bytes 73736 | tf_op jit(solution)/shard_map/ppermute | solution.py:236
  7.1 2.1 %shard_map.86 = (bf16[576,896]{1,0:T(8,128)(2,1)S(1)}, f32[192,256]{1,0:T(8,128)S(1)}) custom-call(bf16[768,256]{1,0:T(8,128)(2,1)} %bitcast.19, bf16[27,3,12]{2,1,0:T(4,128)(2,1)} %bitcast.26, f32[3]{0:T(128)} %bias.1), custom_call_target="tpu_custom_call" | custom-call | tf_op jit(solution)/shard_map/pallas_call | solution.py:255
  9.2 1.1 %collective-permute-done.1.bottom = bf16[48,256]{1,0:T(8,128)(2,1)S(1)} collective-permute-done((bf16[48,256]{1,0:T(8,128)(2,1)S(1)}, bf16[48,256]{1,0:T(8,128)(2,1)S(1)}, u32[]{:S(2)}, u32[]{:S(2)}) %collective-permute-start.1) | collective-permute-done | bytes 24608 | tf_op jit(solution)/shard_map/ppermute | solution.py:236
  10.4 0.0 collective-permute-done.top
  10.4 1.2 %shard_map.89 = (f32[1,1024]{1,0:T(1,128)S(1)}, f32[1,1024]{1,0:T(1,128)S(1)}) custom-call(bf16[768,256]{1,0:T(8,128)(2,1)} %bitcast.20, bf16[56,256]{1,0:T(8,128)(2,1)S(1)} %collective-permute-done.top, bf16[48,256]{1,0:T(8,128)(2,1)S(1)} %collective-permute-done.1.bottom, s32[64,256]{1,0:T(8,128)} %bitcast.22, f32[192,256]{1,0:T(8,128)S(1)} %get-tuple-element.14.logits.after), custom_call_target="tpu_custom_call" | custom-call | tf_op jit(solution)/shard_map/pallas_call | solution.py:262
  11.6 5.6 %collective-permute-start.2 = (f32[1,1024]{1,0:T(1,128)S(1)}, f32[1,1024]{1,0:T(1,128)S(1)}, u32[]{:S(2)}, u32[]{:S(2)}) collective-permute-start(f32[1,1024]{1,0:T(1,128)S(1)} %get-tuple-element.18), channel_id=1, source_target_pairs={{0,16},{16,32},{32,48},{48,64},{64,80},{80,96},{96,112},{1,17},{17... | collective-permute-start | bytes 12296 | tf_op jit(solution)/shard_map/ppermute | solution.py:236
  17.2 1.9 %collective-permute-start.3 = (f32[1,1024]{1,0:T(1,128)S(1)}, f32[1,1024]{1,0:T(1,128)S(1)}, u32[]{:S(2)}, u32[]{:S(2)}) collective-permute-start(f32[1,1024]{1,0:T(1,128)S(1)} %get-tuple-element.19.ids_ends), channel_id=1, source_target_pairs={{16,0},{32,16},{48,32},{64,48},{80,64},{96,80},{112,96},{17,1},{33... | collective-permute-start | bytes 12296 | tf_op jit(solution)/shard_map/ppermute | solution.py:236
  19.1 7.3 %shard_map.88 = (f32[192,256]{1,0:T(8,128)S(1)}, f32[64,128]{1,0:T(8,128)S(1)}, f32[8,768]{1,0:T(8,128)S(1)}) custom-call(bf16[576,896]{1,0:T(8,128)(2,1)S(1)} %get-tuple-element.13.taps, f32[192,256]{1,0:T(8,128)S(1)} %get-tuple-element.14.logits.after, bf16[56,256]{1,0:T(8,128)(2,1)S(1)} %collective-permute-done.top, ...), custom_call_target="tpu_custom_call" | custom-call | tf_op jit(solution)/shard_map/pallas_call | solution.py:272
  26.4 0.0 collective-permute-done.2.left
  26.4 0.0 collective-permute-done.3.right
  26.4 2.2 %shard_map.90 = (bf16[192,256]{1,0:T(8,128)(2,1)}, f32[128,128]{1,0:T(8,128)S(1)}) custom-call(bf16[576,896]{1,0:T(8,128)(2,1)S(1)} %get-tuple-element.13.taps, f32[192,256]{1,0:T(8,128)S(1)} %get-tuple-element.17.logits, f32[1,1024]{1,0:T(1,128)S(1)} %collective-permute-done.2.left, f32[1,1024]{1,0:T(1,128)S(1)} %collective-permute-done.3.right, ...), custom_call_target="tpu_custom_call" | custom-call | tf_op jit(solution)/shard_map/pallas_call | solution.py:279
  28.6 21.2 %all_to_all.11 = f32[128,1,128]{2,1,0:T(1,128)S(1)} all-to-all(f32[128,1,128]{2,1,0:T(1,128)S(1)} %bitcast.17), channel_id=1, replica_groups=mesh['gz'=8,'yx'=16] {'gz','yx'}, dimensions={0} | all-to-all | bytes 131072 | tf_op jit(solution)/shard_map/all_to_all | solution.py:285
  49.7 2.3 %shard_map.91 = f32[32,128]{1,0:T(8,128)} custom-call(f32[128,128]{1,0:T(8,128)S(1)} %bitcast.16, s32[64,128]{1,0:T(8,128)} %bitcast.25), custom_call_target="tpu_custom_call" | custom-call | tf_op jit(solution)/shard_map/pallas_call | solution.py:286
Async XLA Ops:
  1.8 8.5 %collective-permute-start = (bf16[56,256]{1,0:T(8,128)(2,1)S(1)}, bf16[56,256]{1,0:T(8,128)(2,1)S(1)}, u32[]{:S(2)}, u32[]{:S(2)}) collective-permute-start(bf16[56,256]{1,0:T(8,128)(2,1)S(1)} %get-tuple-element.15), channel_id=1, source_target_pairs={{0,1},{1,2},{2,3},{3,4},{4,5},{5,6},{6,7},{7,8},{8,9},{9,10},{10,1... | collective-permute-start | bytes 86024 | tf_op jit(solution)/shard_map/ppermute | solution.py:236
  5.8 4.6 %collective-permute-start.1 = (bf16[48,256]{1,0:T(8,128)(2,1)S(1)}, bf16[48,256]{1,0:T(8,128)(2,1)S(1)}, u32[]{:S(2)}, u32[]{:S(2)}) collective-permute-start(bf16[48,256]{1,0:T(8,128)(2,1)S(1)} %get-tuple-element.16), channel_id=1, source_target_pairs={{1,0},{2,1},{3,2},{4,3},{5,4},{6,5},{7,6},{8,7},{9,8},{10,9},{11,1... | collective-permute-start | bytes 73736 | tf_op jit(solution)/shard_map/ppermute | solution.py:236
  11.6 14.8 %collective-permute-start.2 = (f32[1,1024]{1,0:T(1,128)S(1)}, f32[1,1024]{1,0:T(1,128)S(1)}, u32[]{:S(2)}, u32[]{:S(2)}) collective-permute-start(f32[1,1024]{1,0:T(1,128)S(1)} %get-tuple-element.18), channel_id=1, source_target_pairs={{0,16},{16,32},{32,48},{48,64},{64,80},{80,96},{96,112},{1,17},{17... | collective-permute-start | bytes 12296 | tf_op jit(solution)/shard_map/ppermute | solution.py:236
  17.2 9.2 %collective-permute-start.3 = (f32[1,1024]{1,0:T(1,128)S(1)}, f32[1,1024]{1,0:T(1,128)S(1)}, u32[]{:S(2)}, u32[]{:S(2)}) collective-permute-start(f32[1,1024]{1,0:T(1,128)S(1)} %get-tuple-element.19.ids_ends), channel_id=1, source_target_pairs={{16,0},{32,16},{48,32},{64,48},{80,64},{96,80},{112,96},{17,1},{33... | collective-permute-start | bytes 12296 | tf_op jit(solution)/shard_map/ppermute | solution.py:236

commit v3 on v2

v3 whole, which is shorter than its diff:
```python
import functools

import jax
import jax.numpy as jnp
from jax import lax
from jax.experimental import pallas as pl
from jax.experimental.pallas import tpu as pltpu
from jax.sharding import PartitionSpec as P

C_IN, C_OUT, Z, YD, XD = 12, 3, 4, 16, 256
BUCKET, E_OWN, P_LOC = 64, 4096, 4096
CZ = C_IN * Z
CELLS = CZ * YD
DEPTH = CELLS + 2 * CZ + 32
WIDE = DEPTH + 2 * Z * YD
ROWS = Z * YD
LANES = 128
HIGH = P_LOC // LANES

TAP_ROWS = 9 * ROWS
PART = C_OUT * ROWS
EARLY = 7

f32, bf16, i32 = jnp.float32, jnp.bfloat16, jnp.int32


def iota(shape, dim):
    return lax.broadcasted_iota(i32, shape, dim)


def along(a, b):
    return lax.dot_general(a, b, (((1,), (1,)), ((), ())), preferred_element_type=f32)


def whole(count):
    return [pl.BlockSpec(memory_space=pltpu.VMEM)] * count


def near(shape, dtype):
    return pltpu.VMEM(shape, dtype)


def held(x):
    return pltpu.with_memory_space_constraint(x, pltpu.VMEM)


def even(axis):
    return lax.rem(lax.axis_index(axis), 2) == 0


def rows_kernel(*refs):
    sources, (one, two), held_refs, sems = refs[:6], refs[6:8], refs[8:14], refs[14]
    copies = [pltpu.make_async_copy(a, b, sems.at[i]) for i, (a, b) in enumerate(zip(sources, held_refs))]
    for copy in copies:
        copy.start()
    cells, ids = held_refs[:2]
    row = iota((2 * CZ, CELLS), 0)
    inner = jnp.where(even("yx"), YD - 1, 0)
    wanted = jnp.where(row < CZ, row * YD + inner, (row - CZ) * YD + (YD - 1 - inner))
    pick = jnp.where(iota((2 * CZ, CELLS), 1) == wanted, 1.0, 0.0).astype(bf16)
    copies[0].wait()
    picked = jnp.dot(pick, cells[...], preferred_element_type=f32).astype(bf16)
    copies[1].wait()
    last = jnp.concatenate([ids[(z + 1) * YD - 1 : (z + 1) * YD] for z in range(Z)], axis=0)
    pair = jnp.concatenate([last >> 7, last & 127], axis=0).astype(f32).astype(bf16)
    one[:CZ] = picked[:CZ]
    two[:CZ] = picked[CZ:]
    one[CZ:] = pair
    two[CZ:] = pair
    for copy in copies[2:]:
        copy.wait()


def placed(inner, outer, axis):
    first = even(axis)
    return jnp.where(first, outer, inner), jnp.where(first, inner, outer)


def pick_ends():
    row, lane = iota((8, XD), 0), iota((8, XD), 1)
    return jnp.where((row < 2) & (lane == row * (XD - 1)), 1.0, 0.0).astype(bf16)


def columns_kernel(cells, one, two, ids, after, inner, outer, own, wide):
    top, bottom = placed(one[:CZ], two[:CZ], "yx")
    wide[:CELLS] = cells[...]
    wide[CELLS : CELLS + CZ] = top
    wide[CELLS + CZ : CELLS + 2 * CZ] = bottom
    wide[CELLS + 2 * CZ : DEPTH] = jnp.zeros((DEPTH - CELLS - 2 * CZ, XD), bf16)
    wide[DEPTH : DEPTH + ROWS] = (ids[...] >> 7).astype(f32).astype(bf16)
    wide[DEPTH + ROWS :] = (ids[...] & 127).astype(f32).astype(bf16)
    picked = along(pick_ends(), wide[...])
    first = even("gz")
    inner[...] = jnp.where(first, picked[1:2], picked[0:1])
    outer[...] = jnp.where(first, picked[0:1], picked[1:2])
    own[...] = picked[0:1]


def taps_kernel(cells, weights, bias, ids, slots, taps, logits, sums, flat, value, cross):
    flat[...] = jnp.zeros(flat.shape, f32)
    for i in range(27):
        flat[8 * i : 8 * i + 3, :C_IN] = weights[i].astype(f32)
    k = iota((LANES, DEPTH), 1)
    channel = jnp.where(k < CELLS, k // (Z * YD), ((k - CELLS) % CZ) // Z)
    channel = jnp.where(k < CELLS + 2 * CZ, channel, LANES)
    spread = jnp.where(iota((LANES, DEPTH), 0) == channel, 1.0, 0.0).astype(bf16)
    lines = jnp.dot(flat[...].astype(bf16), spread, preferred_element_type=f32)
    for t in range(DEPTH // LANES):
        y, k = iota((YD, LANES), 0), iota((YD, LANES), 1) + t * LANES
        inner = k < CELLS
        z_in = jnp.where(inner, (k // YD) % Z, (k - CELLS) % Z)
        y_in = jnp.where(inner, k % YD, jnp.where(k < CELLS + CZ, -1, YD))
        y_in = jnp.where(k < CELLS + 2 * CZ, y_in, 3 * YD)
        dy = y_in - y + 1
        for e in range(3):
            for o in range(C_OUT):
                bands = []
                for a in range(3):
                    band = jnp.zeros((YD, LANES), f32)
                    for b in range(3):
                        r = (o * 9 + a * 3 + b) * 8 + e
                        band = jnp.where(dy == b, lines[r : r + 1, t * LANES : (t + 1) * LANES], band)
                    bands.append(band)
                for z in range(Z):
                    tap = jnp.zeros((YD, LANES), f32)
                    for a in range(3):
                        if 0 <= z + a - 1 < Z:
                            tap = jnp.where(z_in == z + a - 1, bands[a], tap)
                    row = ((e * C_OUT + o) * Z + z) * YD
                    taps[row : row + YD, t * LANES : (t + 1) * LANES] = tap.astype(bf16)
    product = jnp.dot(taps[:, :CELLS], cells[...], preferred_element_type=f32)
    channel = iota((PART, XD), 0) // ROWS
    bias = jnp.where(channel == 0, bias[0], jnp.where(channel == 1, bias[1], bias[2]))
    total = shifted(product) + bias
    logits[...] = total
    rows = EARLY * YD
    fill_pairs(total[:rows], crossings(ids[...], None)[:rows], value, cross)
    sums[...] = pair_sums(1, EARLY, range(1, YD - 1), slots, value, cross)


def shifted(product):
    lane = iota((PART, XD), 1)
    total = product[PART : 2 * PART]
    total += jnp.where(lane == 0, 0.0, pltpu.roll(product[:PART], 1, 1))
    return total + jnp.where(lane == XD - 1, 0.0, pltpu.roll(product[2 * PART :], XD - 1, 1))


def sigmoid(x):
    return (1.0 / (1.0 + jnp.exp(-x))).astype(bf16)


def one_hot(line, count, value=None):
    hit = iota((count, line.shape[1]), 0) == line
    return jnp.where(hit, 1.0 if value is None else value, 0.0).astype(bf16)


def pair_hot(line, count, first, second):
    return jnp.concatenate([one_hot(line, count, first), one_hot(line, count, second)], axis=0)


def crossings(here, above):
    m, n = iota((ROWS, XD), 0), iota((ROWS, XD), 1)
    under_z = jnp.concatenate([here[:YD], here[:-YD]], axis=0)
    under_y = pltpu.roll(here, 1, 0)
    if above is not None:
        above = jnp.concatenate([jnp.broadcast_to(above[z : z + 1], (YD, XD)) for z in range(Z)], axis=0)
        under_y = jnp.where(m % YD == 0, above, under_y)
    under_x = jnp.where(n == 0, here, pltpu.roll(here, 1, 1))
    unders = (under_z, under_y, under_x)
    return jnp.concatenate([jnp.where((here != under) & (under > 0), 1.0, 0.0) for under in unders], axis=0)


def fill_pairs(logits, crossed, value, cross):
    n = iota(logits.shape, 1)
    crossed = jnp.where((n > 0) & (n < XD - 1), crossed, 0.0)
    cross[...] = crossed
    value[...] = crossed * sigmoid(logits).astype(f32)


def chunk_sums(chunks):
    a_parts = [pair_hot(slot >> 7, HIGH, value, cross) for slot, value, cross in chunks]
    b_parts = [one_hot(slot & 127, LANES) for slot, _, _ in chunks]
    return along(jnp.concatenate(a_parts, axis=1), jnp.concatenate(b_parts, axis=1))


def pair_sums(first, count, rows, slots, value, cross):
    def step(i, total):
        base = pl.multiple_of(i * YD, YD)
        tiles = slots[pl.ds(base, YD)], value[pl.ds(base, YD)], cross[pl.ds(base, YD)]
        return total + chunk_sums([[tile[j : j + 1] for tile in tiles] for j in rows])

    return lax.fori_loop(first, count, step, jnp.zeros((2 * HIGH, LANES), f32))


def inner_kernel(taps, logits, early, one, two, ids, slots, full, sums, ends, halo, value, cross):
    top, bottom = placed(one[...].astype(f32), two[...].astype(f32), "yx")
    halo[:CZ] = top[:CZ].astype(bf16)
    halo[CZ : 2 * CZ] = bottom[:CZ].astype(bf16)
    halo[2 * CZ :] = jnp.zeros((LANES - 2 * CZ, XD), bf16)
    total = logits[...] + shifted(jnp.dot(taps[:, CELLS:], halo[...], preferred_element_type=f32))
    full[...] = total
    above = top[CZ:]
    above = (above[:Z] * 128.0 + above[Z:]).astype(i32)
    crossed = crossings(ids[...], above)
    fill_pairs(total, crossed, value, cross)
    pad = jnp.zeros((XD - PART, XD), f32)
    numbers = slots[...]
    kinds = [crossed, pad, (numbers >> 7).astype(f32), pad, (numbers & 127).astype(f32), pad]
    ends[...] = along(pick_ends(), jnp.concatenate(kinds, axis=0).astype(bf16))
    outer = [i * YD + y for i in range(1, EARLY) for y in (0, YD - 1)]
    sums[...] = (
        early[...]
        + chunk_sums([[ref[j : j + 1] for ref in (slots, value, cross)] for j in outer])
        + pair_sums(EARLY, C_OUT * Z, range(YD), slots, value, cross)
    )


def send_kernel(taps, logits, inner, outer, own, ends, sums, bucket, first, last, outgoing):
    left, right = placed(inner[...], outer[...], "gz")
    row = iota((8, DEPTH), 0)
    left_row = jnp.where(row == 0, left[:, :DEPTH], 0.0).astype(bf16)
    right_row = jnp.where(row == 0, right[:, :DEPTH], 0.0).astype(bf16)
    first[...] = along(taps[:PART], left_row)
    last[...] = along(taps[2 * PART :], right_row)
    lane = iota((PART, LANES), 1)
    low = logits[:, :LANES] + first[:, 0:1]
    high = logits[:, XD - LANES :] + last[:, 0:1]
    soft = sigmoid(jnp.where(lane < LANES // 2, low, high))
    row, lane = iota((8, LANES), 0), iota((8, LANES), 1)
    pick = jnp.where((row < 2) & (lane == row * (LANES - 1)), 1.0, 0.0).astype(bf16)
    soft = jnp.concatenate([along(pick, soft), jnp.zeros((8, XD - PART), f32)], axis=1)

    beside = left[:, DEPTH : DEPTH + ROWS] * 128.0 + left[:, DEPTH + ROWS :]
    here = own[:, DEPTH : DEPTH + ROWS] * 128.0 + own[:, DEPTH + ROWS :]
    differs = jnp.where((beside != here) & (beside > 0.0), 1.0, 0.0)
    differs = jnp.concatenate([jnp.zeros((1, 2 * ROWS), f32), differs, jnp.zeros((1, XD - PART), f32)], axis=1)
    chunks = []
    for end in range(2):
        crossed = ends[end : end + 1, :XD]
        if end == 0:
            crossed = crossed + differs
        slot = ends[end : end + 1, XD : 2 * XD] * 128.0 + ends[end : end + 1, 2 * XD :]
        chunks.append((slot.astype(i32), soft[end : end + 1] * crossed, crossed))
    total = sums[...] + chunk_sums(chunks)
    total = total.astype(bf16).astype(f32)

    sent = jnp.zeros((LANES, LANES), f32)
    for h0 in range(0, HIGH, 16):
        a_parts, b_parts = [], []
        for h in range(h0, h0 + 16):
            place = bucket[h : h + 1]
            a_parts.append(one_hot(place >> 6, LANES))
            b_parts.append(pair_hot(place & 63, BUCKET, total[h : h + 1], total[HIGH + h : HIGH + h + 1]))
        sent += along(jnp.concatenate(a_parts, axis=1), jnp.concatenate(b_parts, axis=1))
    outgoing[...] = sent


def affinity_kernel(logits, first, last, affinity):
    lane = iota((PART, XD), 1)
    outer = jnp.where(lane == 0, first[:, 0:1], jnp.where(lane == XD - 1, last[:, 0:1], 0.0))
    affinity[...] = sigmoid(logits[...] + outer)


def edges_kernel(arrived, rows, mean):
    n = arrived.shape[0]
    same = jnp.where(iota((n, n), 0) == iota((n, n), 1), 1.0, 0.0).astype(bf16)
    got = lax.dot_general(arrived[...].astype(bf16), same, (((0,), (0,)), ((), ())), preferred_element_type=f32)
    total = jnp.zeros((2 * HIGH, LANES), f32)
    for q0 in range(0, BUCKET, 16):
        a_parts, b_parts = [], []
        for q in range(q0, q0 + 16):
            target = rows[q : q + 1]
            a_parts.append(pair_hot(target >> 7, HIGH, got[q : q + 1], got[BUCKET + q : BUCKET + q + 1]))
            b_parts.append(one_hot(target & 127, LANES))
        total += along(jnp.concatenate(a_parts, axis=1), jnp.concatenate(b_parts, axis=1))
    mean[...] = total[:HIGH] / jnp.maximum(total[HIGH:], 1.0)


def swapped(block, axis, first):
    pairs = [(i, i + 1) for i in range(first, lax.axis_size(axis) - 1, 2)]
    return held(lax.ppermute(block, axis, pairs + [(j, i) for i, j in pairs]))


def local(features, conv_weight, conv_bias, fragments, pair_slot, slot_bucket, arrival_row):
    devices = lax.axis_size("gz") * lax.axis_size("yx")
    inputs = (
        features.reshape(CELLS, XD),
        fragments.reshape(ROWS, XD),
        pair_slot.reshape(PART, XD),
        conv_weight.transpose(0, 2, 3, 4, 1).reshape(27, 3, C_IN),
        slot_bucket.reshape(HIGH, LANES),
        arrival_row[0].T,
    )
    scalar = pl.BlockSpec(memory_space=pltpu.SMEM)
    pairs = [pltpu.VMEM((PART, XD), f32)] * 2
    sums_shape = near((2 * HIGH, LANES), f32)
    lines = near((CZ + 2 * Z, XD), bf16)
    one, two, *inputs = pl.pallas_call(
        rows_kernel,
        out_shape=(lines, lines, *(near(x.shape, x.dtype) for x in inputs)),
        in_specs=[pl.BlockSpec(memory_space=pl.ANY)] * 6,
        out_specs=tuple(whole(8)),
        scratch_shapes=[pltpu.SemaphoreType.DMA((6,))],
    )(*inputs)
    cells, ids, slots, weights, bucket, targets = map(held, inputs)
    two = swapped(two, "yx", 1)
    one = swapped(one, "yx", 0)
    taps, logits, early = pl.pallas_call(
        taps_kernel,
        out_shape=(near((TAP_ROWS, DEPTH), bf16), near((PART, XD), f32), sums_shape),
        in_specs=whole(2) + [scalar] + whole(2),
        out_specs=tuple(whole(3)),
        scratch_shapes=[pltpu.VMEM((27 * 8, LANES), f32)] + [pltpu.VMEM((EARLY * YD, XD), f32)] * 2,
    )(cells, weights, conv_bias, ids, slots)
    taps, logits, early = held(taps), held(logits), held(early)
    inner, outer, own = pl.pallas_call(
        columns_kernel,
        out_shape=(near((1, WIDE), f32),) * 3,
        in_specs=whole(5),
        out_specs=tuple(whole(3)),
        scratch_shapes=[pltpu.VMEM((WIDE, XD), bf16)],
    )(cells, one, two, ids, early)
    outer = swapped(outer, "gz", 1)
    inner = swapped(inner, "gz", 0)
    logits, sums, ends = pl.pallas_call(
        inner_kernel,
        out_shape=(near((PART, XD), f32), sums_shape, near((8, 3 * XD), f32)),
        in_specs=whole(7),
        out_specs=tuple(whole(3)),
        scratch_shapes=[pltpu.VMEM((LANES, XD), bf16)] + pairs,
    )(taps, logits, early, one, two, ids, slots)
    logits = held(logits)
    first, last, outgoing = pl.pallas_call(
        send_kernel,
        out_shape=(near((PART, 8), f32), near((PART, 8), f32), near((devices, 2 * BUCKET), f32)),
        in_specs=whole(8),
        out_specs=tuple(whole(3)),
    )(taps, logits, inner, outer, held(own), held(ends), held(sums), bucket)
    arrived = lax.all_to_all(outgoing, ("gz", "yx"), split_axis=0, concat_axis=0, tiled=True)
    affinity = pl.pallas_call(
        affinity_kernel,
        out_shape=jax.ShapeDtypeStruct((PART, XD), bf16),
        in_specs=whole(3),
        out_specs=whole(1)[0],
    )(logits, held(first), held(last))
    mean = pl.pallas_call(
        edges_kernel,
        out_shape=jax.ShapeDtypeStruct((HIGH, LANES), f32),
        in_specs=whole(2),
        out_specs=whole(1)[0],
    )(held(arrived), targets)
    return affinity.reshape(C_OUT, Z, YD, XD), mean.reshape(E_OWN)


def solution(mesh):
    return jax.shard_map(
        local,
        mesh=mesh,
        in_specs=(
            P(None, None, "yx", "gz"),
            P(),
            P(),
            P(None, "yx", "gz"),
            P(None, None, "yx", "gz"),
            P(("gz", "yx"), None),
            P(("gz", "yx"), None, None),
        ),
        out_specs=(P(None, None, "yx", "gz"), P(("gz", "yx"))),
        check_vma=False,
    )
```

time: 52.5 us -> 42.6 us (0.81)
  blocking collectives: 21.2 us -> 0 us
  waiting for transfers between devices: 1.14 us -> 8.83 us
  starting transfers between devices: 12.7 us -> 19.1 us
  Pallas kernels: 16.4 us -> 13.8 us
    all_to_all x1 -> x0, blocking collectives: 21.2 us -> none  [local(): lax.all_to_all(outgoing, ('gz', 'yx'), split_axis=0, concat_axis=0, tiled...]
    all_to_all x0 -> x1, starting transfers between devices: none -> 11.8 us  [local(): lax.all_to_all(outgoing, ('gz', 'yx'), split_axis=0, concat_axis=0, tiled...]
    all_to_all x0 -> x1, waiting for transfers between devices: none -> 8.82 us  [local(): lax.all_to_all(outgoing, ('gz', 'yx'), split_axis=0, concat_axis=0, tiled...]
    ppermute x4, starting transfers between devices: 12.7 us -> 7.24 us  [swapped(): return held(lax.ppermute(block, axis, pairs + [(j, i) for i, j in pairs]))]
    pallas_call x4 -> x5, Pallas kernels: 11.9 us -> 7.67 us  [the longest x1 3.23 us: local(): pl.pallas_call(inner_kernel, out_shape=(near((PART, XD), f32), sums_shape...]
    pallas_call x1, Pallas kernels: 2.13 us -> 4.54 us  [local(): pl.pallas_call(taps_kernel, out_shape=(near((TAP_ROWS, DEPTH), bf16), nea...]
    ppermute x4, waiting for transfers between devices: 1.14 us -> 0.01 us  [swapped(): return held(lax.ppermute(block, axis, pairs + [(j, i) for i, j in pairs]))]
    pallas_call x1, Pallas kernels: 2.35 us -> 1.6 us  [local(): pl.pallas_call(edges_kernel, out_shape=jax.ShapeDtypeStruct((HIGH, LANES)...]
  transfers between devices with their start and end apart: 4 -> 5, of which waited for: 1 -> 1; matrix products, arithmetic and copies ran while one was open for 0% -> 0% of each run, Pallas kernels for 18% -> 20%
where the time goes in v3:
time: 42.6 us; the launch traced here: 42.4 us
  starting transfers between devices  19.1 us (45%)
  Pallas kernels  13.8 us (32%)
  waiting for transfers between devices  8.83 us (21%)
  between operations  0.71 us (2%)
    all_to_all x1, starting transfers between devices, local(): lax.all_to_all(outgoing, ('gz', 'yx'), split_axis=0, concat_axis=0, tiled...  11.8 us
    all_to_all x1, waiting for transfers between devices, local(): lax.all_to_all(outgoing, ('gz', 'yx'), split_axis=0, concat_axis=0, tiled...  8.82 us
    ppermute x4, starting transfers between devices, swapped(): return held(lax.ppermute(block, axis, pairs + [(j, i) for i, j in pairs]))  7.24 us
    pallas_call x1, Pallas kernels, local(): pl.pallas_call(taps_kernel, out_shape=(near((TAP_ROWS, DEPTH), bf16), nea...  4.54 us
    pallas_call x1, Pallas kernels, local(): pl.pallas_call(inner_kernel, out_shape=(near((PART, XD), f32), sums_shape...  3.23 us
    pallas_call x1, Pallas kernels, local(): pl.pallas_call(send_kernel, out_shape=(near((PART, 8), f32), near((PART,...  2.13 us
    pallas_call x1, Pallas kernels, local(): pl.pallas_call(edges_kernel, out_shape=jax.ShapeDtypeStruct((HIGH, LANES)...  1.6 us
    pallas_call x1, Pallas kernels, local(): pl.pallas_call(rows_kernel, out_shape=(lines, lines, *(near(x.shape, x.dt...  1.27 us
  transfers between devices with their start and end apart: 5, of which 1 were waited for; matrix products, arithmetic and copies ran while one was open for 0% of the time, Pallas kernels for 20%

profile of v3, /device:TPU:1, one launch (start us, length us, event | category | flops | bytes accessed | tf_op | source)
XLA Modules:
  0.0 42.4 jit_solution(4473446282870969955)
XLA Ops:
  0.6 1.3 %shard_map.86 = (bf16[56,256]{1,0:T(8,128)(2,1)S(1)}, bf16[56,256]{1,0:T(8,128)(2,1)S(1)}, bf16[768,256]{1,0:T(8,128)(2,1)S(1)}, s32[64,256]{1,0:T(8,128)S(1)}, ...) custom-call(bf16[768,256]{1,0:T(8,128)(2,1)} %bitcast.17, ...), custom_call_target="tpu_custom_call" | custom-call | tf_op jit(solution)/shard_map/pallas_call | solution.py:298
  1.9 2.1 %collective-permute-start = (bf16[56,256]{1,0:T(8,128)(2,1)S(1)}, bf16[56,256]{1,0:T(8,128)(2,1)S(1)}, u32[]{:S(2)}, u32[]{:S(2)}) collective-permute-start(bf16[56,256]{1,0:T(8,128)(2,1)S(1)} %get-tuple-element.29), channel_id=1, source_target_pairs={{0,1},{2,3},{4,5},{6,7},{8,9},{10,11},{12,13},{14,15},{1,0},{3,2},... | collective-permute-start | bytes 86024 | tf_op jit(solution)/shard_map/ppermute | solution.py:281
  4.0 0.7 %collective-permute-start.1 = (bf16[56,256]{1,0:T(8,128)(2,1)S(1)}, bf16[56,256]{1,0:T(8,128)(2,1)S(1)}, u32[]{:S(2)}, u32[]{:S(2)}) collective-permute-start(bf16[56,256]{1,0:T(8,128)(2,1)S(1)} %get-tuple-element.30), channel_id=1, source_target_pairs={{1,2},{3,4},{5,6},{7,8},{9,10},{11,12},{13,14},{2,1},{4,3},{6,5},{... | collective-permute-start | bytes 86024 | tf_op jit(solution)/shard_map/ppermute | solution.py:281
  4.7 4.5 %shard_map.87 = (bf16[576,896]{1,0:T(8,128)(2,1)S(1)}, f32[192,256]{1,0:T(8,128)S(1)}, f32[64,128]{1,0:T(8,128)S(1)}) custom-call(bf16[768,256]{1,0:T(8,128)(2,1)S(1)} %get-tuple-element.22.cells, bf16[27,3,12]{2,1,0:T(4,128)(2,1)S(1)} %get-tuple-element.23.weights, f32[3]{0:T(128)} %bias.1, s32[64,256]{1,0:T(8,128)S(1)} %get-tuple-element.24.ids, ...), custom_call_target="tpu_custom_call" | custom-call | tf_op jit(solution)/shard_map/pallas_call | solution.py:308
  9.2 0.0 collective-permute-done.one
  9.2 0.0 collective-permute-done.1.two
  9.2 0.3 shard_map.89
  9.5 1.0 %collective-permute-start.2 = (f32[1,1024]{1,0:T(1,128)S(1)}, f32[1,1024]{1,0:T(1,128)S(1)}, u32[]{:S(2)}, u32[]{:S(2)}) collective-permute-start(f32[1,1024]{1,0:T(1,128)S(1)} %get-tuple-element.32), channel_id=1, source_target_pairs={{0,16},{32,48},{64,80},{96,112},{16,0},{48,32},{80,64},{112,96},{1... | collective-permute-start | bytes 12296 | tf_op jit(solution)/shard_map/ppermute | solution.py:281
  10.5 3.4 %collective-permute-start.3 = (f32[1,1024]{1,0:T(1,128)S(1)}, f32[1,1024]{1,0:T(1,128)S(1)}, u32[]{:S(2)}, u32[]{:S(2)}) collective-permute-start(f32[1,1024]{1,0:T(1,128)S(1)} %get-tuple-element.33), channel_id=1, source_target_pairs={{16,32},{48,64},{80,96},{32,16},{64,48},{96,80},{17,33},{49,65},{8... | collective-permute-start | bytes 12296 | tf_op jit(solution)/shard_map/ppermute | solution.py:281
  14.0 3.2 %shard_map.88 = (f32[192,256]{1,0:T(8,128)S(1)}, f32[64,128]{1,0:T(8,128)S(1)}, f32[8,768]{1,0:T(8,128)S(1)}) custom-call(bf16[576,896]{1,0:T(8,128)(2,1)S(1)} %get-tuple-element.26.taps, f32[192,256]{1,0:T(8,128)S(1)} %get-tuple-element.27.logits, f32[64,128]{1,0:T(8,128)S(1)} %get-tuple-element.28.early.after, ...), custom_call_target="tpu_custom_call" | custom-call | tf_op jit(solution)/shard_map/pallas_call | solution.py:325
  17.2 0.0 collective-permute-done.2.inner
  17.2 0.0 collective-permute-done.3.outer
  17.3 2.1 %shard_map.90 = (f32[192,8]{1,0:T(8,128)S(1)}, f32[192,8]{1,0:T(8,128)S(1)}, f32[128,128]{1,0:T(8,128)}) custom-call(bf16[576,896]{1,0:T(8,128)(2,1)S(1)} %get-tuple-element.26.taps, f32[192,256]{1,0:T(8,128)S(1)} %get-tuple-element.31.logits, f32[1,1024]{1,0:T(1,128)S(1)} %collective-permute-done.2.inner, f32[1,1024]{1,0:T(1,128)S(1)} %collective-permute-done.3.outer, ...), custom_call_target="tpu_custom_call" | custom-call | tf_op jit(solution)/shard_map/pallas_call | solution.py:333
  19.4 11.8 %all-to-all-start = ((f32[128,1,128]{2,1,0:T(1,128)}), f32[128,1,128]{2,1,0:T(1,128)S(1)}, u32[]{:S(2)}, u32[]{:S(2)}) async-start(f32[128,1,128]{2,1,0:T(1,128)} %bitcast.10), calls=%async_computation | async-start | bytes 131072 | tf_op jit(solution)/shard_map/all_to_all | solution.py:339
  31.2 0.8 %shard_map.91 = bf16[192,256]{1,0:T(8,128)(2,1)} custom-call(f32[192,256]{1,0:T(8,128)S(1)} %get-tuple-element.31.logits, f32[192,8]{1,0:T(8,128)S(1)} %get-tuple-element.38.first, f32[192,8]{1,0:T(8,128)S(1)} %get-tuple-element.39.last), custom_call_target="tpu_custom_call" | custom-call | tf_op jit(solution)/shard_map/pallas_call | solution.py:340
  32.0 8.8 %all-to-all-done = f32[128,1,128]{2,1,0:T(1,128)S(1)} async-done(((f32[128,1,128]{2,1,0:T(1,128)}), f32[128,1,128]{2,1,0:T(1,128)S(1)}, u32[]{:S(2)}, u32[]{:S(2)}) %all-to-all-start) | async-done | bytes 65568 | tf_op jit(solution)/shard_map/all_to_all | solution.py:339
  40.8 1.6 %shard_map.92 = f32[32,128]{1,0:T(8,128)} custom-call(f32[128,128]{1,0:T(8,128)S(1)} %bitcast.16, s32[64,128]{1,0:T(8,128)S(1)} %get-tuple-element.41.rows), custom_call_target="tpu_custom_call" | custom-call | tf_op jit(solution)/shard_map/pallas_call | solution.py:346
Async XLA Ops:
  1.9 7.3 %collective-permute-start = (bf16[56,256]{1,0:T(8,128)(2,1)S(1)}, bf16[56,256]{1,0:T(8,128)(2,1)S(1)}, u32[]{:S(2)}, u32[]{:S(2)}) collective-permute-start(bf16[56,256]{1,0:T(8,128)(2,1)S(1)} %get-tuple-element.29), channel_id=1, source_target_pairs={{0,1},{2,3},{4,5},{6,7},{8,9},{10,11},{12,13},{14,15},{1,0},{3,2},... | collective-permute-start | bytes 86024 | tf_op jit(solution)/shard_map/ppermute | solution.py:281
  4.0 5.2 %collective-permute-start.1 = (bf16[56,256]{1,0:T(8,128)(2,1)S(1)}, bf16[56,256]{1,0:T(8,128)(2,1)S(1)}, u32[]{:S(2)}, u32[]{:S(2)}) collective-permute-start(bf16[56,256]{1,0:T(8,128)(2,1)S(1)} %get-tuple-element.30), channel_id=1, source_target_pairs={{1,2},{3,4},{5,6},{7,8},{9,10},{11,12},{13,14},{2,1},{4,3},{6,5},{... | collective-permute-start | bytes 86024 | tf_op jit(solution)/shard_map/ppermute | solution.py:281
  9.5 7.7 %collective-permute-start.2 = (f32[1,1024]{1,0:T(1,128)S(1)}, f32[1,1024]{1,0:T(1,128)S(1)}, u32[]{:S(2)}, u32[]{:S(2)}) collective-permute-start(f32[1,1024]{1,0:T(1,128)S(1)} %get-tuple-element.32), channel_id=1, source_target_pairs={{0,16},{32,48},{64,80},{96,112},{16,0},{48,32},{80,64},{112,96},{1... | collective-permute-start | bytes 12296 | tf_op jit(solution)/shard_map/ppermute | solution.py:281
  10.5 6.7 %collective-permute-start.3 = (f32[1,1024]{1,0:T(1,128)S(1)}, f32[1,1024]{1,0:T(1,128)S(1)}, u32[]{:S(2)}, u32[]{:S(2)}) collective-permute-start(f32[1,1024]{1,0:T(1,128)S(1)} %get-tuple-element.33), channel_id=1, source_target_pairs={{16,32},{48,64},{80,96},{32,16},{64,48},{96,80},{17,33},{49,65},{8... | collective-permute-start | bytes 12296 | tf_op jit(solution)/shard_map/ppermute | solution.py:281
  19.4 21.4 %all-to-all-start = ((f32[128,1,128]{2,1,0:T(1,128)}), f32[128,1,128]{2,1,0:T(1,128)S(1)}, u32[]{:S(2)}, u32[]{:S(2)}) async-start(f32[128,1,128]{2,1,0:T(1,128)} %bitcast.10), calls=%async_computation | async-start | bytes 131072 | tf_op jit(solution)/shard_map/all_to_all | solution.py:339

commit v4 on v3

--- a/solution.py
+++ b/solution.py
@@ -20,6 +20,8 @@
 TAP_ROWS = 9 * ROWS
 PART = C_OUT * ROWS
 EARLY = 7
+BATCH = 48
+LOW, HALF, STEP = 96, 48, 12
 
 f32, bf16, i32 = jnp.float32, jnp.bfloat16, jnp.int32
 
@@ -49,7 +51,8 @@
 
 
 def rows_kernel(*refs):
-    sources, (one, two), held_refs, sems = refs[:6], refs[6:8], refs[8:14], refs[14]
+    count = len(refs) // 2 - 1
+    sources, (one, two), held_refs, sems = refs[:count], refs[count : count + 2], refs[count + 2 : -1], refs[-1]
     copies = [pltpu.make_async_copy(a, b, sems.at[i]) for i, (a, b) in enumerate(zip(sources, held_refs))]
     for copy in copies:
         copy.start()
@@ -81,7 +84,7 @@
     return jnp.where((row < 2) & (lane == row * (XD - 1)), 1.0, 0.0).astype(bf16)
 
 
-def columns_kernel(cells, one, two, ids, after, inner, outer, own, wide):
+def columns_kernel(two, one, cells, ids, after, inner, outer, own, wide):
     top, bottom = placed(one[:CZ], two[:CZ], "yx")
     wide[:CELLS] = cells[...]
     wide[CELLS : CELLS + CZ] = top
@@ -104,38 +107,37 @@
     channel = jnp.where(k < CELLS, k // (Z * YD), ((k - CELLS) % CZ) // Z)
     channel = jnp.where(k < CELLS + 2 * CZ, channel, LANES)
     spread = jnp.where(iota((LANES, DEPTH), 0) == channel, 1.0, 0.0).astype(bf16)
-    lines = jnp.dot(flat[...].astype(bf16), spread, preferred_element_type=f32)
+    lines = jnp.dot(flat[...].astype(bf16), spread, preferred_element_type=f32).astype(bf16)
     for t in range(DEPTH // LANES):
         y, k = iota((YD, LANES), 0), iota((YD, LANES), 1) + t * LANES
         inner = k < CELLS
-        z_in = jnp.where(inner, (k // YD) % Z, (k - CELLS) % Z)
+        z_in = small(jnp.where(inner, (k // YD) % Z, (k - CELLS) % Z))
         y_in = jnp.where(inner, k % YD, jnp.where(k < CELLS + CZ, -1, YD))
         y_in = jnp.where(k < CELLS + 2 * CZ, y_in, 3 * YD)
-        dy = y_in - y + 1
+        dy = small(y_in - y + 1)
         for e in range(3):
             for o in range(C_OUT):
                 bands = []
                 for a in range(3):
-                    band = jnp.zeros((YD, LANES), f32)
+                    band = jnp.zeros((YD, LANES), bf16)
                     for b in range(3):
                         r = (o * 9 + a * 3 + b) * 8 + e
-                        band = jnp.where(dy == b, lines[r : r + 1, t * LANES : (t + 1) * LANES], band)
+                        band = jnp.where(dy == float(b), lines[r : r + 1, t * LANES : (t + 1) * LANES], band)
                     bands.append(band)
                 for z in range(Z):
-                    tap = jnp.zeros((YD, LANES), f32)
+                    tap = jnp.zeros((YD, LANES), bf16)
                     for a in range(3):
                         if 0 <= z + a - 1 < Z:
-                            tap = jnp.where(z_in == z + a - 1, bands[a], tap)
+                            tap = jnp.where(z_in == float(z + a - 1), bands[a], tap)
                     row = ((e * C_OUT + o) * Z + z) * YD
-                    taps[row : row + YD, t * LANES : (t + 1) * LANES] = tap.astype(bf16)
+                    taps[row : row + YD, t * LANES : (t + 1) * LANES] = tap
     product = jnp.dot(taps[:, :CELLS], cells[...], preferred_element_type=f32)
-    channel = iota((PART, XD), 0) // ROWS
-    bias = jnp.where(channel == 0, bias[0], jnp.where(channel == 1, bias[1], bias[2]))
-    total = shifted(product) + bias
+    offset = jnp.concatenate([jnp.broadcast_to(bias[:, o : o + 1], (ROWS, 1)) for o in range(C_OUT)], axis=0)
+    total = shifted(product) + offset
     logits[...] = total
     rows = EARLY * YD
     fill_pairs(total[:rows], crossings(ids[...], None)[:rows], value, cross)
-    sums[...] = pair_sums(1, EARLY, range(1, YD - 1), slots, value, cross)
+    sums[...] = batched([line for i in range(1, EARLY) for line in lines_of(i, range(1, YD - 1), slots, value, cross)])
 
 
 def shifted(product):
@@ -150,12 +152,36 @@
 
 
 def one_hot(line, count, value=None):
-    hit = iota((count, line.shape[1]), 0) == line
-    return jnp.where(hit, 1.0 if value is None else value, 0.0).astype(bf16)
+    rows = iota((count, line.shape[1]), 0).astype(f32).astype(bf16)
+    return jnp.where(rows == line, jnp.ones((), bf16) if value is None else value, jnp.zeros((), bf16))
 
 
 def pair_hot(line, count, first, second):
     return jnp.concatenate([one_hot(line, count, first), one_hot(line, count, second)], axis=0)
+
+
+def small(x):
+    return x.astype(f32).astype(bf16)
+
+
+def split(number):
+    q = ((number >> 5) * 171) >> 9
+    return small((q & 3) * STEP + (q >> 2)), small(number - q * LOW)
+
+
+def chunk_sums(chunks):
+    a_parts = [pair_hot(row, HALF, value, cross) for row, _, value, cross in chunks]
+    b_parts = [one_hot(column, LOW) for _, column, _, _ in chunks]
+    return along(jnp.concatenate(a_parts, axis=1), jnp.concatenate(b_parts, axis=1))
+
+
+def relaid(total):
+    a, b, c, d = (total[j * STEP : (j + 1) * STEP] for j in range(4))
+    return (
+        jnp.concatenate([a, b[:, :32]], axis=1),
+        jnp.concatenate([b[:, 32:], c[:, :64]], axis=1),
+        jnp.concatenate([c[:, 64:], d], axis=1),
+    )
 
 
 def crossings(here, above):
@@ -177,22 +203,17 @@
     value[...] = crossed * sigmoid(logits).astype(f32)
 
 
-def chunk_sums(chunks):
-    a_parts = [pair_hot(slot >> 7, HIGH, value, cross) for slot, value, cross in chunks]
-    b_parts = [one_hot(slot & 127, LANES) for slot, _, _ in chunks]
-    return along(jnp.concatenate(a_parts, axis=1), jnp.concatenate(b_parts, axis=1))
-
-
-def pair_sums(first, count, rows, slots, value, cross):
-    def step(i, total):
-        base = pl.multiple_of(i * YD, YD)
-        tiles = slots[pl.ds(base, YD)], value[pl.ds(base, YD)], cross[pl.ds(base, YD)]
-        return total + chunk_sums([[tile[j : j + 1] for tile in tiles] for j in rows])
-
-    return lax.fori_loop(first, count, step, jnp.zeros((2 * HIGH, LANES), f32))
-
-
-def inner_kernel(taps, logits, early, one, two, ids, slots, full, sums, ends, halo, value, cross):
+def lines_of(i, rows, slots, value, cross):
+    at = slice(i * YD, (i + 1) * YD)
+    tiles = (*split(slots[at]), value[at].astype(bf16), cross[at].astype(bf16))
+    return [[tile[j : j + 1] for tile in tiles] for j in rows]
+
+
+def batched(chunks, size=BATCH):
+    return sum(chunk_sums(chunks[i : i + size]) for i in range(0, len(chunks), size))
+
+
+def inner_kernel(two, one, taps, logits, early, ids, slots, full, sums, ends, halo, value, cross):
     top, bottom = placed(one[...].astype(f32), two[...].astype(f32), "yx")
     halo[:CZ] = top[:CZ].astype(bf16)
     halo[CZ : 2 * CZ] = bottom[:CZ].astype(bf16)
@@ -207,15 +228,12 @@
     numbers = slots[...]
     kinds = [crossed, pad, (numbers >> 7).astype(f32), pad, (numbers & 127).astype(f32), pad]
     ends[...] = along(pick_ends(), jnp.concatenate(kinds, axis=0).astype(bf16))
-    outer = [i * YD + y for i in range(1, EARLY) for y in (0, YD - 1)]
-    sums[...] = (
-        early[...]
-        + chunk_sums([[ref[j : j + 1] for ref in (slots, value, cross)] for j in outer])
-        + pair_sums(EARLY, C_OUT * Z, range(YD), slots, value, cross)
-    )
-
-
-def send_kernel(taps, logits, inner, outer, own, ends, sums, bucket, first, last, outgoing):
+    chunks = [line for i in range(1, EARLY) for line in lines_of(i, (0, YD - 1), slots, value, cross)]
+    chunks += [line for i in range(EARLY, C_OUT * Z) for line in lines_of(i, range(YD), slots, value, cross)]
+    sums[...] = early[...] + batched(chunks)
+
+
+def send_kernel(outer, inner, taps, logits, own, ends, sums, bucket, first, last, outgoing):
     left, right = placed(inner[...], outer[...], "gz")
     row = iota((8, DEPTH), 0)
     left_row = jnp.where(row == 0, left[:, :DEPTH], 0.0).astype(bf16)
@@ -240,18 +258,16 @@
         if end == 0:
             crossed = crossed + differs
         slot = ends[end : end + 1, XD : 2 * XD] * 128.0 + ends[end : end + 1, 2 * XD :]
-        chunks.append((slot.astype(i32), soft[end : end + 1] * crossed, crossed))
+        chunks.append((*split(slot.astype(i32)), (soft[end : end + 1] * crossed).astype(bf16), crossed.astype(bf16)))
     total = sums[...] + chunk_sums(chunks)
-    total = total.astype(bf16).astype(f32)
-
-    sent = jnp.zeros((LANES, LANES), f32)
-    for h0 in range(0, HIGH, 16):
-        a_parts, b_parts = [], []
-        for h in range(h0, h0 + 16):
-            place = bucket[h : h + 1]
-            a_parts.append(one_hot(place >> 6, LANES))
-            b_parts.append(pair_hot(place & 63, BUCKET, total[h : h + 1], total[HIGH + h : HIGH + h + 1]))
-        sent += along(jnp.concatenate(a_parts, axis=1), jnp.concatenate(b_parts, axis=1))
+    kinds = [relaid(total[:HALF].astype(bf16)), relaid(total[HALF:].astype(bf16))]
+    owners, places = small(bucket[...] >> 6), small(bucket[...] & 63)
+    a_parts, b_parts = [], []
+    for h in range(HIGH):
+        k, j = divmod(h, 3)
+        a_parts.append(one_hot(owners[h : h + 1], LANES))
+        b_parts.append(pair_hot(places[h : h + 1], BUCKET, kinds[0][j][k : k + 1], kinds[1][j][k : k + 1]))
+    sent = along(jnp.concatenate(a_parts, axis=1), jnp.concatenate(b_parts, axis=1))
     outgoing[...] = sent
 
 
@@ -265,15 +281,18 @@
     n = arrived.shape[0]
     same = jnp.where(iota((n, n), 0) == iota((n, n), 1), 1.0, 0.0).astype(bf16)
     got = lax.dot_general(arrived[...].astype(bf16), same, (((0,), (0,)), ((), ())), preferred_element_type=f32)
-    total = jnp.zeros((2 * HIGH, LANES), f32)
-    for q0 in range(0, BUCKET, 16):
-        a_parts, b_parts = [], []
-        for q in range(q0, q0 + 16):
-            target = rows[q : q + 1]
-            a_parts.append(pair_hot(target >> 7, HIGH, got[q : q + 1], got[BUCKET + q : BUCKET + q + 1]))
-            b_parts.append(one_hot(target & 127, LANES))
-        total += along(jnp.concatenate(a_parts, axis=1), jnp.concatenate(b_parts, axis=1))
-    mean[...] = total[:HIGH] / jnp.maximum(total[HIGH:], 1.0)
+    got = got.astype(bf16)
+    row, column = split(rows[...])
+    total = chunk_sums(
+        [
+            (row[q : q + 1], column[q : q + 1], got[q : q + 1], got[BUCKET + q : BUCKET + q + 1])
+            for q in range(BUCKET)
+        ]
+    )
+    parts = relaid(total[:HALF] / jnp.maximum(total[HALF:], 1.0))
+    for h in range(HIGH):
+        k, j = divmod(h, 3)
+        mean[h : h + 1] = parts[j][k : k + 1]
 
 
 def swapped(block, axis, first):
@@ -290,28 +309,28 @@
         conv_weight.transpose(0, 2, 3, 4, 1).reshape(27, 3, C_IN),
         slot_bucket.reshape(HIGH, LANES),
         arrival_row[0].T,
+        conv_bias.reshape(1, C_OUT),
     )
-    scalar = pl.BlockSpec(memory_space=pltpu.SMEM)
     pairs = [pltpu.VMEM((PART, XD), f32)] * 2
-    sums_shape = near((2 * HIGH, LANES), f32)
+    sums_shape = near((2 * HALF, LOW), f32)
     lines = near((CZ + 2 * Z, XD), bf16)
     one, two, *inputs = pl.pallas_call(
         rows_kernel,
         out_shape=(lines, lines, *(near(x.shape, x.dtype) for x in inputs)),
-        in_specs=[pl.BlockSpec(memory_space=pl.ANY)] * 6,
-        out_specs=tuple(whole(8)),
-        scratch_shapes=[pltpu.SemaphoreType.DMA((6,))],
+        in_specs=[pl.BlockSpec(memory_space=pl.ANY)] * len(inputs),
+        out_specs=tuple(whole(2 + len(inputs))),
+        scratch_shapes=[pltpu.SemaphoreType.DMA((len(inputs),))],
     )(*inputs)
-    cells, ids, slots, weights, bucket, targets = map(held, inputs)
+    cells, ids, slots, weights, bucket, targets, bias = map(held, inputs)
     two = swapped(two, "yx", 1)
     one = swapped(one, "yx", 0)
     taps, logits, early = pl.pallas_call(
         taps_kernel,
         out_shape=(near((TAP_ROWS, DEPTH), bf16), near((PART, XD), f32), sums_shape),
-        in_specs=whole(2) + [scalar] + whole(2),
+        in_specs=whole(5),
         out_specs=tuple(whole(3)),
         scratch_shapes=[pltpu.VMEM((27 * 8, LANES), f32)] + [pltpu.VMEM((EARLY * YD, XD), f32)] * 2,
-    )(cells, weights, conv_bias, ids, slots)
+    )(cells, weights, bias, ids, slots)
     taps, logits, early = held(taps), held(logits), held(early)
     inner, outer, own = pl.pallas_call(
         columns_kernel,
@@ -319,7 +338,7 @@
         in_specs=whole(5),
         out_specs=tuple(whole(3)),
         scratch_shapes=[pltpu.VMEM((WIDE, XD), bf16)],
-    )(cells, one, two, ids, early)
+    )(two, one, cells, ids, early)
     outer = swapped(outer, "gz", 1)
     inner = swapped(inner, "gz", 0)
     logits, sums, ends = pl.pallas_call(
@@ -328,15 +347,15 @@
         in_specs=whole(7),
         out_specs=tuple(whole(3)),
         scratch_shapes=[pltpu.VMEM((LANES, XD), bf16)] + pairs,
-    )(taps, logits, early, one, two, ids, slots)
+    )(two, one, taps, logits, early, ids, slots)
     logits = held(logits)
     first, last, outgoing = pl.pallas_call(
         send_kernel,
         out_shape=(near((PART, 8), f32), near((PART, 8), f32), near((devices, 2 * BUCKET), f32)),
         in_specs=whole(8),
         out_specs=tuple(whole(3)),
-    )(taps, logits, inner, outer, held(own), held(ends), held(sums), bucket)
-    arrived = lax.all_to_all(outgoing, ("gz", "yx"), split_axis=0, concat_axis=0, tiled=True)
+    )(outer, inner, taps, logits, held(own), held(ends), held(sums), bucket)
+    arrived = lax.all_to_all(held(outgoing), ("gz", "yx"), split_axis=0, concat_axis=0, tiled=True)
     affinity = pl.pallas_call(
         affinity_kernel,
         out_shape=jax.ShapeDtypeStruct((PART, XD), bf16),

time: 42.6 us -> 40 us (0.939)
  Pallas kernels: 13.8 us -> 10.2 us
  starting transfers between devices: 19.1 us -> 20.1 us
    ppermute x4, starting transfers between devices: 7.24 us -> 9.98 us  [swapped(): return held(lax.ppermute(block, axis, pairs + [(j, i) for i, j in pairs]))]
    pallas_call x1, Pallas kernels: 4.54 us -> 2.55 us  [local(): pl.pallas_call(taps_kernel, out_shape=(near((TAP_ROWS, DEPTH), bf16), nea...]
    all_to_all x1, starting transfers between devices: 11.8 us -> 10.1 us  [local(): lax.all_to_all(held(outgoing), ('gz', 'yx'), split_axis=0, concat_axis=0,...]
    pallas_call x1, Pallas kernels: 3.23 us -> 1.71 us  [local(): pl.pallas_call(inner_kernel, out_shape=(near((PART, XD), f32), sums_shape...]
  transfers between devices with their start and end apart: 5 -> 5, of which waited for: 1 -> 1; matrix products, arithmetic and copies ran while one was open for 0% -> 0% of each run, Pallas kernels for 20% -> 13%
where the time goes in v4:
time: 40 us; the launch traced here: 39.8 us
  starting transfers between devices  20.1 us (50%)
  Pallas kernels  10.2 us (25%)
  waiting for transfers between devices  8.83 us (22%)
  between operations  0.73 us (2%)
    all_to_all x1, starting transfers between devices, local(): lax.all_to_all(held(outgoing), ('gz', 'yx'), split_axis=0, concat_axis=0,...  10.1 us
    ppermute x4, starting transfers between devices, swapped(): return held(lax.ppermute(block, axis, pairs + [(j, i) for i, j in pairs]))  9.98 us
    all_to_all x1, waiting for transfers between devices, local(): lax.all_to_all(held(outgoing), ('gz', 'yx'), split_axis=0, concat_axis=0,...  8.82 us
    pallas_call x1, Pallas kernels, local(): pl.pallas_call(taps_kernel, out_shape=(near((TAP_ROWS, DEPTH), bf16), nea...  2.55 us
    pallas_call x1, Pallas kernels, local(): pl.pallas_call(send_kernel, out_shape=(near((PART, 8), f32), near((PART,...  2.21 us
    pallas_call x1, Pallas kernels, local(): pl.pallas_call(inner_kernel, out_shape=(near((PART, XD), f32), sums_shape...  1.71 us
    pallas_call x1, Pallas kernels, local(): pl.pallas_call(edges_kernel, out_shape=jax.ShapeDtypeStruct((HIGH, LANES)...  1.42 us
    pallas_call x1, Pallas kernels, local(): pl.pallas_call(rows_kernel, out_shape=(lines, lines, *(near(x.shape, x.dt...  1.29 us
  transfers between devices with their start and end apart: 5, of which 1 were waited for; matrix products, arithmetic and copies ran while one was open for 0% of the time, Pallas kernels for 13%

profile of v4, /device:TPU:1, one launch (start us, length us, event | category | flops | bytes accessed | tf_op | source)
XLA Modules:
  0.0 39.8 jit_solution(18233149313411195884)
XLA Ops:
  0.6 1.3 %shard_map.86 = (bf16[56,256]{1,0:T(8,128)(2,1)S(1)}, bf16[56,256]{1,0:T(8,128)(2,1)S(1)}, bf16[768,256]{1,0:T(8,128)(2,1)S(1)}, s32[64,256]{1,0:T(8,128)S(1)}, ...) custom-call(bf16[768,256]{1,0:T(8,128)(2,1)} %bitcast.18, ...), custom_call_target="tpu_custom_call" | custom-call | tf_op jit(solution)/shard_map/pallas_call | solution.py:317
  1.9 0.7 %collective-permute-start = (bf16[56,256]{1,0:T(8,128)(2,1)S(1)}, bf16[56,256]{1,0:T(8,128)(2,1)S(1)}, u32[]{:S(2)}, u32[]{:S(2)}) collective-permute-start(bf16[56,256]{1,0:T(8,128)(2,1)S(1)} %get-tuple-element.23), channel_id=1, source_target_pairs={{1,2},{3,4},{5,6},{7,8},{9,10},{11,12},{13,14},{2,1},{4,3},{6,5},{... | collective-permute-start | bytes 86024 | tf_op jit(solution)/shard_map/ppermute | solution.py:300
  2.6 4.6 %collective-permute-start.1 = (bf16[56,256]{1,0:T(8,128)(2,1)S(1)}, bf16[56,256]{1,0:T(8,128)(2,1)S(1)}, u32[]{:S(2)}, u32[]{:S(2)}) collective-permute-start(bf16[56,256]{1,0:T(8,128)(2,1)S(1)} %get-tuple-element.24), channel_id=1, source_target_pairs={{0,1},{2,3},{4,5},{6,7},{8,9},{10,11},{12,13},{14,15},{1,0},{3,2},... | collective-permute-start | bytes 86024 | tf_op jit(solution)/shard_map/ppermute | solution.py:300
  7.2 2.5 %shard_map.87 = (bf16[576,896]{1,0:T(8,128)(2,1)S(1)}, f32[192,256]{1,0:T(8,128)S(1)}, f32[96,96]{1,0:T(8,128)S(1)}) custom-call(bf16[768,256]{1,0:T(8,128)(2,1)S(1)} %get-tuple-element.25.cells, bf16[27,3,12]{2,1,0:T(4,128)(2,1)S(1)} %get-tuple-element.26.weights, f32[1,3]{1,0:T(1,128)S(1)} %get-tuple-element.27.bias, s32[64,256]{1,0:T(8,128)S(1)} %get-tuple-element.28.ids, ...), custom_call_target="tpu_custom_call" | custom-call | tf_op jit(solution)/shard_map/pallas_call | solution.py:327
  9.7 0.0 collective-permute-done.two
  9.7 0.0 collective-permute-done.1.one
  9.7 0.3 shard_map.89
  10.0 4.7 %collective-permute-start.2 = (f32[1,1024]{1,0:T(1,128)S(1)}, f32[1,1024]{1,0:T(1,128)S(1)}, u32[]{:S(2)}, u32[]{:S(2)}) collective-permute-start(f32[1,1024]{1,0:T(1,128)S(1)} %get-tuple-element.34), channel_id=1, source_target_pairs={{16,32},{48,64},{80,96},{32,16},{64,48},{96,80},{17,33},{49,65},{8... | collective-permute-start | bytes 12296 | tf_op jit(solution)/shard_map/ppermute | solution.py:300
  14.7 0.1 collective-permute-start.3
  14.8 1.7 %shard_map.88 = (f32[192,256]{1,0:T(8,128)S(1)}, f32[96,96]{1,0:T(8,128)S(1)}, f32[8,768]{1,0:T(8,128)S(1)}) custom-call(bf16[56,256]{1,0:T(8,128)(2,1)S(1)} %collective-permute-done.two, bf16[56,256]{1,0:T(8,128)(2,1)S(1)} %collective-permute-done.1.one, bf16[576,896]{1,0:T(8,128)(2,1)S(1)} %get-tuple-element.30.taps, ...), custom_call_target="tpu_custom_call" | custom-call | tf_op jit(solution)/shard_map/pallas_call | solution.py:344
  16.5 0.0 collective-permute-done.2.outer
  16.5 0.0 collective-permute-done.3.inner
  16.5 2.2 %shard_map.90 = (f32[192,8]{1,0:T(8,128)S(1)}, f32[192,8]{1,0:T(8,128)S(1)}, f32[128,128]{1,0:T(8,128)}) custom-call(f32[1,1024]{1,0:T(1,128)S(1)} %collective-permute-done.2.outer, f32[1,1024]{1,0:T(1,128)S(1)} %collective-permute-done.3.inner, bf16[576,896]{1,0:T(8,128)(2,1)S(1)} %get-tuple-element.30.taps, f32[192,256]{1,0:T(8,128)S(1)} %get-tuple-element.33.logits, ...), custom_call_target="tpu_custom_call" | custom-call | tf_op jit(solution)/shard_map/pallas_call | solution.py:352
  18.7 10.1 %all-to-all-start = ((f32[128,1,128]{2,1,0:T(1,128)}), f32[128,1,128]{2,1,0:T(1,128)S(1)}, u32[]{:S(2)}, u32[]{:S(2)}) async-start(f32[128,1,128]{2,1,0:T(1,128)} %bitcast.11), calls=%async_computation | async-start | bytes 131072 | tf_op jit(solution)/shard_map/all_to_all | solution.py:358
  28.8 0.8 %shard_map.91 = bf16[192,256]{1,0:T(8,128)(2,1)} custom-call(f32[192,256]{1,0:T(8,128)S(1)} %get-tuple-element.33.logits, f32[192,8]{1,0:T(8,128)S(1)} %get-tuple-element.40.first, f32[192,8]{1,0:T(8,128)S(1)} %get-tuple-element.41.last), custom_call_target="tpu_custom_call" | custom-call | tf_op jit(solution)/shard_map/pallas_call | solution.py:359
  29.6 8.8 %all-to-all-done = f32[128,1,128]{2,1,0:T(1,128)S(1)} async-done(((f32[128,1,128]{2,1,0:T(1,128)}), f32[128,1,128]{2,1,0:T(1,128)S(1)}, u32[]{:S(2)}, u32[]{:S(2)}) %all-to-all-start) | async-done | bytes 65568 | tf_op jit(solution)/shard_map/all_to_all | solution.py:358
  38.4 1.4 %shard_map.92 = f32[32,128]{1,0:T(8,128)} custom-call(f32[128,128]{1,0:T(8,128)S(1)} %bitcast.17, s32[64,128]{1,0:T(8,128)S(1)} %get-tuple-element.43.rows), custom_call_target="tpu_custom_call" | custom-call | tf_op jit(solution)/shard_map/pallas_call | solution.py:365
Async XLA Ops:
  1.9 7.8 %collective-permute-start = (bf16[56,256]{1,0:T(8,128)(2,1)S(1)}, bf16[56,256]{1,0:T(8,128)(2,1)S(1)}, u32[]{:S(2)}, u32[]{:S(2)}) collective-permute-start(bf16[56,256]{1,0:T(8,128)(2,1)S(1)} %get-tuple-element.23), channel_id=1, source_target_pairs={{1,2},{3,4},{5,6},{7,8},{9,10},{11,12},{13,14},{2,1},{4,3},{6,5},{... | collective-permute-start | bytes 86024 | tf_op jit(solution)/shard_map/ppermute | solution.py:300
  2.6 7.1 %collective-permute-start.1 = (bf16[56,256]{1,0:T(8,128)(2,1)S(1)}, bf16[56,256]{1,0:T(8,128)(2,1)S(1)}, u32[]{:S(2)}, u32[]{:S(2)}) collective-permute-start(bf16[56,256]{1,0:T(8,128)(2,1)S(1)} %get-tuple-element.24), channel_id=1, source_target_pairs={{0,1},{2,3},{4,5},{6,7},{8,9},{10,11},{12,13},{14,15},{1,0},{3,2},... | collective-permute-start | bytes 86024 | tf_op jit(solution)/shard_map/ppermute | solution.py:300
  10.0 6.5 %collective-permute-start.2 = (f32[1,1024]{1,0:T(1,128)S(1)}, f32[1,1024]{1,0:T(1,128)S(1)}, u32[]{:S(2)}, u32[]{:S(2)}) collective-permute-start(f32[1,1024]{1,0:T(1,128)S(1)} %get-tuple-element.34), channel_id=1, source_target_pairs={{16,32},{48,64},{80,96},{32,16},{64,48},{96,80},{17,33},{49,65},{8... | collective-permute-start | bytes 12296 | tf_op jit(solution)/shard_map/ppermute | solution.py:300
  14.7 1.8 %collective-permute-start.3 = (f32[1,1024]{1,0:T(1,128)S(1)}, f32[1,1024]{1,0:T(1,128)S(1)}, u32[]{:S(2)}, u32[]{:S(2)}) collective-permute-start(f32[1,1024]{1,0:T(1,128)S(1)} %get-tuple-element.35), channel_id=1, source_target_pairs={{0,16},{32,48},{64,80},{96,112},{16,0},{48,32},{80,64},{112,96},{1... | collective-permute-start | bytes 12296 | tf_op jit(solution)/shard_map/ppermute | solution.py:300
  18.7 19.7 %all-to-all-start = ((f32[128,1,128]{2,1,0:T(1,128)}), f32[128,1,128]{2,1,0:T(1,128)S(1)}, u32[]{:S(2)}, u32[]{:S(2)}) async-start(f32[128,1,128]{2,1,0:T(1,128)} %bitcast.11), calls=%async_computation | async-start | bytes 131072 | tf_op jit(solution)/shard_map/all_to_all | solution.py:358

commit v5 on v4

--- a/solution.py
+++ b/solution.py
@@ -19,7 +19,7 @@
 
 TAP_ROWS = 9 * ROWS
 PART = C_OUT * ROWS
-EARLY = 7
+EARLY = 9
 BATCH = 48
 LOW, HALF, STEP = 96, 48, 12
 
@@ -226,27 +226,32 @@
     fill_pairs(total, crossed, value, cross)
     pad = jnp.zeros((XD - PART, XD), f32)
     numbers = slots[...]
-    kinds = [crossed, pad, (numbers >> 7).astype(f32), pad, (numbers & 127).astype(f32), pad]
-    ends[...] = along(pick_ends(), jnp.concatenate(kinds, axis=0).astype(bf16))
+    kinds = [crossed, (numbers >> 7).astype(f32), (numbers & 127).astype(f32)]
+    rest = total
+    for _ in range(3):
+        kinds.append(rest.astype(bf16).astype(f32))
+        rest = rest - kinds[-1]
+    kinds = jnp.concatenate([part for kind in kinds for part in (kind, pad)], axis=0)
+    picked = along(pick_ends(), kinds.astype(bf16))
+    ends[:, : 3 * XD] = picked[:, : 3 * XD]
+    ends[:, 3 * XD :] = picked[:, 3 * XD : 4 * XD] + picked[:, 4 * XD : 5 * XD] + picked[:, 5 * XD :]
     chunks = [line for i in range(1, EARLY) for line in lines_of(i, (0, YD - 1), slots, value, cross)]
     chunks += [line for i in range(EARLY, C_OUT * Z) for line in lines_of(i, range(YD), slots, value, cross)]
     sums[...] = early[...] + batched(chunks)
 
 
-def send_kernel(outer, inner, taps, logits, own, ends, sums, bucket, first, last, outgoing):
+def end_rows(left, right):
+    row = iota((8, DEPTH), 0)
+    return jnp.where(row == 0, left[:, :DEPTH], jnp.where(row == 1, right[:, :DEPTH], 0.0)).astype(bf16)
+
+
+def send_kernel(outer, inner, taps, own, ends, sums, bucket, outgoing):
     left, right = placed(inner[...], outer[...], "gz")
-    row = iota((8, DEPTH), 0)
-    left_row = jnp.where(row == 0, left[:, :DEPTH], 0.0).astype(bf16)
-    right_row = jnp.where(row == 0, right[:, :DEPTH], 0.0).astype(bf16)
-    first[...] = along(taps[:PART], left_row)
-    last[...] = along(taps[2 * PART :], right_row)
-    lane = iota((PART, LANES), 1)
-    low = logits[:, :LANES] + first[:, 0:1]
-    high = logits[:, XD - LANES :] + last[:, 0:1]
-    soft = sigmoid(jnp.where(lane < LANES // 2, low, high))
-    row, lane = iota((8, LANES), 0), iota((8, LANES), 1)
-    pick = jnp.where((row < 2) & (lane == row * (LANES - 1)), 1.0, 0.0).astype(bf16)
-    soft = jnp.concatenate([along(pick, soft), jnp.zeros((8, XD - PART), f32)], axis=1)
+    both = end_rows(left, right)
+    first = along(both, taps[:PART])[0:1] + ends[0:1, 3 * XD : 3 * XD + PART]
+    last = along(both, taps[2 * PART :])[1:2] + ends[1:2, 3 * XD : 3 * XD + PART]
+    soft = sigmoid(jnp.concatenate([first, last], axis=0)).astype(f32)
+    soft = jnp.concatenate([soft, jnp.zeros((2, XD - PART), f32)], axis=1)
 
     beside = left[:, DEPTH : DEPTH + ROWS] * 128.0 + left[:, DEPTH + ROWS :]
     here = own[:, DEPTH : DEPTH + ROWS] * 128.0 + own[:, DEPTH + ROWS :]
@@ -257,10 +262,10 @@
         crossed = ends[end : end + 1, :XD]
         if end == 0:
             crossed = crossed + differs
-        slot = ends[end : end + 1, XD : 2 * XD] * 128.0 + ends[end : end + 1, 2 * XD :]
+        slot = ends[end : end + 1, XD : 2 * XD] * 128.0 + ends[end : end + 1, 2 * XD : 3 * XD]
         chunks.append((*split(slot.astype(i32)), (soft[end : end + 1] * crossed).astype(bf16), crossed.astype(bf16)))
     total = sums[...] + chunk_sums(chunks)
-    kinds = [relaid(total[:HALF].astype(bf16)), relaid(total[HALF:].astype(bf16))]
+    kinds = [[part.astype(bf16) for part in relaid(total[at : at + HALF])] for at in (0, HALF)]
     owners, places = small(bucket[...] >> 6), small(bucket[...] & 63)
     a_parts, b_parts = [], []
     for h in range(HIGH):
@@ -271,10 +276,13 @@
     outgoing[...] = sent
 
 
-def affinity_kernel(logits, first, last, affinity):
+def affinity_kernel(outer, inner, taps, logits, affinity):
+    both = end_rows(*placed(inner[...], outer[...], "gz"))
+    first = along(taps[:PART], both)[:, 0:1]
+    last = along(taps[2 * PART :], both)[:, 1:2]
     lane = iota((PART, XD), 1)
-    outer = jnp.where(lane == 0, first[:, 0:1], jnp.where(lane == XD - 1, last[:, 0:1], 0.0))
-    affinity[...] = sigmoid(logits[...] + outer)
+    ends = jnp.where(lane == 0, first, jnp.where(lane == XD - 1, last, 0.0))
+    affinity[...] = sigmoid(logits[...] + ends)
 
 
 def edges_kernel(arrived, rows, mean):
@@ -343,25 +351,25 @@
     inner = swapped(inner, "gz", 0)
     logits, sums, ends = pl.pallas_call(
         inner_kernel,
-        out_shape=(near((PART, XD), f32), sums_shape, near((8, 3 * XD), f32)),
+        out_shape=(near((PART, XD), f32), sums_shape, near((8, 4 * XD), f32)),
         in_specs=whole(7),
         out_specs=tuple(whole(3)),
         scratch_shapes=[pltpu.VMEM((LANES, XD), bf16)] + pairs,
     )(two, one, taps, logits, early, ids, slots)
     logits = held(logits)
-    first, last, outgoing = pl.pallas_call(
+    outgoing = pl.pallas_call(
         send_kernel,
-        out_shape=(near((PART, 8), f32), near((PART, 8), f32), near((devices, 2 * BUCKET), f32)),
-        in_specs=whole(8),
-        out_specs=tuple(whole(3)),
-    )(outer, inner, taps, logits, held(own), held(ends), held(sums), bucket)
+        out_shape=near((devices, 2 * BUCKET), f32),
+        in_specs=whole(7),
+        out_specs=whole(1)[0],
+    )(outer, inner, taps, held(own), held(ends), held(sums), bucket)
     arrived = lax.all_to_all(held(outgoing), ("gz", "yx"), split_axis=0, concat_axis=0, tiled=True)
     affinity = pl.pallas_call(
         affinity_kernel,
         out_shape=jax.ShapeDtypeStruct((PART, XD), bf16),
-        in_specs=whole(3),
+        in_specs=whole(4),
         out_specs=whole(1)[0],
-    )(logits, held(first), held(last))
+    )(outer, inner, taps, logits)
     mean = pl.pallas_call(
         edges_kernel,
         out_shape=jax.ShapeDtypeStruct((HIGH, LANES), f32),

time: 40 us -> 39.5 us (0.988)
  starting transfers between devices: 20.1 us -> 19.7 us
  transfers between devices with their start and end apart: 5 -> 5, of which waited for: 1 -> 1; matrix products, arithmetic and copies ran while one was open for 0% -> 0% of each run, Pallas kernels for 13% -> 14%
where the time goes in v5:
time: 39.5 us; the launch traced here: 39.3 us
  starting transfers between devices  19.7 us (50%)
  Pallas kernels  10.3 us (26%)
  waiting for transfers between devices  8.54 us (22%)
  between operations  0.73 us (2%)
    ppermute x4, starting transfers between devices, swapped(): return held(lax.ppermute(block, axis, pairs + [(j, i) for i, j in pairs]))  9.98 us
    all_to_all x1, starting transfers between devices, local(): lax.all_to_all(held(outgoing), ('gz', 'yx'), split_axis=0, concat_axis=0,...  9.72 us
    all_to_all x1, waiting for transfers between devices, local(): lax.all_to_all(held(outgoing), ('gz', 'yx'), split_axis=0, concat_axis=0,...  8.53 us
    pallas_call x1, Pallas kernels, local(): pl.pallas_call(taps_kernel, out_shape=(near((TAP_ROWS, DEPTH), bf16), nea...  2.9 us
    pallas_call x1, Pallas kernels, local(): pl.pallas_call(send_kernel, out_shape=near((devices, 2 * BUCKET), f32), i...  2.01 us
    pallas_call x1, Pallas kernels, local(): pl.pallas_call(edges_kernel, out_shape=jax.ShapeDtypeStruct((HIGH, LANES)...  1.41 us
    pallas_call x1, Pallas kernels, local(): pl.pallas_call(inner_kernel, out_shape=(near((PART, XD), f32), sums_shape...  1.4 us
    pallas_call x1, Pallas kernels, local(): pl.pallas_call(rows_kernel, out_shape=(lines, lines, *(near(x.shape, x.dt...  1.29 us
  transfers between devices with their start and end apart: 5, of which 1 were waited for; matrix products, arithmetic and copies ran while one was open for 0% of the time, Pallas kernels for 14%

profile of v5, /device:TPU:1, one launch (start us, length us, event | category | flops | bytes accessed | tf_op | source)
XLA Modules:
  0.0 39.3 jit_solution(5859862256831464656)
XLA Ops:
  0.6 1.3 %shard_map.86 = (bf16[56,256]{1,0:T(8,128)(2,1)S(1)}, bf16[56,256]{1,0:T(8,128)(2,1)S(1)}, bf16[768,256]{1,0:T(8,128)(2,1)S(1)}, s32[64,256]{1,0:T(8,128)S(1)}, ...) custom-call(bf16[768,256]{1,0:T(8,128)(2,1)} %bitcast.18, ...), custom_call_target="tpu_custom_call" | custom-call | tf_op jit(solution)/shard_map/pallas_call | solution.py:325
  1.9 0.7 %collective-permute-start = (bf16[56,256]{1,0:T(8,128)(2,1)S(1)}, bf16[56,256]{1,0:T(8,128)(2,1)S(1)}, u32[]{:S(2)}, u32[]{:S(2)}) collective-permute-start(bf16[56,256]{1,0:T(8,128)(2,1)S(1)} %get-tuple-element.20), channel_id=1, source_target_pairs={{1,2},{3,4},{5,6},{7,8},{9,10},{11,12},{13,14},{2,1},{4,3},{6,5},{... | collective-permute-start | bytes 86024 | tf_op jit(solution)/shard_map/ppermute | solution.py:308
  2.6 4.6 %collective-permute-start.1 = (bf16[56,256]{1,0:T(8,128)(2,1)S(1)}, bf16[56,256]{1,0:T(8,128)(2,1)S(1)}, u32[]{:S(2)}, u32[]{:S(2)}) collective-permute-start(bf16[56,256]{1,0:T(8,128)(2,1)S(1)} %get-tuple-element.21), channel_id=1, source_target_pairs={{0,1},{2,3},{4,5},{6,7},{8,9},{10,11},{12,13},{14,15},{1,0},{3,2},... | collective-permute-start | bytes 86024 | tf_op jit(solution)/shard_map/ppermute | solution.py:308
  7.2 2.9 %shard_map.87 = (bf16[576,896]{1,0:T(8,128)(2,1)S(1)}, f32[192,256]{1,0:T(8,128)S(1)}, f32[96,96]{1,0:T(8,128)S(1)}) custom-call(bf16[768,256]{1,0:T(8,128)(2,1)S(1)} %get-tuple-element.22.cells, bf16[27,3,12]{2,1,0:T(4,128)(2,1)S(1)} %get-tuple-element.24.weights, f32[1,3]{1,0:T(1,128)S(1)} %get-tuple-element.25.bias, s32[64,256]{1,0:T(8,128)S(1)} %get-tuple-element.23.ids, ...), custom_call_target="tpu_custom_call" | custom-call | tf_op jit(solution)/shard_map/pallas_call | solution.py:335
  10.1 0.0 collective-permute-done.two
  10.1 0.0 collective-permute-done.1.one
  10.1 0.3 shard_map.88
  10.4 4.7 %collective-permute-start.2 = (f32[1,1024]{1,0:T(1,128)S(1)}, f32[1,1024]{1,0:T(1,128)S(1)}, u32[]{:S(2)}, u32[]{:S(2)}) collective-permute-start(f32[1,1024]{1,0:T(1,128)S(1)} %get-tuple-element.28), channel_id=1, source_target_pairs={{16,32},{48,64},{80,96},{32,16},{64,48},{96,80},{17,33},{49,65},{8... | collective-permute-start | bytes 12296 | tf_op jit(solution)/shard_map/ppermute | solution.py:308
  15.0 0.1 collective-permute-start.3
  15.1 1.4 %shard_map.89 = (f32[192,256]{1,0:T(8,128)S(1)}, f32[96,96]{1,0:T(8,128)S(1)}, f32[8,1024]{1,0:T(8,128)S(1)}) custom-call(bf16[56,256]{1,0:T(8,128)(2,1)S(1)} %collective-permute-done.two, bf16[56,256]{1,0:T(8,128)(2,1)S(1)} %collective-permute-done.1.one, bf16[576,896]{1,0:T(8,128)(2,1)S(1)} %get-tuple-element.30.taps, ...), custom_call_target="tpu_custom_call" | custom-call | tf_op jit(solution)/shard_map/pallas_call | solution.py:352
  16.5 0.0 collective-permute-done.2.outer
  16.6 0.0 collective-permute-done.3.inner
  16.6 2.0 %shard_map.91 = f32[128,128]{1,0:T(8,128)} custom-call(f32[1,1024]{1,0:T(1,128)S(1)} %collective-permute-done.2.outer, f32[1,1024]{1,0:T(1,128)S(1)} %collective-permute-done.3.inner, bf16[576,896]{1,0:T(8,128)(2,1)S(1)} %get-tuple-element.30.taps, f32[1,1024]{1,0:T(1,128)S(1)} %get-tuple-element.33.own, f32[8,1024]{1,0:T(8,128)S(1)} %get-tuple-element.34.ends, ...), custom_call_target="tpu_custom_call" | custom-call | tf_op jit(solution)/shard_map/pallas_call | solution.py:360
  18.6 9.7 %all-to-all-start = ((f32[128,1,128]{2,1,0:T(1,128)}), f32[128,1,128]{2,1,0:T(1,128)S(1)}, u32[]{:S(2)}, u32[]{:S(2)}) async-start(f32[128,1,128]{2,1,0:T(1,128)} %bitcast.11), calls=%async_computation | async-start | bytes 131072 | tf_op jit(solution)/shard_map/all_to_all | solution.py:366
  28.3 1.1 %shard_map.90 = bf16[192,256]{1,0:T(8,128)(2,1)} custom-call(f32[1,1024]{1,0:T(1,128)S(1)} %collective-permute-done.2.outer, f32[1,1024]{1,0:T(1,128)S(1)} %collective-permute-done.3.inner, bf16[576,896]{1,0:T(8,128)(2,1)S(1)} %get-tuple-element.30.taps, f32[192,256]{1,0:T(8,128)S(1)} %get-tuple-element.32.logits), custom_call_target="tpu_custom_call" | custom-call | tf_op jit(solution)/shard_map/pallas_call | solution.py:367
  29.4 8.5 %all-to-all-done = f32[128,1,128]{2,1,0:T(1,128)S(1)} async-done(((f32[128,1,128]{2,1,0:T(1,128)}), f32[128,1,128]{2,1,0:T(1,128)S(1)}, u32[]{:S(2)}, u32[]{:S(2)}) %all-to-all-start) | async-done | bytes 65568 | tf_op jit(solution)/shard_map/all_to_all | solution.py:366
  37.9 1.4 %shard_map.92 = f32[32,128]{1,0:T(8,128)} custom-call(f32[128,128]{1,0:T(8,128)S(1)} %bitcast.17, s32[64,128]{1,0:T(8,128)S(1)} %get-tuple-element.37.rows), custom_call_target="tpu_custom_call" | custom-call | tf_op jit(solution)/shard_map/pallas_call | solution.py:373
Async XLA Ops:
  1.9 8.2 %collective-permute-start = (bf16[56,256]{1,0:T(8,128)(2,1)S(1)}, bf16[56,256]{1,0:T(8,128)(2,1)S(1)}, u32[]{:S(2)}, u32[]{:S(2)}) collective-permute-start(bf16[56,256]{1,0:T(8,128)(2,1)S(1)} %get-tuple-element.20), channel_id=1, source_target_pairs={{1,2},{3,4},{5,6},{7,8},{9,10},{11,12},{13,14},{2,1},{4,3},{6,5},{... | collective-permute-start | bytes 86024 | tf_op jit(solution)/shard_map/ppermute | solution.py:308
  2.6 7.5 %collective-permute-start.1 = (bf16[56,256]{1,0:T(8,128)(2,1)S(1)}, bf16[56,256]{1,0:T(8,128)(2,1)S(1)}, u32[]{:S(2)}, u32[]{:S(2)}) collective-permute-start(bf16[56,256]{1,0:T(8,128)(2,1)S(1)} %get-tuple-element.21), channel_id=1, source_target_pairs={{0,1},{2,3},{4,5},{6,7},{8,9},{10,11},{12,13},{14,15},{1,0},{3,2},... | collective-permute-start | bytes 86024 | tf_op jit(solution)/shard_map/ppermute | solution.py:308
  10.4 6.2 %collective-permute-start.2 = (f32[1,1024]{1,0:T(1,128)S(1)}, f32[1,1024]{1,0:T(1,128)S(1)}, u32[]{:S(2)}, u32[]{:S(2)}) collective-permute-start(f32[1,1024]{1,0:T(1,128)S(1)} %get-tuple-element.28), channel_id=1, source_target_pairs={{16,32},{48,64},{80,96},{32,16},{64,48},{96,80},{17,33},{49,65},{8... | collective-permute-start | bytes 12296 | tf_op jit(solution)/shard_map/ppermute | solution.py:308
  15.0 1.5 %collective-permute-start.3 = (f32[1,1024]{1,0:T(1,128)S(1)}, f32[1,1024]{1,0:T(1,128)S(1)}, u32[]{:S(2)}, u32[]{:S(2)}) collective-permute-start(f32[1,1024]{1,0:T(1,128)S(1)} %get-tuple-element.29), channel_id=1, source_target_pairs={{0,16},{32,48},{64,80},{96,112},{16,0},{48,32},{80,64},{112,96},{1... | collective-permute-start | bytes 12296 | tf_op jit(solution)/shard_map/ppermute | solution.py:308
  18.6 19.3 %all-to-all-start = ((f32[128,1,128]{2,1,0:T(1,128)}), f32[128,1,128]{2,1,0:T(1,128)S(1)}, u32[]{:S(2)}, u32[]{:S(2)}) async-start(f32[128,1,128]{2,1,0:T(1,128)} %bitcast.11), calls=%async_computation | async-start | bytes 131072 | tf_op jit(solution)/shard_map/all_to_all | solution.py:366

commit v6 on v5

--- a/solution.py
+++ b/solution.py
@@ -75,8 +75,10 @@
 
 
 def placed(inner, outer, axis):
-    first = even(axis)
-    return jnp.where(first, outer, inner), jnp.where(first, inner, outer)
+    at, last, first = lax.axis_index(axis), lax.axis_size(axis) - 1, even(axis)
+    before, after = jnp.where(first, outer, inner), jnp.where(first, inner, outer)
+    zero = jnp.zeros((), before.dtype)
+    return jnp.where(at == 0, zero, before), jnp.where(at == last, zero, after)
 
 
 def pick_ends():
@@ -303,9 +305,14 @@
         mean[h : h + 1] = parts[j][k : k + 1]
 
 
-def swapped(block, axis, first):
-    pairs = [(i, i + 1) for i in range(first, lax.axis_size(axis) - 1, 2)]
-    return held(lax.ppermute(block, axis, pairs + [(j, i) for i, j in pairs]))
+def swapped(block, axis, first, ring=False):
+    size = lax.axis_size(axis)
+    other = [i + 1 if (i - first) % 2 == 0 else i - 1 for i in range(size)]
+    if ring:
+        other = [i % size for i in other]
+    else:
+        other = [j if 0 <= j < size else i for i, j in enumerate(other)]
+    return held(lax.ppermute(block, axis, list(enumerate(other))))
 
 
 def local(features, conv_weight, conv_bias, fragments, pair_slot, slot_bucket, arrival_row):
@@ -330,7 +337,7 @@
         scratch_shapes=[pltpu.SemaphoreType.DMA((len(inputs),))],
     )(*inputs)
     cells, ids, slots, weights, bucket, targets, bias = map(held, inputs)
-    two = swapped(two, "yx", 1)
+    two = swapped(two, "yx", 1, ring=True)
     one = swapped(one, "yx", 0)
     taps, logits, early = pl.pallas_call(
         taps_kernel,
@@ -347,7 +354,7 @@
         out_specs=tuple(whole(3)),
         scratch_shapes=[pltpu.VMEM((WIDE, XD), bf16)],
     )(two, one, cells, ids, early)
-    outer = swapped(outer, "gz", 1)
+    outer = swapped(outer, "gz", 1, ring=True)
     inner = swapped(inner, "gz", 0)
     logits, sums, ends = pl.pallas_call(
         inner_kernel,

time: 39.5 us -> 36.8 us (0.932)
  starting transfers between devices: 19.7 us -> 17.1 us
    all_to_all x1, starting transfers between devices: 9.72 us -> 7.01 us  [local(): lax.all_to_all(held(outgoing), ('gz', 'yx'), split_axis=0, concat_axis=0,...]
  transfers between devices with their start and end apart: 5 -> 5, of which waited for: 1 -> 1; matrix products, arithmetic and copies ran while one was open for 0% -> 0% of each run, Pallas kernels for 14% -> 15%
where the time goes in v6:
time: 36.8 us; the launch traced here: 36.6 us
  starting transfers between devices  17.1 us (46%)
  Pallas kernels  10.3 us (28%)
  waiting for transfers between devices  8.54 us (23%)
  between operations  0.71 us (2%)
    ppermute x4, starting transfers between devices, swapped(): return held(lax.ppermute(block, axis, list(enumerate(other))))  10.1 us
    all_to_all x1, waiting for transfers between devices, local(): lax.all_to_all(held(outgoing), ('gz', 'yx'), split_axis=0, concat_axis=0,...  8.53 us
    all_to_all x1, starting transfers between devices, local(): lax.all_to_all(held(outgoing), ('gz', 'yx'), split_axis=0, concat_axis=0,...  7.01 us
    pallas_call x1, Pallas kernels, local(): pl.pallas_call(taps_kernel, out_shape=(near((TAP_ROWS, DEPTH), bf16), nea...  2.91 us
    pallas_call x1, Pallas kernels, local(): pl.pallas_call(send_kernel, out_shape=near((devices, 2 * BUCKET), f32), i...  2.01 us
    pallas_call x1, Pallas kernels, local(): pl.pallas_call(edges_kernel, out_shape=jax.ShapeDtypeStruct((HIGH, LANES)...  1.42 us
    pallas_call x1, Pallas kernels, local(): pl.pallas_call(inner_kernel, out_shape=(near((PART, XD), f32), sums_shape...  1.4 us
    pallas_call x1, Pallas kernels, local(): pl.pallas_call(rows_kernel, out_shape=(lines, lines, *(near(x.shape, x.dt...  1.29 us
  transfers between devices with their start and end apart: 5, of which 1 were waited for; matrix products, arithmetic and copies ran while one was open for 0% of the time, Pallas kernels for 15%

profile of v6, /device:TPU:1, one launch (start us, length us, event | category | flops | bytes accessed | tf_op | source)
XLA Modules:
  0.0 36.6 jit_solution(15607565213441615502)
XLA Ops:
  0.6 1.3 %shard_map.86 = (bf16[56,256]{1,0:T(8,128)(2,1)S(1)}, bf16[56,256]{1,0:T(8,128)(2,1)S(1)}, bf16[768,256]{1,0:T(8,128)(2,1)S(1)}, s32[64,256]{1,0:T(8,128)S(1)}, ...) custom-call(bf16[768,256]{1,0:T(8,128)(2,1)} %bitcast.18, ...), custom_call_target="tpu_custom_call" | custom-call | tf_op jit(solution)/shard_map/pallas_call | solution.py:332
  1.9 5.8 %collective-permute-start = (bf16[56,256]{1,0:T(8,128)(2,1)S(1)}, bf16[56,256]{1,0:T(8,128)(2,1)S(1)}, u32[]{:S(2)}, u32[]{:S(2)}) collective-permute-start(bf16[56,256]{1,0:T(8,128)(2,1)S(1)} %get-tuple-element.20), channel_id=1, source_target_pairs={{0,15},{1,2},{2,1},{3,4},{4,3},{5,6},{6,5},{7,8},{8,7},{9,10},{10,... | collective-permute-start | bytes 86024 | tf_op jit(solution)/shard_map/ppermute | solution.py:315
  7.8 0.0 collective-permute-start.1
  7.8 2.9 %shard_map.87 = (bf16[576,896]{1,0:T(8,128)(2,1)S(1)}, f32[192,256]{1,0:T(8,128)S(1)}, f32[96,96]{1,0:T(8,128)S(1)}) custom-call(bf16[768,256]{1,0:T(8,128)(2,1)S(1)} %get-tuple-element.22.cells, bf16[27,3,12]{2,1,0:T(4,128)(2,1)S(1)} %get-tuple-element.24.weights, f32[1,3]{1,0:T(1,128)S(1)} %get-tuple-element.25.bias, s32[64,256]{1,0:T(8,128)S(1)} %get-tuple-element.23.ids, ...), custom_call_target="tpu_custom_call" | custom-call | tf_op jit(solution)/shard_map/pallas_call | solution.py:342
  10.7 0.0 collective-permute-done.two
  10.7 0.0 collective-permute-done.1.one
  10.7 0.3 shard_map.88
  11.0 3.5 %collective-permute-start.2 = (f32[1,1024]{1,0:T(1,128)S(1)}, f32[1,1024]{1,0:T(1,128)S(1)}, u32[]{:S(2)}, u32[]{:S(2)}) collective-permute-start(f32[1,1024]{1,0:T(1,128)S(1)} %get-tuple-element.28), channel_id=1, source_target_pairs={{0,112},{16,32},{32,16},{48,64},{64,48},{80,96},{96,80},{112,0},{1... | collective-permute-start | bytes 12296 | tf_op jit(solution)/shard_map/ppermute | solution.py:315
  14.4 0.7 %collective-permute-start.3 = (f32[1,1024]{1,0:T(1,128)S(1)}, f32[1,1024]{1,0:T(1,128)S(1)}, u32[]{:S(2)}, u32[]{:S(2)}) collective-permute-start(f32[1,1024]{1,0:T(1,128)S(1)} %get-tuple-element.29), channel_id=1, source_target_pairs={{0,16},{16,0},{32,48},{48,32},{64,80},{80,64},{96,112},{112,96},{1... | collective-permute-start | bytes 12296 | tf_op jit(solution)/shard_map/ppermute | solution.py:315
  15.2 1.4 %shard_map.89 = (f32[192,256]{1,0:T(8,128)S(1)}, f32[96,96]{1,0:T(8,128)S(1)}, f32[8,1024]{1,0:T(8,128)S(1)}) custom-call(bf16[56,256]{1,0:T(8,128)(2,1)S(1)} %collective-permute-done.two, bf16[56,256]{1,0:T(8,128)(2,1)S(1)} %collective-permute-done.1.one, bf16[576,896]{1,0:T(8,128)(2,1)S(1)} %get-tuple-element.30.taps, ...), custom_call_target="tpu_custom_call" | custom-call | tf_op jit(solution)/shard_map/pallas_call | solution.py:359
  16.6 0.0 collective-permute-done.2.outer
  16.6 0.0 collective-permute-done.3.inner
  16.6 2.0 %shard_map.91 = f32[128,128]{1,0:T(8,128)} custom-call(f32[1,1024]{1,0:T(1,128)S(1)} %collective-permute-done.2.outer, f32[1,1024]{1,0:T(1,128)S(1)} %collective-permute-done.3.inner, bf16[576,896]{1,0:T(8,128)(2,1)S(1)} %get-tuple-element.30.taps, f32[1,1024]{1,0:T(1,128)S(1)} %get-tuple-element.33.own, f32[8,1024]{1,0:T(8,128)S(1)} %get-tuple-element.34.ends, ...), custom_call_target="tpu_custom_call" | custom-call | tf_op jit(solution)/shard_map/pallas_call | solution.py:367
  18.6 7.0 %all-to-all-start = ((f32[128,1,128]{2,1,0:T(1,128)}), f32[128,1,128]{2,1,0:T(1,128)S(1)}, u32[]{:S(2)}, u32[]{:S(2)}) async-start(f32[128,1,128]{2,1,0:T(1,128)} %bitcast.11), calls=%async_computation | async-start | bytes 131072 | tf_op jit(solution)/shard_map/all_to_all | solution.py:373
  25.6 1.1 %shard_map.90 = bf16[192,256]{1,0:T(8,128)(2,1)} custom-call(f32[1,1024]{1,0:T(1,128)S(1)} %collective-permute-done.2.outer, f32[1,1024]{1,0:T(1,128)S(1)} %collective-permute-done.3.inner, bf16[576,896]{1,0:T(8,128)(2,1)S(1)} %get-tuple-element.30.taps, f32[192,256]{1,0:T(8,128)S(1)} %get-tuple-element.32.logits), custom_call_target="tpu_custom_call" | custom-call | tf_op jit(solution)/shard_map/pallas_call | solution.py:374
  26.7 8.5 %all-to-all-done = f32[128,1,128]{2,1,0:T(1,128)S(1)} async-done(((f32[128,1,128]{2,1,0:T(1,128)}), f32[128,1,128]{2,1,0:T(1,128)S(1)}, u32[]{:S(2)}, u32[]{:S(2)}) %all-to-all-start) | async-done | bytes 65568 | tf_op jit(solution)/shard_map/all_to_all | solution.py:373
  35.2 1.4 %shard_map.92 = f32[32,128]{1,0:T(8,128)} custom-call(f32[128,128]{1,0:T(8,128)S(1)} %bitcast.17, s32[64,128]{1,0:T(8,128)S(1)} %get-tuple-element.37.rows), custom_call_target="tpu_custom_call" | custom-call | tf_op jit(solution)/shard_map/pallas_call | solution.py:380
Async XLA Ops:
  1.9 8.7 %collective-permute-start = (bf16[56,256]{1,0:T(8,128)(2,1)S(1)}, bf16[56,256]{1,0:T(8,128)(2,1)S(1)}, u32[]{:S(2)}, u32[]{:S(2)}) collective-permute-start(bf16[56,256]{1,0:T(8,128)(2,1)S(1)} %get-tuple-element.20), channel_id=1, source_target_pairs={{0,15},{1,2},{2,1},{3,4},{4,3},{5,6},{6,5},{7,8},{8,7},{9,10},{10,... | collective-permute-start | bytes 86024 | tf_op jit(solution)/shard_map/ppermute | solution.py:315
  7.8 2.9 %collective-permute-start.1 = (bf16[56,256]{1,0:T(8,128)(2,1)S(1)}, bf16[56,256]{1,0:T(8,128)(2,1)S(1)}, u32[]{:S(2)}, u32[]{:S(2)}) collective-permute-start(bf16[56,256]{1,0:T(8,128)(2,1)S(1)} %get-tuple-element.21), channel_id=1, source_target_pairs={{0,1},{1,0},{2,3},{3,2},{4,5},{5,4},{6,7},{7,6},{8,9},{9,8},{10,11... | collective-permute-start | bytes 86024 | tf_op jit(solution)/shard_map/ppermute | solution.py:315
  11.0 5.6 %collective-permute-start.2 = (f32[1,1024]{1,0:T(1,128)S(1)}, f32[1,1024]{1,0:T(1,128)S(1)}, u32[]{:S(2)}, u32[]{:S(2)}) collective-permute-start(f32[1,1024]{1,0:T(1,128)S(1)} %get-tuple-element.28), channel_id=1, source_target_pairs={{0,112},{16,32},{32,16},{48,64},{64,48},{80,96},{96,80},{112,0},{1... | collective-permute-start | bytes 12296 | tf_op jit(solution)/shard_map/ppermute | solution.py:315
  14.4 2.2 %collective-permute-start.3 = (f32[1,1024]{1,0:T(1,128)S(1)}, f32[1,1024]{1,0:T(1,128)S(1)}, u32[]{:S(2)}, u32[]{:S(2)}) collective-permute-start(f32[1,1024]{1,0:T(1,128)S(1)} %get-tuple-element.29), channel_id=1, source_target_pairs={{0,16},{16,0},{32,48},{48,32},{64,80},{80,64},{96,112},{112,96},{1... | collective-permute-start | bytes 12296 | tf_op jit(solution)/shard_map/ppermute | solution.py:315
  18.6 16.6 %all-to-all-start = ((f32[128,1,128]{2,1,0:T(1,128)}), f32[128,1,128]{2,1,0:T(1,128)S(1)}, u32[]{:S(2)}, u32[]{:S(2)}) async-start(f32[128,1,128]{2,1,0:T(1,128)} %bitcast.11), calls=%async_computation | async-start | bytes 131072 | tf_op jit(solution)/shard_map/all_to_all | solution.py:373

commit v7 on v5

--- a/solution.py
+++ b/solution.py
@@ -75,8 +75,10 @@
 
 
 def placed(inner, outer, axis):
-    first = even(axis)
-    return jnp.where(first, outer, inner), jnp.where(first, inner, outer)
+    at, last, first = lax.axis_index(axis), lax.axis_size(axis) - 1, even(axis)
+    before, after = jnp.where(first, outer, inner), jnp.where(first, inner, outer)
+    zero = jnp.zeros((), before.dtype)
+    return jnp.where(at == 0, zero, before), jnp.where(at == last, zero, after)
 
 
 def pick_ends():
@@ -304,8 +306,18 @@
 
 
 def swapped(block, axis, first):
-    pairs = [(i, i + 1) for i in range(first, lax.axis_size(axis) - 1, 2)]
-    return held(lax.ppermute(block, axis, pairs + [(j, i) for i, j in pairs]))
+    gz, yx = lax.axis_size("gz"), lax.axis_size("yx")
+    pairs = []
+    for g in range(gz):
+        for y in range(yx):
+            at, size = (g, gz) if axis == "gz" else (y, yx)
+            to = at + 1 if (at - first) % 2 == 0 else at - 1
+            if not 0 <= to < size:
+                g_to, y_to = (g, y ^ 1) if axis == "gz" else (g ^ 1, y)
+            else:
+                g_to, y_to = (to, y) if axis == "gz" else (g, to)
+            pairs.append((g * yx + y, g_to * yx + y_to))
+    return held(lax.ppermute(block, ("gz", "yx"), pairs))
 
 
 def local(features, conv_weight, conv_bias, fragments, pair_slot, slot_bucket, arrival_row):

time: 39.5 us -> 35.8 us (0.906)
  starting transfers between devices: 19.7 us -> 16 us
    ppermute x4, starting transfers between devices: 9.98 us -> 6.16 us  [swapped(): return held(lax.ppermute(block, ('gz', 'yx'), pairs))]
  transfers between devices with their start and end apart: 5 -> 5, of which waited for: 1 -> 1; matrix products, arithmetic and copies ran while one was open for 0% -> 0% of each run, Pallas kernels for 14% -> 15%
where the time goes in v7:
time: 35.8 us; the launch traced here: 35.6 us
  starting transfers between devices  16 us (45%)
  Pallas kernels  10.3 us (29%)
  waiting for transfers between devices  8.54 us (24%)
  between operations  0.71 us (2%)
    all_to_all x1, starting transfers between devices, local(): lax.all_to_all(held(outgoing), ('gz', 'yx'), split_axis=0, concat_axis=0,...  9.88 us
    all_to_all x1, waiting for transfers between devices, local(): lax.all_to_all(held(outgoing), ('gz', 'yx'), split_axis=0, concat_axis=0,...  8.53 us
    ppermute x4, starting transfers between devices, swapped(): return held(lax.ppermute(block, ('gz', 'yx'), pairs))  6.16 us
    pallas_call x1, Pallas kernels, local(): pl.pallas_call(taps_kernel, out_shape=(near((TAP_ROWS, DEPTH), bf16), nea...  2.9 us
    pallas_call x1, Pallas kernels, local(): pl.pallas_call(send_kernel, out_shape=near((devices, 2 * BUCKET), f32), i...  2.01 us
    pallas_call x1, Pallas kernels, local(): pl.pallas_call(edges_kernel, out_shape=jax.ShapeDtypeStruct((HIGH, LANES)...  1.42 us
    pallas_call x1, Pallas kernels, local(): pl.pallas_call(inner_kernel, out_shape=(near((PART, XD), f32), sums_shape...  1.39 us
    pallas_call x1, Pallas kernels, local(): pl.pallas_call(rows_kernel, out_shape=(lines, lines, *(near(x.shape, x.dt...  1.29 us
  transfers between devices with their start and end apart: 5, of which 1 were waited for; matrix products, arithmetic and copies ran while one was open for 0% of the time, Pallas kernels for 15%

profile of v7, /device:TPU:1, one launch (start us, length us, event | category | flops | bytes accessed | tf_op | source)
XLA Modules:
  0.0 35.6 jit_solution(998338392315662529)
XLA Ops:
  0.6 1.3 %shard_map.86 = (bf16[56,256]{1,0:T(8,128)(2,1)S(1)}, bf16[56,256]{1,0:T(8,128)(2,1)S(1)}, bf16[768,256]{1,0:T(8,128)(2,1)S(1)}, s32[64,256]{1,0:T(8,128)S(1)}, ...) custom-call(bf16[768,256]{1,0:T(8,128)(2,1)} %bitcast.18, ...), custom_call_target="tpu_custom_call" | custom-call | tf_op jit(solution)/shard_map/pallas_call | solution.py:337
  1.9 1.5 %collective-permute-start = (bf16[56,256]{1,0:T(8,128)(2,1)S(1)}, bf16[56,256]{1,0:T(8,128)(2,1)S(1)}, u32[]{:S(2)}, u32[]{:S(2)}) collective-permute-start(bf16[56,256]{1,0:T(8,128)(2,1)S(1)} %get-tuple-element.20), channel_id=1, source_target_pairs={{0,16},{1,2},{2,1},{3,4},{4,3},{5,6},{6,5},{7,8},{8,7},{9,10},{10,... | collective-permute-start | bytes 86024 | tf_op jit(solution)/shard_map/ppermute | solution.py:320
  3.4 1.9 %collective-permute-start.1 = (bf16[56,256]{1,0:T(8,128)(2,1)S(1)}, bf16[56,256]{1,0:T(8,128)(2,1)S(1)}, u32[]{:S(2)}, u32[]{:S(2)}) collective-permute-start(bf16[56,256]{1,0:T(8,128)(2,1)S(1)} %get-tuple-element.21), channel_id=1, source_target_pairs={{0,1},{1,0},{2,3},{3,2},{4,5},{5,4},{6,7},{7,6},{8,9},{9,8},{10,11... | collective-permute-start | bytes 86024 | tf_op jit(solution)/shard_map/ppermute | solution.py:320
  5.2 2.9 %shard_map.87 = (bf16[576,896]{1,0:T(8,128)(2,1)S(1)}, f32[192,256]{1,0:T(8,128)S(1)}, f32[96,96]{1,0:T(8,128)S(1)}) custom-call(bf16[768,256]{1,0:T(8,128)(2,1)S(1)} %get-tuple-element.22.cells, bf16[27,3,12]{2,1,0:T(4,128)(2,1)S(1)} %get-tuple-element.24.weights, f32[1,3]{1,0:T(1,128)S(1)} %get-tuple-element.25.bias, s32[64,256]{1,0:T(8,128)S(1)} %get-tuple-element.23.ids, ...), custom_call_target="tpu_custom_call" | custom-call | tf_op jit(solution)/shard_map/pallas_call | solution.py:347
  8.2 0.0 collective-permute-done.two
  8.2 0.0 collective-permute-done.1.one
  8.2 0.3 shard_map.88
  8.4 2.8 %collective-permute-start.2 = (f32[1,1024]{1,0:T(1,128)S(1)}, f32[1,1024]{1,0:T(1,128)S(1)}, u32[]{:S(2)}, u32[]{:S(2)}) collective-permute-start(f32[1,1024]{1,0:T(1,128)S(1)} %get-tuple-element.28), channel_id=1, source_target_pairs={{0,1},{1,0},{2,3},{3,2},{4,5},{5,4},{6,7},{7,6},{8,9},{9,8},{10,11... | collective-permute-start | bytes 12296 | tf_op jit(solution)/shard_map/ppermute | solution.py:320
  11.3 0.0 collective-permute-start.3
  11.3 1.4 %shard_map.89 = (f32[192,256]{1,0:T(8,128)S(1)}, f32[96,96]{1,0:T(8,128)S(1)}, f32[8,1024]{1,0:T(8,128)S(1)}) custom-call(bf16[56,256]{1,0:T(8,128)(2,1)S(1)} %collective-permute-done.two, bf16[56,256]{1,0:T(8,128)(2,1)S(1)} %collective-permute-done.1.one, bf16[576,896]{1,0:T(8,128)(2,1)S(1)} %get-tuple-element.30.taps, ...), custom_call_target="tpu_custom_call" | custom-call | tf_op jit(solution)/shard_map/pallas_call | solution.py:364
  12.7 0.0 collective-permute-done.2.outer
  12.7 0.0 collective-permute-done.3.inner
  12.7 2.0 %shard_map.91 = f32[128,128]{1,0:T(8,128)} custom-call(f32[1,1024]{1,0:T(1,128)S(1)} %collective-permute-done.2.outer, f32[1,1024]{1,0:T(1,128)S(1)} %collective-permute-done.3.inner, bf16[576,896]{1,0:T(8,128)(2,1)S(1)} %get-tuple-element.30.taps, f32[1,1024]{1,0:T(1,128)S(1)} %get-tuple-element.33.own, f32[8,1024]{1,0:T(8,128)S(1)} %get-tuple-element.34.ends, ...), custom_call_target="tpu_custom_call" | custom-call | tf_op jit(solution)/shard_map/pallas_call | solution.py:372
  14.7 9.9 %all-to-all-start = ((f32[128,1,128]{2,1,0:T(1,128)}), f32[128,1,128]{2,1,0:T(1,128)S(1)}, u32[]{:S(2)}, u32[]{:S(2)}) async-start(f32[128,1,128]{2,1,0:T(1,128)} %bitcast.11), calls=%async_computation | async-start | bytes 131072 | tf_op jit(solution)/shard_map/all_to_all | solution.py:378
  24.6 1.1 %shard_map.90 = bf16[192,256]{1,0:T(8,128)(2,1)} custom-call(f32[1,1024]{1,0:T(1,128)S(1)} %collective-permute-done.2.outer, f32[1,1024]{1,0:T(1,128)S(1)} %collective-permute-done.3.inner, bf16[576,896]{1,0:T(8,128)(2,1)S(1)} %get-tuple-element.30.taps, f32[192,256]{1,0:T(8,128)S(1)} %get-tuple-element.32.logits), custom_call_target="tpu_custom_call" | custom-call | tf_op jit(solution)/shard_map/pallas_call | solution.py:379
  25.7 8.5 %all-to-all-done = f32[128,1,128]{2,1,0:T(1,128)S(1)} async-done(((f32[128,1,128]{2,1,0:T(1,128)}), f32[128,1,128]{2,1,0:T(1,128)S(1)}, u32[]{:S(2)}, u32[]{:S(2)}) %all-to-all-start) | async-done | bytes 65568 | tf_op jit(solution)/shard_map/all_to_all | solution.py:378
  34.2 1.4 %shard_map.92 = f32[32,128]{1,0:T(8,128)} custom-call(f32[128,128]{1,0:T(8,128)S(1)} %bitcast.17, s32[64,128]{1,0:T(8,128)S(1)} %get-tuple-element.37.rows), custom_call_target="tpu_custom_call" | custom-call | tf_op jit(solution)/shard_map/pallas_call | solution.py:385
Async XLA Ops:
  1.9 6.2 %collective-permute-start = (bf16[56,256]{1,0:T(8,128)(2,1)S(1)}, bf16[56,256]{1,0:T(8,128)(2,1)S(1)}, u32[]{:S(2)}, u32[]{:S(2)}) collective-permute-start(bf16[56,256]{1,0:T(8,128)(2,1)S(1)} %get-tuple-element.20), channel_id=1, source_target_pairs={{0,16},{1,2},{2,1},{3,4},{4,3},{5,6},{6,5},{7,8},{8,7},{9,10},{10,... | collective-permute-start | bytes 86024 | tf_op jit(solution)/shard_map/ppermute | solution.py:320
  3.4 4.8 %collective-permute-start.1 = (bf16[56,256]{1,0:T(8,128)(2,1)S(1)}, bf16[56,256]{1,0:T(8,128)(2,1)S(1)}, u32[]{:S(2)}, u32[]{:S(2)}) collective-permute-start(bf16[56,256]{1,0:T(8,128)(2,1)S(1)} %get-tuple-element.21), channel_id=1, source_target_pairs={{0,1},{1,0},{2,3},{3,2},{4,5},{5,4},{6,7},{7,6},{8,9},{9,8},{10,11... | collective-permute-start | bytes 86024 | tf_op jit(solution)/shard_map/ppermute | solution.py:320
  8.4 4.2 %collective-permute-start.2 = (f32[1,1024]{1,0:T(1,128)S(1)}, f32[1,1024]{1,0:T(1,128)S(1)}, u32[]{:S(2)}, u32[]{:S(2)}) collective-permute-start(f32[1,1024]{1,0:T(1,128)S(1)} %get-tuple-element.28), channel_id=1, source_target_pairs={{0,1},{1,0},{2,3},{3,2},{4,5},{5,4},{6,7},{7,6},{8,9},{9,8},{10,11... | collective-permute-start | bytes 12296 | tf_op jit(solution)/shard_map/ppermute | solution.py:320
  11.3 1.4 %collective-permute-start.3 = (f32[1,1024]{1,0:T(1,128)S(1)}, f32[1,1024]{1,0:T(1,128)S(1)}, u32[]{:S(2)}, u32[]{:S(2)}) collective-permute-start(f32[1,1024]{1,0:T(1,128)S(1)} %get-tuple-element.29), channel_id=1, source_target_pairs={{0,16},{1,17},{2,18},{3,19},{4,20},{5,21},{6,22},{7,23},{8,24},{9,... | collective-permute-start | bytes 12296 | tf_op jit(solution)/shard_map/ppermute | solution.py:320
  14.7 19.5 %all-to-all-start = ((f32[128,1,128]{2,1,0:T(1,128)}), f32[128,1,128]{2,1,0:T(1,128)S(1)}, u32[]{:S(2)}, u32[]{:S(2)}) async-start(f32[128,1,128]{2,1,0:T(1,128)} %bitcast.11), calls=%async_computation | async-start | bytes 131072 | tf_op jit(solution)/shard_map/all_to_all | solution.py:378

commit v8 on v7

--- a/solution.py
+++ b/solution.py
@@ -288,10 +288,7 @@
 
 
 def edges_kernel(arrived, rows, mean):
-    n = arrived.shape[0]
-    same = jnp.where(iota((n, n), 0) == iota((n, n), 1), 1.0, 0.0).astype(bf16)
-    got = lax.dot_general(arrived[...].astype(bf16), same, (((0,), (0,)), ((), ())), preferred_element_type=f32)
-    got = got.astype(bf16)
+    got = arrived[...].T.astype(bf16)
     row, column = split(rows[...])
     total = chunk_sums(
         [

time: 35.8 us -> 35.7 us (level)
  no operation moved by 1% of the time
where the time goes in v8:
time: 35.7 us; the launch traced here: 35.5 us
  starting transfers between devices  16 us (45%)
  Pallas kernels  10.2 us (29%)
  waiting for transfers between devices  8.54 us (24%)
  between operations  0.71 us (2%)
    all_to_all x1, starting transfers between devices, local(): lax.all_to_all(held(outgoing), ('gz', 'yx'), split_axis=0, concat_axis=0,...  9.88 us
    all_to_all x1, waiting for transfers between devices, local(): lax.all_to_all(held(outgoing), ('gz', 'yx'), split_axis=0, concat_axis=0,...  8.53 us
    ppermute x4, starting transfers between devices, swapped(): return held(lax.ppermute(block, ('gz', 'yx'), pairs))  6.16 us
    pallas_call x1, Pallas kernels, local(): pl.pallas_call(taps_kernel, out_shape=(near((TAP_ROWS, DEPTH), bf16), nea...  2.9 us
    pallas_call x1, Pallas kernels, local(): pl.pallas_call(send_kernel, out_shape=near((devices, 2 * BUCKET), f32), i...  2.01 us
    pallas_call x1, Pallas kernels, local(): pl.pallas_call(inner_kernel, out_shape=(near((PART, XD), f32), sums_shape...  1.39 us
    pallas_call x1, Pallas kernels, local(): pl.pallas_call(edges_kernel, out_shape=jax.ShapeDtypeStruct((HIGH, LANES)...  1.31 us
    pallas_call x1, Pallas kernels, local(): pl.pallas_call(rows_kernel, out_shape=(lines, lines, *(near(x.shape, x.dt...  1.29 us
  transfers between devices with their start and end apart: 5, of which 1 were waited for; matrix products, arithmetic and copies ran while one was open for 0% of the time, Pallas kernels for 15%

profile of v8, /device:TPU:1, one launch (start us, length us, event | category | flops | bytes accessed | tf_op | source)
XLA Modules:
  0.0 35.5 jit_solution(4705151989353283391)
XLA Ops:
  0.6 1.3 %shard_map.86 = (bf16[56,256]{1,0:T(8,128)(2,1)S(1)}, bf16[56,256]{1,0:T(8,128)(2,1)S(1)}, bf16[768,256]{1,0:T(8,128)(2,1)S(1)}, s32[64,256]{1,0:T(8,128)S(1)}, ...) custom-call(bf16[768,256]{1,0:T(8,128)(2,1)} %bitcast.18, ...), custom_call_target="tpu_custom_call" | custom-call | tf_op jit(solution)/shard_map/pallas_call | solution.py:334
  1.9 1.5 %collective-permute-start = (bf16[56,256]{1,0:T(8,128)(2,1)S(1)}, bf16[56,256]{1,0:T(8,128)(2,1)S(1)}, u32[]{:S(2)}, u32[]{:S(2)}) collective-permute-start(bf16[56,256]{1,0:T(8,128)(2,1)S(1)} %get-tuple-element.20), channel_id=1, source_target_pairs={{0,16},{1,2},{2,1},{3,4},{4,3},{5,6},{6,5},{7,8},{8,7},{9,10},{10,... | collective-permute-start | bytes 86024 | tf_op jit(solution)/shard_map/ppermute | solution.py:317
  3.4 1.9 %collective-permute-start.1 = (bf16[56,256]{1,0:T(8,128)(2,1)S(1)}, bf16[56,256]{1,0:T(8,128)(2,1)S(1)}, u32[]{:S(2)}, u32[]{:S(2)}) collective-permute-start(bf16[56,256]{1,0:T(8,128)(2,1)S(1)} %get-tuple-element.21), channel_id=1, source_target_pairs={{0,1},{1,0},{2,3},{3,2},{4,5},{5,4},{6,7},{7,6},{8,9},{9,8},{10,11... | collective-permute-start | bytes 86024 | tf_op jit(solution)/shard_map/ppermute | solution.py:317
  5.2 2.9 %shard_map.87 = (bf16[576,896]{1,0:T(8,128)(2,1)S(1)}, f32[192,256]{1,0:T(8,128)S(1)}, f32[96,96]{1,0:T(8,128)S(1)}) custom-call(bf16[768,256]{1,0:T(8,128)(2,1)S(1)} %get-tuple-element.22.cells, bf16[27,3,12]{2,1,0:T(4,128)(2,1)S(1)} %get-tuple-element.24.weights, f32[1,3]{1,0:T(1,128)S(1)} %get-tuple-element.25.bias, s32[64,256]{1,0:T(8,128)S(1)} %get-tuple-element.23.ids, ...), custom_call_target="tpu_custom_call" | custom-call | tf_op jit(solution)/shard_map/pallas_call | solution.py:344
  8.2 0.0 collective-permute-done.two
  8.2 0.0 collective-permute-done.1.one
  8.2 0.3 shard_map.88
  8.4 2.8 %collective-permute-start.2 = (f32[1,1024]{1,0:T(1,128)S(1)}, f32[1,1024]{1,0:T(1,128)S(1)}, u32[]{:S(2)}, u32[]{:S(2)}) collective-permute-start(f32[1,1024]{1,0:T(1,128)S(1)} %get-tuple-element.28), channel_id=1, source_target_pairs={{0,1},{1,0},{2,3},{3,2},{4,5},{5,4},{6,7},{7,6},{8,9},{9,8},{10,11... | collective-permute-start | bytes 12296 | tf_op jit(solution)/shard_map/ppermute | solution.py:317
  11.3 0.0 collective-permute-start.3
  11.3 1.4 %shard_map.89 = (f32[192,256]{1,0:T(8,128)S(1)}, f32[96,96]{1,0:T(8,128)S(1)}, f32[8,1024]{1,0:T(8,128)S(1)}) custom-call(bf16[56,256]{1,0:T(8,128)(2,1)S(1)} %collective-permute-done.two, bf16[56,256]{1,0:T(8,128)(2,1)S(1)} %collective-permute-done.1.one, bf16[576,896]{1,0:T(8,128)(2,1)S(1)} %get-tuple-element.30.taps, ...), custom_call_target="tpu_custom_call" | custom-call | tf_op jit(solution)/shard_map/pallas_call | solution.py:361
  12.7 0.0 collective-permute-done.2.outer
  12.7 0.0 collective-permute-done.3.inner
  12.7 2.0 %shard_map.91 = f32[128,128]{1,0:T(8,128)} custom-call(f32[1,1024]{1,0:T(1,128)S(1)} %collective-permute-done.2.outer, f32[1,1024]{1,0:T(1,128)S(1)} %collective-permute-done.3.inner, bf16[576,896]{1,0:T(8,128)(2,1)S(1)} %get-tuple-element.30.taps, f32[1,1024]{1,0:T(1,128)S(1)} %get-tuple-element.33.own, f32[8,1024]{1,0:T(8,128)S(1)} %get-tuple-element.34.ends, ...), custom_call_target="tpu_custom_call" | custom-call | tf_op jit(solution)/shard_map/pallas_call | solution.py:369
  14.7 9.9 %all-to-all-start = ((f32[128,1,128]{2,1,0:T(1,128)}), f32[128,1,128]{2,1,0:T(1,128)S(1)}, u32[]{:S(2)}, u32[]{:S(2)}) async-start(f32[128,1,128]{2,1,0:T(1,128)} %bitcast.11), calls=%async_computation | async-start | bytes 131072 | tf_op jit(solution)/shard_map/all_to_all | solution.py:375
  24.6 1.1 %shard_map.90 = bf16[192,256]{1,0:T(8,128)(2,1)} custom-call(f32[1,1024]{1,0:T(1,128)S(1)} %collective-permute-done.2.outer, f32[1,1024]{1,0:T(1,128)S(1)} %collective-permute-done.3.inner, bf16[576,896]{1,0:T(8,128)(2,1)S(1)} %get-tuple-element.30.taps, f32[192,256]{1,0:T(8,128)S(1)} %get-tuple-element.32.logits), custom_call_target="tpu_custom_call" | custom-call | tf_op jit(solution)/shard_map/pallas_call | solution.py:376
  25.7 8.5 %all-to-all-done = f32[128,1,128]{2,1,0:T(1,128)S(1)} async-done(((f32[128,1,128]{2,1,0:T(1,128)}), f32[128,1,128]{2,1,0:T(1,128)S(1)}, u32[]{:S(2)}, u32[]{:S(2)}) %all-to-all-start) | async-done | bytes 65568 | tf_op jit(solution)/shard_map/all_to_all | solution.py:375
  34.2 1.3 %shard_map.92 = f32[32,128]{1,0:T(8,128)} custom-call(f32[128,128]{1,0:T(8,128)S(1)} %bitcast.17, s32[64,128]{1,0:T(8,128)S(1)} %get-tuple-element.37.rows), custom_call_target="tpu_custom_call" | custom-call | tf_op jit(solution)/shard_map/pallas_call | solution.py:382
Async XLA Ops:
  1.9 6.2 %collective-permute-start = (bf16[56,256]{1,0:T(8,128)(2,1)S(1)}, bf16[56,256]{1,0:T(8,128)(2,1)S(1)}, u32[]{:S(2)}, u32[]{:S(2)}) collective-permute-start(bf16[56,256]{1,0:T(8,128)(2,1)S(1)} %get-tuple-element.20), channel_id=1, source_target_pairs={{0,16},{1,2},{2,1},{3,4},{4,3},{5,6},{6,5},{7,8},{8,7},{9,10},{10,... | collective-permute-start | bytes 86024 | tf_op jit(solution)/shard_map/ppermute | solution.py:317
  3.4 4.8 %collective-permute-start.1 = (bf16[56,256]{1,0:T(8,128)(2,1)S(1)}, bf16[56,256]{1,0:T(8,128)(2,1)S(1)}, u32[]{:S(2)}, u32[]{:S(2)}) collective-permute-start(bf16[56,256]{1,0:T(8,128)(2,1)S(1)} %get-tuple-element.21), channel_id=1, source_target_pairs={{0,1},{1,0},{2,3},{3,2},{4,5},{5,4},{6,7},{7,6},{8,9},{9,8},{10,11... | collective-permute-start | bytes 86024 | tf_op jit(solution)/shard_map/ppermute | solution.py:317
  8.4 4.2 %collective-permute-start.2 = (f32[1,1024]{1,0:T(1,128)S(1)}, f32[1,1024]{1,0:T(1,128)S(1)}, u32[]{:S(2)}, u32[]{:S(2)}) collective-permute-start(f32[1,1024]{1,0:T(1,128)S(1)} %get-tuple-element.28), channel_id=1, source_target_pairs={{0,1},{1,0},{2,3},{3,2},{4,5},{5,4},{6,7},{7,6},{8,9},{9,8},{10,11... | collective-permute-start | bytes 12296 | tf_op jit(solution)/shard_map/ppermute | solution.py:317
  11.3 1.4 %collective-permute-start.3 = (f32[1,1024]{1,0:T(1,128)S(1)}, f32[1,1024]{1,0:T(1,128)S(1)}, u32[]{:S(2)}, u32[]{:S(2)}) collective-permute-start(f32[1,1024]{1,0:T(1,128)S(1)} %get-tuple-element.29), channel_id=1, source_target_pairs={{0,16},{1,17},{2,18},{3,19},{4,20},{5,21},{6,22},{7,23},{8,24},{9,... | collective-permute-start | bytes 12296 | tf_op jit(solution)/shard_map/ppermute | solution.py:317
  14.7 19.5 %all-to-all-start = ((f32[128,1,128]{2,1,0:T(1,128)}), f32[128,1,128]{2,1,0:T(1,128)S(1)}, u32[]{:S(2)}, u32[]{:S(2)}) async-start(f32[128,1,128]{2,1,0:T(1,128)} %bitcast.11), calls=%async_computation | async-start | bytes 131072 | tf_op jit(solution)/shard_map/all_to_all | solution.py:375

commit v9 on v8

--- a/solution.py
+++ b/solution.py
@@ -20,7 +20,7 @@
 TAP_ROWS = 9 * ROWS
 PART = C_OUT * ROWS
 EARLY = 9
-BATCH = 48
+BATCH = 128
 LOW, HALF, STEP = 96, 48, 12
 
 f32, bf16, i32 = jnp.float32, jnp.bfloat16, jnp.int32

time: 35.7 us -> 35.7 us (level)
  no operation moved by 1% of the time
where the time goes in v9:
time: 35.7 us; the launch traced here: 35.5 us
  starting transfers between devices  16.1 us (45%)
  Pallas kernels  10.2 us (29%)
  waiting for transfers between devices  8.54 us (24%)
  between operations  0.7 us (2%)
    all_to_all x1, starting transfers between devices, local(): lax.all_to_all(held(outgoing), ('gz', 'yx'), split_axis=0, concat_axis=0,...  9.91 us
    all_to_all x1, waiting for transfers between devices, local(): lax.all_to_all(held(outgoing), ('gz', 'yx'), split_axis=0, concat_axis=0,...  8.53 us
    ppermute x4, starting transfers between devices, swapped(): return held(lax.ppermute(block, ('gz', 'yx'), pairs))  6.16 us
    pallas_call x1, Pallas kernels, local(): pl.pallas_call(taps_kernel, out_shape=(near((TAP_ROWS, DEPTH), bf16), nea...  2.88 us
    pallas_call x1, Pallas kernels, local(): pl.pallas_call(send_kernel, out_shape=near((devices, 2 * BUCKET), f32), i...  2.01 us
    pallas_call x1, Pallas kernels, local(): pl.pallas_call(inner_kernel, out_shape=(near((PART, XD), f32), sums_shape...  1.39 us
    pallas_call x1, Pallas kernels, local(): pl.pallas_call(edges_kernel, out_shape=jax.ShapeDtypeStruct((HIGH, LANES)...  1.31 us
    pallas_call x1, Pallas kernels, local(): pl.pallas_call(rows_kernel, out_shape=(lines, lines, *(near(x.shape, x.dt...  1.29 us
  transfers between devices with their start and end apart: 5, of which 1 were waited for; matrix products, arithmetic and copies ran while one was open for 0% of the time, Pallas kernels for 15%

profile of v9, /device:TPU:1, one launch (start us, length us, event | category | flops | bytes accessed | tf_op | source)
XLA Modules:
  0.0 35.5 jit_solution(17034393864147935516)
XLA Ops:
  0.6 1.3 %shard_map.86 = (bf16[56,256]{1,0:T(8,128)(2,1)S(1)}, bf16[56,256]{1,0:T(8,128)(2,1)S(1)}, bf16[768,256]{1,0:T(8,128)(2,1)S(1)}, s32[64,256]{1,0:T(8,128)S(1)}, ...) custom-call(bf16[768,256]{1,0:T(8,128)(2,1)} %bitcast.18, ...), custom_call_target="tpu_custom_call" | custom-call | tf_op jit(solution)/shard_map/pallas_call | solution.py:334
  1.9 1.5 %collective-permute-start = (bf16[56,256]{1,0:T(8,128)(2,1)S(1)}, bf16[56,256]{1,0:T(8,128)(2,1)S(1)}, u32[]{:S(2)}, u32[]{:S(2)}) collective-permute-start(bf16[56,256]{1,0:T(8,128)(2,1)S(1)} %get-tuple-element.20), channel_id=1, source_target_pairs={{0,16},{1,2},{2,1},{3,4},{4,3},{5,6},{6,5},{7,8},{8,7},{9,10},{10,... | collective-permute-start | bytes 86024 | tf_op jit(solution)/shard_map/ppermute | solution.py:317
  3.4 1.9 %collective-permute-start.1 = (bf16[56,256]{1,0:T(8,128)(2,1)S(1)}, bf16[56,256]{1,0:T(8,128)(2,1)S(1)}, u32[]{:S(2)}, u32[]{:S(2)}) collective-permute-start(bf16[56,256]{1,0:T(8,128)(2,1)S(1)} %get-tuple-element.21), channel_id=1, source_target_pairs={{0,1},{1,0},{2,3},{3,2},{4,5},{5,4},{6,7},{7,6},{8,9},{9,8},{10,11... | collective-permute-start | bytes 86024 | tf_op jit(solution)/shard_map/ppermute | solution.py:317
  5.2 2.9 %shard_map.87 = (bf16[576,896]{1,0:T(8,128)(2,1)S(1)}, f32[192,256]{1,0:T(8,128)S(1)}, f32[96,96]{1,0:T(8,128)S(1)}) custom-call(bf16[768,256]{1,0:T(8,128)(2,1)S(1)} %get-tuple-element.22.cells, bf16[27,3,12]{2,1,0:T(4,128)(2,1)S(1)} %get-tuple-element.24.weights, f32[1,3]{1,0:T(1,128)S(1)} %get-tuple-element.25.bias, s32[64,256]{1,0:T(8,128)S(1)} %get-tuple-element.23.ids, ...), custom_call_target="tpu_custom_call" | custom-call | tf_op jit(solution)/shard_map/pallas_call | solution.py:344
  8.1 0.0 collective-permute-done.two
  8.1 0.0 collective-permute-done.1.one
  8.2 0.3 shard_map.88
  8.4 2.8 %collective-permute-start.2 = (f32[1,1024]{1,0:T(1,128)S(1)}, f32[1,1024]{1,0:T(1,128)S(1)}, u32[]{:S(2)}, u32[]{:S(2)}) collective-permute-start(f32[1,1024]{1,0:T(1,128)S(1)} %get-tuple-element.28), channel_id=1, source_target_pairs={{0,1},{1,0},{2,3},{3,2},{4,5},{5,4},{6,7},{7,6},{8,9},{9,8},{10,11... | collective-permute-start | bytes 12296 | tf_op jit(solution)/shard_map/ppermute | solution.py:317
  11.3 0.0 collective-permute-start.3
  11.3 1.4 %shard_map.89 = (f32[192,256]{1,0:T(8,128)S(1)}, f32[96,96]{1,0:T(8,128)S(1)}, f32[8,1024]{1,0:T(8,128)S(1)}) custom-call(bf16[56,256]{1,0:T(8,128)(2,1)S(1)} %collective-permute-done.two, bf16[56,256]{1,0:T(8,128)(2,1)S(1)} %collective-permute-done.1.one, bf16[576,896]{1,0:T(8,128)(2,1)S(1)} %get-tuple-element.30.taps, ...), custom_call_target="tpu_custom_call" | custom-call | tf_op jit(solution)/shard_map/pallas_call | solution.py:361
  12.7 0.0 collective-permute-done.2.outer
  12.7 0.0 collective-permute-done.3.inner
  12.7 2.0 %shard_map.91 = f32[128,128]{1,0:T(8,128)} custom-call(f32[1,1024]{1,0:T(1,128)S(1)} %collective-permute-done.2.outer, f32[1,1024]{1,0:T(1,128)S(1)} %collective-permute-done.3.inner, bf16[576,896]{1,0:T(8,128)(2,1)S(1)} %get-tuple-element.30.taps, f32[1,1024]{1,0:T(1,128)S(1)} %get-tuple-element.33.own, f32[8,1024]{1,0:T(8,128)S(1)} %get-tuple-element.34.ends, ...), custom_call_target="tpu_custom_call" | custom-call | tf_op jit(solution)/shard_map/pallas_call | solution.py:369
  14.7 9.9 %all-to-all-start = ((f32[128,1,128]{2,1,0:T(1,128)}), f32[128,1,128]{2,1,0:T(1,128)S(1)}, u32[]{:S(2)}, u32[]{:S(2)}) async-start(f32[128,1,128]{2,1,0:T(1,128)} %bitcast.11), calls=%async_computation | async-start | bytes 131072 | tf_op jit(solution)/shard_map/all_to_all | solution.py:375
  24.6 1.1 %shard_map.90 = bf16[192,256]{1,0:T(8,128)(2,1)} custom-call(f32[1,1024]{1,0:T(1,128)S(1)} %collective-permute-done.2.outer, f32[1,1024]{1,0:T(1,128)S(1)} %collective-permute-done.3.inner, bf16[576,896]{1,0:T(8,128)(2,1)S(1)} %get-tuple-element.30.taps, f32[192,256]{1,0:T(8,128)S(1)} %get-tuple-element.32.logits), custom_call_target="tpu_custom_call" | custom-call | tf_op jit(solution)/shard_map/pallas_call | solution.py:376
  25.7 8.5 %all-to-all-done = f32[128,1,128]{2,1,0:T(1,128)S(1)} async-done(((f32[128,1,128]{2,1,0:T(1,128)}), f32[128,1,128]{2,1,0:T(1,128)S(1)}, u32[]{:S(2)}, u32[]{:S(2)}) %all-to-all-start) | async-done | bytes 65568 | tf_op jit(solution)/shard_map/all_to_all | solution.py:375
  34.2 1.3 %shard_map.92 = f32[32,128]{1,0:T(8,128)} custom-call(f32[128,128]{1,0:T(8,128)S(1)} %bitcast.17, s32[64,128]{1,0:T(8,128)S(1)} %get-tuple-element.37.rows), custom_call_target="tpu_custom_call" | custom-call | tf_op jit(solution)/shard_map/pallas_call | solution.py:382
Async XLA Ops:
  1.9 6.2 %collective-permute-start = (bf16[56,256]{1,0:T(8,128)(2,1)S(1)}, bf16[56,256]{1,0:T(8,128)(2,1)S(1)}, u32[]{:S(2)}, u32[]{:S(2)}) collective-permute-start(bf16[56,256]{1,0:T(8,128)(2,1)S(1)} %get-tuple-element.20), channel_id=1, source_target_pairs={{0,16},{1,2},{2,1},{3,4},{4,3},{5,6},{6,5},{7,8},{8,7},{9,10},{10,... | collective-permute-start | bytes 86024 | tf_op jit(solution)/shard_map/ppermute | solution.py:317
  3.4 4.8 %collective-permute-start.1 = (bf16[56,256]{1,0:T(8,128)(2,1)S(1)}, bf16[56,256]{1,0:T(8,128)(2,1)S(1)}, u32[]{:S(2)}, u32[]{:S(2)}) collective-permute-start(bf16[56,256]{1,0:T(8,128)(2,1)S(1)} %get-tuple-element.21), channel_id=1, source_target_pairs={{0,1},{1,0},{2,3},{3,2},{4,5},{5,4},{6,7},{7,6},{8,9},{9,8},{10,11... | collective-permute-start | bytes 86024 | tf_op jit(solution)/shard_map/ppermute | solution.py:317
  8.4 4.2 %collective-permute-start.2 = (f32[1,1024]{1,0:T(1,128)S(1)}, f32[1,1024]{1,0:T(1,128)S(1)}, u32[]{:S(2)}, u32[]{:S(2)}) collective-permute-start(f32[1,1024]{1,0:T(1,128)S(1)} %get-tuple-element.28), channel_id=1, source_target_pairs={{0,1},{1,0},{2,3},{3,2},{4,5},{5,4},{6,7},{7,6},{8,9},{9,8},{10,11... | collective-permute-start | bytes 12296 | tf_op jit(solution)/shard_map/ppermute | solution.py:317
  11.3 1.4 %collective-permute-start.3 = (f32[1,1024]{1,0:T(1,128)S(1)}, f32[1,1024]{1,0:T(1,128)S(1)}, u32[]{:S(2)}, u32[]{:S(2)}) collective-permute-start(f32[1,1024]{1,0:T(1,128)S(1)} %get-tuple-element.29), channel_id=1, source_target_pairs={{0,16},{1,17},{2,18},{3,19},{4,20},{5,21},{6,22},{7,23},{8,24},{9,... | collective-permute-start | bytes 12296 | tf_op jit(solution)/shard_map/ppermute | solution.py:317
  14.7 19.5 %all-to-all-start = ((f32[128,1,128]{2,1,0:T(1,128)}), f32[128,1,128]{2,1,0:T(1,128)S(1)}, u32[]{:S(2)}, u32[]{:S(2)}) async-start(f32[128,1,128]{2,1,0:T(1,128)} %bitcast.11), calls=%async_computation | async-start | bytes 131072 | tf_op jit(solution)/shard_map/all_to_all | solution.py:375
